TPU v7x, 32 devices: a whole 2x2x4 slice. The times are simulated.
32 devices in a mesh: seq: 8 (over z, x), head: 4 (over y, core).
Axes of the slice: x: 2, y: 2, z: 4, core: 2. Of those that a mesh axis runs over, the one named last changes fastest.
Arguments:
- queries: bfloat16 [2, 1024, 2048], P(None, 'seq', 'head'), may hold values from -6 to 6
- keys: bfloat16 [2, 1024, 2048], P(None, 'seq', 'head'), may hold values from -6 to 6
- values: bfloat16 [2, 1024, 2048], P(None, 'seq', 'head'), may hold values from -6 to 6
- out_grad: bfloat16 [2, 1024, 2048], P(None, 'seq', 'head'), may hold values from -6 to 6
- out_gain: float32 [2, 2048], P(None, 'head'), may hold values from 0.5 to 1.5
Outputs:
- normed: bfloat16 [2, 1024, 2048], P(None, 'seq', 'head')
- grad_queries: bfloat16 [2, 1024, 2048], P(None, 'seq', 'head')
- grad_keys: bfloat16 [2, 1024, 2048], P(None, 'seq', 'head')
- grad_values: bfloat16 [2, 1024, 2048], P(None, 'seq', 'head')
All inputs are finite; a program needn't handle non-finite values.
Results may differ from a plain program's by a relative error of at most 0.0058.
Values sent between devices are 32-bit elements; how exact they have to be, the bound alone decides.
No kernel may reach another device: no remote copies, remote signals or barrier semaphores. Data moves between devices by JAX's collectives and lax.ppermute only.
A program may use at most 192 MiB of HBM per device.

v0:
```python
import jax
import jax.numpy as jnp
from jax import lax
from jax.sharding import PartitionSpec as P

DH = 128
CH = 128


EPSILON = 1e-06


def entering(array, axis, combine, identity, reverse):
    count, place = (lax.axis_size(axis), lax.axis_index(axis))
    everything = lax.all_gather(array, axis)
    start = jnp.broadcast_to(jnp.asarray(identity, array.dtype), array.shape)

    def step(k, before):
        at = count - 1 - k if reverse else k
        reached = at > place if reverse else at < place
        new = combine(before, everything[at])
        return jnp.where(reached, new, before)

    return lax.fori_loop(0, count, step, start)


def add_states(earlier, later):
    return earlier + later


def per_device(queries, keys, values, out_grad, out_gain):
    layers, tok_rows, feat_width = queries.shape
    heads_dev = feat_width // DH
    blocks_dev = tok_rows // CH
    score_scale = DH ** (-0.5)

    def heads_first(array):
        return array.reshape(layers, blocks_dev, CH, heads_dev, DH).transpose(0, 3, 1, 2, 4)

    def tokens_back(array):
        return array.transpose(0, 2, 3, 1, 4).reshape(layers, tok_rows, feat_width)

    q_blocks = heads_first(queries)
    k_blocks = heads_first(keys)
    v_blocks = heads_first(values)
    grad_in = heads_first(out_grad)
    gain_rows = out_gain.reshape(layers, heads_dev, 1, 1, DH)
    rows_idx = lax.broadcasted_iota(jnp.int32, (CH, CH), 0)
    cols_idx = lax.broadcasted_iota(jnp.int32, (CH, CH), 1)
    causal = rows_idx >= cols_idx
    kv_blocks = jnp.einsum(
        "lhbcd,lhbce->lhbde", k_blocks, v_blocks, preferred_element_type=jnp.float32
    )
    kv_total = jnp.sum(kv_blocks, 2)
    carried = jnp.stack(
        [
            entering(kv_total[layer], "seq", add_states, jnp.zeros_like(kv_total[layer]), False)
            for layer in range(layers)
        ]
    )
    local_prefix = jnp.cumsum(kv_blocks, 2) - kv_blocks
    state16 = (carried[:, :, None] + local_prefix).astype(jnp.bfloat16)
    scores = (
        jnp.einsum("lhbcd,lhbsd->lhbcs", q_blocks, k_blocks, preferred_element_type=jnp.float32)
        * score_scale
    )
    attn_weights = jnp.where(causal, scores, 0.0).astype(jnp.bfloat16)
    attn = score_scale * jnp.einsum(
        "lhbcd,lhbde->lhbce", q_blocks, state16, preferred_element_type=jnp.float32
    )
    attn = attn + jnp.einsum(
        "lhbcs,lhbse->lhbce", attn_weights, v_blocks, preferred_element_type=jnp.float32
    )
    upper = gain_rows * grad_in.astype(jnp.float32)
    square_sum, cross_sum = lax.psum(
        (jnp.sum(attn * attn, (1, 4)), jnp.sum(upper * attn, (1, 4))), "head"
    )
    total_width = feat_width * lax.axis_size("head")
    root = jnp.sqrt(square_sum / total_width + EPSILON)[:, None, :, :, None]
    cross_mean = (cross_sum / total_width)[:, None, :, :, None]
    normed = (attn / root * gain_rows).astype(jnp.bfloat16)
    g_blocks = (upper / root - attn * cross_mean / (root * root * root)).astype(jnp.bfloat16)
    dscores = (
        jnp.einsum("lhbce,lhbse->lhbcs", g_blocks, v_blocks, preferred_element_type=jnp.float32)
        * score_scale
    )
    dweights = jnp.where(causal, dscores, 0.0).astype(jnp.bfloat16)
    back_blocks = jnp.einsum(
        "lhbcd,lhbce->lhbde", q_blocks, g_blocks, preferred_element_type=jnp.float32
    )
    back_total = jnp.sum(back_blocks, 2)
    later_sum = jnp.stack(
        [
            entering(back_total[layer], "seq", add_states, jnp.zeros_like(back_total[layer]), True)
            for layer in range(layers)
        ]
    )
    local_suffix = back_total[:, :, None] - jnp.cumsum(back_blocks, 2)
    back16 = (score_scale * (later_sum[:, :, None] + local_suffix)).astype(jnp.bfloat16)
    grad_q = score_scale * jnp.einsum(
        "lhbce,lhbde->lhbcd", g_blocks, state16, preferred_element_type=jnp.float32
    )
    grad_q = grad_q + jnp.einsum(
        "lhbcs,lhbsd->lhbcd", dweights, k_blocks, preferred_element_type=jnp.float32
    )
    grad_k = jnp.einsum("lhbce,lhbde->lhbcd", v_blocks, back16, preferred_element_type=jnp.float32)
    grad_k = grad_k + jnp.einsum(
        "lhbcs,lhbcd->lhbsd", dweights, q_blocks, preferred_element_type=jnp.float32
    )
    grad_v = jnp.einsum("lhbcd,lhbde->lhbce", k_blocks, back16, preferred_element_type=jnp.float32)
    grad_v = grad_v + jnp.einsum(
        "lhbcs,lhbce->lhbse", attn_weights, g_blocks, preferred_element_type=jnp.float32
    )
    return (
        tokens_back(normed),
        tokens_back(grad_q.astype(jnp.bfloat16)),
        tokens_back(grad_k.astype(jnp.bfloat16)),
        tokens_back(grad_v.astype(jnp.bfloat16)),
    )


def solution(mesh):
    in_specs = (
        P(None, "seq", "head"),
        P(None, "seq", "head"),
        P(None, "seq", "head"),
        P(None, "seq", "head"),
        P(None, "head"),
    )
    out_specs = (
        P(None, "seq", "head"),
        P(None, "seq", "head"),
        P(None, "seq", "head"),
        P(None, "seq", "head"),
    )
    return jax.shard_map(
        per_device, mesh=mesh, in_specs=in_specs, out_specs=out_specs, check_vma=False
    )
```

profile of v0, /device:TPU:0, one launch (start us, length us, event | category | flops | bytes accessed | tf_op | source)
XLA Modules:
  0.0 245.9 jit_solution(16735177507181375245)
XLA Ops:
  7.2 1.1 reshape.154
  12.0 50.7 %all-gather.7.cloned.1.call-done = f32[8,4,128,128]{3,2,1,0:T(8,128)} async-done(((f32[1,4,128,128]{3,2,1,0:T(8,128)}), f32[8,4,128,128]{3,2,1,0:T(8,128)}) %all-gather.7.cloned.1.call-update) | async-done | bytes 2097168 | tf_op jit(solution)/shard_map/all_gather | solution.py:15
  62.7 8.5 %while.61 = (s32[]{:T(128)}, f32[4,128,128]{2,1,0:T(8,128)S(1)}, s32[]{:T(128)}, f32[8,4,128,128]{3,2,1,0:T(8,128)}, s32[]{:T(128)}, /*index=5*/s32[]{:T(128)}) while((s32[]{:T(128)}, f32[4,128,128]{2,1,0:T(8,128)S(1)}, s32[]{:T(128)}, f32[8,4,128,128]{3,2,1,0:T(8,128)}, s32[]{:T(128)}, /*index=5*/s32[]{:T(128)}) %tuple.140), condition=%wide.region_3.4_spmd.clone, body=%wide.region_2.3_spmd.clone.sunk | while | flops 196612 | bytes 786533 | solution.py:24
  63.8 1.0 add_select_fusion.9
  64.9 1.0 add_select_fusion.9
  67.0 1.0 add_select_fusion.9
  69.1 1.0 add_select_fusion.9
  70.2 1.1 add_select_fusion.9
  71.3 42.0 %all-gather.5.cloned.1.call-done = f32[8,4,128,128]{3,2,1,0:T(8,128)} async-done(((f32[1,4,128,128]{3,2,1,0:T(8,128)}), f32[8,4,128,128]{3,2,1,0:T(8,128)}) %all-gather.5.cloned.1.call-update) | async-done | bytes 2097168 | tf_op jit(solution)/shard_map/all_gather | solution.py:15
  113.3 8.5 %while.60 = (s32[]{:T(128)}, f32[4,128,128]{2,1,0:T(8,128)S(1)}, s32[]{:T(128)}, f32[8,4,128,128]{3,2,1,0:T(8,128)}, s32[]{:T(128)}, /*index=5*/s32[]{:T(128)}) while((s32[]{:T(128)}, f32[4,128,128]{2,1,0:T(8,128)S(1)}, s32[]{:T(128)}, f32[8,4,128,128]{3,2,1,0:T(8,128)}, s32[]{:T(128)}, /*index=5*/s32[]{:T(128)}) %tuple.143), condition=%wide.region_1.2_spmd.clone, body=%wide.region_0.0_spmd.clone.sunk | while | flops 196612 | bytes 786533 | solution.py:24
  115.4 1.0 add_select_fusion.8
  117.5 1.0 add_select_fusion.8
  119.6 1.0 add_select_fusion.8
  122.7 5.7 %all-reduce = (f32[2,1,128]{2,0,1:T(2,128)S(1)}, f32[2,1,128]{2,0,1:T(2,128)S(1)}) all-reduce(f32[2,1,128]{2,0,1:T(2,128)S(1)} %bitcast.149, f32[2,1,128]{2,0,1:T(2,128)S(1)} %bitcast.148), channel_id=1, replica_groups=mesh['seq'=8,'head'=4] {'head'}, use_global_device_ids=true, to_apply=%region_5.6 | all-reduce | flops 512 | bytes 4096 | tf_op jit(solution)/shard_map/psum | solution.py:75
  134.6 43.3 %all-gather.11.cloned.1.call-done = f32[8,4,128,128]{3,2,1,0:T(8,128)} async-done(((f32[1,4,128,128]{3,2,1,0:T(8,128)}), f32[8,4,128,128]{3,2,1,0:T(8,128)}) %all-gather.11.cloned.1.call-update) | async-done | bytes 2097168 | tf_op jit(solution)/shard_map/all_gather | solution.py:15
  177.9 8.5 %while.63 = (s32[]{:T(128)}, f32[4,128,128]{2,1,0:T(8,128)S(1)}, s32[]{:T(128)}, f32[8,4,128,128]{3,2,1,0:T(8,128)}, s32[]{:T(128)}, /*index=5*/s32[]{:T(128)}, s32[]{:T(128)}, s32[]{:T(128)}) while((s32[]{:T(128)}, f32[4,128,128]{2,1,0:T(8,128)S(1)}, s32[]{:T(128)}, f32[8,4,128,128]{3,2,1,0:T(8,128)}, s32[]{:T(128)}, ...), condition=%wide.region_11.12_spmd.clone, body=%wide.region_10.11_spmd.clone.sunk | while | flops 196616 | bytes 786595 | solution.py:24
  179.0 1.0 add_select_fusion.11
  182.2 1.0 add_select_fusion.11
  185.4 1.1 add_select_fusion.11
  186.5 41.8 %all-gather.9.cloned.1.call-done = f32[8,4,128,128]{3,2,1,0:T(8,128)} async-done(((f32[1,4,128,128]{3,2,1,0:T(8,128)}), f32[8,4,128,128]{3,2,1,0:T(8,128)}) %all-gather.9.cloned.1.call-update) | async-done | bytes 2097168 | tf_op jit(solution)/shard_map/all_gather | solution.py:15
  228.3 8.6 %while.62 = (s32[]{:T(128)}, f32[4,128,128]{2,1,0:T(8,128)S(1)}, s32[]{:T(128)}, f32[8,4,128,128]{3,2,1,0:T(8,128)}, s32[]{:T(128)}, /*index=5*/s32[]{:T(128)}, s32[]{:T(128)}, s32[]{:T(128)}) while((s32[]{:T(128)}, f32[4,128,128]{2,1,0:T(8,128)S(1)}, s32[]{:T(128)}, f32[8,4,128,128]{3,2,1,0:T(8,128)}, s32[]{:T(128)}, ...), condition=%wide.region_9.10_spmd.clone, body=%wide.region_8.9_spmd.clone.sunk | while | flops 196616 | bytes 786595 | solution.py:24
  228.3 1.1 add_select_fusion.10
  229.4 1.0 add_select_fusion.10
  234.8 1.0 add_select_fusion.10
  (69 shorter events, 31.9 us)
Async XLA Ops:
  7.2 4.1 %copy-start.2 = (bf16[2,128,512]{2,1,0:T(8,128)(2,1)S(1)}, bf16[2,128,512]{2,1,0:T(8,128)(2,1)}, u32[]{:S(2)}) copy-start(bf16[2,128,512]{2,1,0:T(8,128)(2,1)} %param.13) | copy-start | bytes 786436
  7.2 4.3 %copy-start.3 = (f32[2,512]{1,0:T(2,128)S(1)}, f32[2,512]{1,0:T(2,128)}, u32[]{:S(2)}) copy-start(f32[2,512]{1,0:T(2,128)} %param.17) | copy-start | bytes 12292
  7.2 4.3 %copy-start.1 = (bf16[2,128,512]{2,1,0:T(8,128)(2,1)S(1)}, bf16[2,128,512]{2,1,0:T(8,128)(2,1)}, u32[]{:S(2)}) copy-start(bf16[2,128,512]{2,1,0:T(8,128)(2,1)} %param.16) | copy-start | bytes 786436
  7.2 55.6 %all-gather.7.cloned.1.call-start = ((), (), s32[]{:S(2)}) async-start(), calls=%async_computation.1 | async-start | bytes 2359296 | tf_op jit(solution)/shard_map/all_gather | solution.py:15
  10.5 102.8 %all-gather.5.cloned.1.call-start = ((), (), s32[]{:S(2)}) async-start(), calls=%async_computation | async-start | bytes 2359296 | tf_op jit(solution)/shard_map/all_gather | solution.py:15
  11.2 166.7 %all-gather.11.cloned.1.call-start = ((), (), s32[]{:S(2)}) async-start(), calls=%async_computation.3 | async-start | bytes 2359296 | tf_op jit(solution)/shard_map/all_gather | solution.py:15
  129.8 98.5 %all-gather.9.cloned.1.call-start = ((), (), s32[]{:S(2)}) async-start(), calls=%async_computation.2 | async-start | bytes 2359296 | tf_op jit(solution)/shard_map/all_gather | solution.py:15
  228.3 8.7 %copy-start = (f32[2,4,128,128]{2,3,1,0:T(8,128)S(1)}, f32[2,4,128,128]{2,3,1,0:T(8,128)}, u32[]{:S(2)}) copy-start(f32[2,4,128,128]{2,3,1,0:T(8,128)} %fusion.40) | copy-start | bytes 1572868
Sparse Core Ops, SparseCore 0:
  10.7 51.9 all-gather.6
  65.4 47.7 all-gather.4
  129.9 48.0 all-gather.10
  180.5 47.7 all-gather.8
where the time goes:
time: 247 us; the launch traced here: 246 us
  waiting for transfers between devices  179 us (72%)
  other arithmetic  34.2 us (14%)
  between operations  14 us (6%)
  local copies, waits for them, and re-layouts  7.67 us (3%)
  blocking collectives  5.67 us (2%)
  matrix products  4.32 us (2%)
    all_gather x4, waiting for transfers between devices, entering(): everything = lax.all_gather(array, axis)  178 us
    select_n x32, other arithmetic, step(): return jnp.where(reached, new, before)  33.4 us
    psum x1, blocking collectives, per_device(): lax.psum((jnp.sum(attn * attn, (1, 4)), jnp.sum(upper * attn, (1, 4))), '...  5.67 us
  transfers between devices with their start and end apart: 4, of which 4 were waited for; matrix products, arithmetic and copies ran while one was open for 9% of the time, Pallas kernels for 0%

commit v1 on v0

v1 whole, which is shorter than its diff:
```python
import functools

import jax
import jax.numpy as jnp
from jax import lax
from jax.experimental import pallas as pl
from jax.experimental.pallas import tpu as pltpu
from jax.sharding import PartitionSpec as P

DH = 128
CH = 128
GROUP = 4

EPSILON = 1e-06
SCALE = DH ** (-0.5)
F32 = jnp.float32
BF16 = jnp.bfloat16


def dot(a, b, ca, cb):
    return lax.dot_general(a, b, (((ca,), (cb,)), ((), ())), preferred_element_type=F32)


def lanes(head):
    return pl.ds(pl.multiple_of(head * DH, DH), DH)


def causal_mask():
    rows = lax.broadcasted_iota(jnp.int32, (CH, CH), 0)
    cols = lax.broadcasted_iota(jnp.int32, (CH, CH), 1)
    return rows >= cols


def kv_kernel(place_ref, k_ref, v_ref, *outs):
    place = place_ref[0]
    for turn, out in enumerate(outs):
        at = lanes(lax.bitwise_xor(place, turn))
        for layer in range(k_ref.shape[0]):
            out[layer] = dot(k_ref[layer, :, at], v_ref[layer, :, at], 0, 0)


def local_kernel(q_ref, k_ref, v_ref, w_ref, loc_ref):
    mask = causal_mask()
    layers, _, width = q_ref.shape
    for layer in range(layers):
        for head in range(width // DH):
            at = pl.ds(head * DH, DH)
            scores = dot(q_ref[layer, :, at], k_ref[layer, :, at], 1, 1) * SCALE
            w = jnp.where(mask, scores, 0.0).astype(BF16)
            w_ref[layer, :, at] = w
            loc_ref[layer, :, at] = dot(w, v_ref[layer, :, at], 1, 0)


def attn_kernel(place_ref, q_ref, loc_ref, g_ref, gain_ref, *rest):
    states, (attn_ref, s16_ref, sums_ref) = rest[:GROUP], rest[GROUP:]
    place = place_ref[0]
    layers = q_ref.shape[0]
    lane = lax.broadcasted_iota(jnp.int32, (CH, CH), 1)
    columns = jnp.zeros((CH, CH), F32)
    for layer in range(layers):
        square = jnp.zeros((CH, DH), F32)
        cross = jnp.zeros((CH, DH), F32)
        for turn in range(GROUP):
            at = lanes(lax.bitwise_xor(place, turn))
            s16 = states[turn][layer].astype(BF16)
            s16_ref[layer, :, at] = s16
            attn = SCALE * dot(q_ref[layer, :, at], s16, 1, 0) + loc_ref[layer, :, at]
            attn_ref[layer, :, at] = attn
            upper = gain_ref[layer : layer + 1, at] * g_ref[layer, :, at].astype(F32)
            square += attn * attn
            cross += upper * attn
        columns += jnp.where(lane == 2 * layer, jnp.sum(square, 1, keepdims=True), 0.0)
        columns += jnp.where(lane == 2 * layer + 1, jnp.sum(cross, 1, keepdims=True), 0.0)
    sums_ref[...] = columns.T[: sums_ref.shape[0]]


def grad_kernel(total_width, place_ref, attn_ref, g_ref, gain_ref, q_ref, *rest):
    parts = rest[: len(rest) - GROUP - 2]
    normed_ref, ga_ref = rest[len(parts) : len(parts) + 2]
    outs = rest[len(parts) + 2 :]
    place = place_ref[0]
    layers = attn_ref.shape[0]
    sums = parts[0][...]
    for part in parts[1:]:
        sums = sums + part[...]
    sums = jnp.concatenate([sums, jnp.zeros((CH - sums.shape[0], CH), F32)], 0).T
    for layer in range(layers):
        square = sums[:, 2 * layer : 2 * layer + 1] * (1.0 / total_width)
        cross = sums[:, 2 * layer + 1 : 2 * layer + 2] * (1.0 / total_width)
        inv = 1.0 / jnp.sqrt(square + EPSILON)
        back = cross * (inv * inv * inv)
        for turn in range(GROUP):
            at = lanes(lax.bitwise_xor(place, turn))
            attn = attn_ref[layer, :, at]
            gain = gain_ref[layer : layer + 1, at]
            normed_ref[layer, :, at] = (attn * inv * gain).astype(BF16)
            upper = gain * g_ref[layer, :, at].astype(F32)
            ga = (upper * inv - attn * back).astype(BF16)
            ga_ref[layer, :, at] = ga
            outs[turn][layer] = dot(q_ref[layer, :, at], ga, 0, 0)


def inner_kernel(q_ref, k_ref, v_ref, ga_ref, s16_ref, w_ref, gq_ref, gkl_ref, gvl_ref):
    mask = causal_mask()
    layers, _, width = q_ref.shape
    for layer in range(layers):
        for head in range(width // DH):
            at = pl.ds(head * DH, DH)
            ga = ga_ref[layer, :, at]
            dscores = dot(ga, v_ref[layer, :, at], 1, 1) * SCALE
            dw = jnp.where(mask, dscores, 0.0).astype(BF16)
            gq = SCALE * dot(ga, s16_ref[layer, :, at], 1, 1)
            gq_ref[layer, :, at] = (gq + dot(dw, k_ref[layer, :, at], 1, 0)).astype(BF16)
            gkl_ref[layer, :, at] = dot(dw, q_ref[layer, :, at], 0, 0)
            gvl_ref[layer, :, at] = dot(w_ref[layer, :, at], ga, 0, 0)


def outer_kernel(place_ref, k_ref, v_ref, gkl_ref, gvl_ref, *rest):
    backs, (gk_ref, gv_ref) = rest[:GROUP], rest[GROUP:]
    place = place_ref[0]
    for layer in range(k_ref.shape[0]):
        for turn in range(GROUP):
            at = lanes(lax.bitwise_xor(place, turn))
            b16 = (SCALE * backs[turn][layer]).astype(BF16)
            gk = dot(v_ref[layer, :, at], b16, 1, 1) + gkl_ref[layer, :, at]
            gv = dot(k_ref[layer, :, at], b16, 1, 0) + gvl_ref[layer, :, at]
            gk_ref[layer, :, at] = gk.astype(BF16)
            gv_ref[layer, :, at] = gv.astype(BF16)


def call(body, outs, smem, flops, *args):
    moved = sum(a.size * a.dtype.itemsize for a in [*args, *outs])
    return pl.pallas_call(
        body,
        out_shape=outs,
        in_specs=[pl.BlockSpec(memory_space=pltpu.SMEM)] * smem
        + [pl.BlockSpec(memory_space=pltpu.VMEM)] * (len(args) - smem),
        out_specs=[pl.BlockSpec(memory_space=pltpu.VMEM)] * len(outs),
        cost_estimate=pl.CostEstimate(flops=flops, bytes_accessed=moved, transcendentals=0),
    )(*args)


def carried(chunks, place, count, reverse):
    def swap(array, turn):
        return lax.ppermute(array, "seq", [(i, i ^ turn) for i in range(count)])

    def shift(array, by):
        if reverse:
            pairs = [(i + by, i) for i in range(count - by)]
        else:
            pairs = [(i, i + by) for i in range(count - by)]
        return lax.ppermute(array, "seq", pairs)

    got = [chunks[0]] + [swap(chunks[t], t) for t in range(1, GROUP)]
    total = got[0] + got[1] + got[2] + got[3]
    outside = shift(total, GROUP)
    by = 1
    while by < count // GROUP - 1:
        outside = outside + shift(outside, by * GROUP)
        by *= 2
    results = []
    for turn in range(GROUP):
        goal = lax.bitwise_xor(place, turn)
        value = outside
        for t in range(GROUP):
            source = lax.bitwise_xor(place, t)
            reached = source > goal if reverse else source < goal
            value = value + jnp.where(reached, got[t], 0.0)
        results.append(value)
    return [results[0]] + [swap(results[t], t) for t in range(1, GROUP)]


def per_device(seq_count, head_count, queries, keys, values, out_grad, out_gain):
    layers, tok_rows, width = queries.shape
    heads = width // DH
    assert tok_rows == CH and heads == GROUP and seq_count % GROUP == 0
    assert 2 * layers <= 8
    place = lax.axis_index("seq") % GROUP
    place_arg = place.astype(jnp.int32).reshape(1)
    wide = lambda dtype: jax.ShapeDtypeStruct((layers, CH, width), dtype)
    blocks = [jax.ShapeDtypeStruct((layers, DH, DH), F32)] * GROUP
    product = 2 * layers * heads * CH * DH * DH

    kv = call(kv_kernel, blocks, 1, product, place_arg, keys, values)
    states = carried(kv, place, seq_count, False)
    weights, local = call(
        local_kernel, [wide(BF16), wide(F32)], 0, 2 * product, queries, keys, values
    )
    attn, s16, sums = call(
        attn_kernel,
        [wide(F32), wide(BF16), jax.ShapeDtypeStruct((8, CH), F32)],
        1,
        product,
        place_arg,
        queries,
        local,
        out_grad,
        out_gain,
        *states,
    )
    parts = [sums] + [
        lax.ppermute(sums, "head", [(i, (i + by) % head_count) for i in range(head_count)])
        for by in range(1, head_count)
    ]
    normed, ga, *products = call(
        functools.partial(grad_kernel, width * head_count),
        [wide(BF16), wide(BF16), *blocks],
        1,
        product,
        place_arg,
        attn,
        out_grad,
        out_gain,
        queries,
        *parts,
    )
    later = carried(products, place, seq_count, True)
    grad_q, gk_local, gv_local = call(
        inner_kernel,
        [wide(BF16), wide(F32), wide(F32)],
        0,
        5 * product,
        queries,
        keys,
        values,
        ga,
        s16,
        weights,
    )
    grad_k, grad_v = call(
        outer_kernel,
        [wide(BF16), wide(BF16)],
        1,
        2 * product,
        place_arg,
        keys,
        values,
        gk_local,
        gv_local,
        *later,
    )
    return normed, grad_q, grad_k, grad_v


def solution(mesh):
    block = P(None, "seq", "head")
    return jax.shard_map(
        functools.partial(per_device, mesh.shape["seq"], mesh.shape["head"]),
        mesh=mesh,
        in_specs=(block, block, block, block, P(None, "head")),
        out_specs=(block, block, block, block),
        check_vma=False,
    )
```

time: 247 us -> 74 us (0.30)
  waiting for transfers between devices: 179 us -> 26.4 us
  other arithmetic: 34.2 us -> 3.53 us
  starting transfers between devices: 0.16 us -> 23.8 us
  Pallas kernels: 0 us -> 17.1 us
  between operations: 14 us -> 0.78 us
  local copies, waits for them, and re-layouts: 7.67 us -> 2 us
  blocking collectives: 5.67 us -> 0 us
  matrix products: 4.32 us -> 0 us
    all_gather x4 -> x0, waiting for transfers between devices: 178 us -> none  [entering(): everything = lax.all_gather(array, axis)]
    select_n x32 -> x0, other arithmetic: 33.4 us -> none  [step(): return jnp.where(reached, new, before)]
    ppermute x0 -> x17, waiting for transfers between devices: none -> 26.4 us  [the longest x12 12.7 us: swap(): return lax.ppermute(array, 'seq', [(i, i ^ turn) for i in range(count)])]
    ppermute x0 -> x17, starting transfers between devices: none -> 23.8 us  [the longest x12 16.1 us: swap(): return lax.ppermute(array, 'seq', [(i, i ^ turn) for i in range(count)])]
    pallas_call x0 -> x6, Pallas kernels: none -> 17.1 us  [call(): pl.pallas_call(body, out_shape=outs, in_specs=[pl.BlockSpec(memory_space=...]
    psum x1 -> x0, blocking collectives: 5.67 us -> none  [per_device(): lax.psum((jnp.sum(attn * attn, (1, 4)), jnp.sum(upper * attn, (1, 4))), '...]
    dot_general x12 -> x0, matrix products: 4.32 us -> none  [the longest x1 1.02 us: per_device(): jnp.einsum('lhbcs,lhbcd->lhbsd', dweights, q_blocks, preferred_element_ty...]
    add x0 -> x4, other arithmetic: none -> 3.53 us  [the longest x2 2.01 us: carried(): total = got[0] + got[1] + got[2] + got[3]]
  transfers between devices with their start and end apart: 4 -> 17, of which waited for: 4 -> 11; matrix products, arithmetic and copies ran while one was open for 9% -> 0% of each run, Pallas kernels for 0% -> 10%
where the time goes in v1:
time: 74 us; the launch traced here: 73.6 us
  waiting for transfers between devices  26.4 us (36%)
  starting transfers between devices  23.8 us (32%)
  Pallas kernels  17.1 us (23%)
  other arithmetic  3.53 us (5%)
  local copies, waits for them, and re-layouts  2 us (3%)
  between operations  0.78 us (1%)
    pallas_call x6, Pallas kernels, call(): pl.pallas_call(body, out_shape=outs, in_specs=[pl.BlockSpec(memory_space=...  17.1 us
    ppermute x12, starting transfers between devices, swap(): return lax.ppermute(array, 'seq', [(i, i ^ turn) for i in range(count)])  16.1 us
    ppermute x12, waiting for transfers between devices, swap(): return lax.ppermute(array, 'seq', [(i, i ^ turn) for i in range(count)])  12.7 us
    ppermute x2, waiting for transfers between devices, shift(): return lax.ppermute(array, 'seq', pairs)  10.7 us
    ppermute x2, starting transfers between devices, shift(): return lax.ppermute(array, 'seq', pairs)  5.97 us
    ppermute x3, waiting for transfers between devices, per_device(): lax.ppermute(sums, 'head', [(i, (i + by) % head_count) for i in range(hea...  3.01 us
    add x2, other arithmetic, carried(): total = got[0] + got[1] + got[2] + got[3]  2.01 us
    unnamed x22, local copies, waits for them, and re-layouts  2 us
  transfers between devices with their start and end apart: 17, of which 11 were waited for; matrix products, arithmetic and copies ran while one was open for 0% of the time, Pallas kernels for 10%

profile of v1, /device:TPU:0, one launch (start us, length us, event | category | flops | bytes accessed | tf_op | source)
XLA Modules:
  0.0 73.6 jit_solution(5313669866984521872)
XLA Ops:
  0.6 2.0 %shard_map.85 = (f32[2,128,128]{2,1,0:T(8,128)}, f32[2,128,128]{2,1,0:T(8,128)}, f32[2,128,128]{2,1,0:T(8,128)}, f32[2,128,128]{2,1,0:T(8,128)}) custom-call(s32[1]{0:T(128)} %bitcast.place_ref, bf16[2,128,512]{2,1,0:T(8,128)(2,1)} %k_ref.7, bf16[2,128,512]{2,1,0:T(8,128)(2,1)} %v_ref.7), custom_call_target="tpu_custom_call" | custom-call | flops 33554432 | bytes 1048580 | tf_op jit(solution)/shard_map/pallas_call | solution.py:133
  2.7 2.9 %collective-permute-start = (f32[2,128,128]{2,1,0:T(8,128)}, f32[2,128,128]{2,1,0:T(8,128)S(1)}, u32[]{:S(2)}, u32[]{:S(2)}) collective-permute-start(f32[2,128,128]{2,1,0:T(8,128)} %get-tuple-element.26), channel_id=1, source_target_pairs={{0,4},{4,0},{8,12},{12,8},{16,20},{20,16},{24,28},{28,24},{1,5},{5... | collective-permute-start | bytes 393224 | tf_op jit(solution)/shard_map/ppermute | solution.py:145
  5.6 1.6 %collective-permute-start.1 = (f32[2,128,128]{2,1,0:T(8,128)}, f32[2,128,128]{2,1,0:T(8,128)S(1)}, u32[]{:S(2)}, u32[]{:S(2)}) collective-permute-start(f32[2,128,128]{2,1,0:T(8,128)} %get-tuple-element.27), channel_id=1, source_target_pairs={{0,8},{4,12},{8,0},{12,4},{16,24},{20,28},{24,16},{28,20},{1,9},{5... | collective-permute-start | bytes 393224 | tf_op jit(solution)/shard_map/ppermute | solution.py:145
  7.2 2.1 %collective-permute-done = f32[2,128,128]{2,1,0:T(8,128)S(1)} collective-permute-done((f32[2,128,128]{2,1,0:T(8,128)}, f32[2,128,128]{2,1,0:T(8,128)S(1)}, u32[]{:S(2)}, u32[]{:S(2)}) %collective-permute-start) | collective-permute-done | bytes 131104 | tf_op jit(solution)/shard_map/ppermute | solution.py:145
  9.3 2.9 %collective-permute-done.1 = f32[2,128,128]{2,1,0:T(8,128)S(1)} collective-permute-done((f32[2,128,128]{2,1,0:T(8,128)}, f32[2,128,128]{2,1,0:T(8,128)S(1)}, u32[]{:S(2)}, u32[]{:S(2)}) %collective-permute-start.1) | collective-permute-done | bytes 131104 | tf_op jit(solution)/shard_map/ppermute | solution.py:145
  12.2 1.2 %collective-permute-done.2 = f32[2,128,128]{2,1,0:T(8,128)S(1)} collective-permute-done((f32[2,128,128]{2,1,0:T(8,128)}, f32[2,128,128]{2,1,0:T(8,128)S(1)}, u32[]{:S(2)}, u32[]{:S(2)}) %collective-permute-start.2) | collective-permute-done | bytes 131104 | tf_op jit(solution)/shard_map/ppermute | solution.py:145
  14.4 4.7 %collective-permute-start.3 = (f32[2,128,128]{2,1,0:T(8,128)S(1)}, f32[2,128,128]{2,1,0:T(8,128)S(1)}, u32[]{:S(2)}, u32[]{:S(2)}) collective-permute-start(f32[2,128,128]{2,1,0:T(8,128)S(1)} %add_add_fusion.1), channel_id=1, source_target_pairs={{0,16},{4,20},{8,24},{12,28},{1,17},{5,21},{9,25},{13,29},{2,18},{... | collective-permute-start | bytes 393224 | tf_op jit(solution)/shard_map/ppermute | solution.py:152
  19.1 2.5 %collective-permute-done.3 = f32[2,128,128]{2,1,0:T(8,128)S(1)} collective-permute-done((f32[2,128,128]{2,1,0:T(8,128)S(1)}, f32[2,128,128]{2,1,0:T(8,128)S(1)}, u32[]{:S(2)}, u32[]{:S(2)}) %collective-permute-start.3) | collective-permute-done | bytes 131104 | tf_op jit(solution)/shard_map/ppermute | solution.py:152
  22.3 3.9 %collective-permute-start.6 = (f32[2,128,128]{2,1,0:T(8,128)S(1)}, f32[2,128,128]{2,1,0:T(8,128)S(1)}, u32[]{:S(2)}, u32[]{:S(2)}) collective-permute-start(f32[2,128,128]{2,1,0:T(8,128)S(1)} %get-tuple-element.48), channel_id=1, source_target_pairs={{0,12},{4,8},{8,4},{12,0},{16,28},{20,24},{24,20},{28,16},{1,13},{... | collective-permute-start | bytes 393224 | tf_op jit(solution)/shard_map/ppermute | solution.py:145
  26.9 3.3 %shard_map.84 = (bf16[2,128,512]{2,1,0:T(8,128)(2,1)}, f32[2,128,512]{2,1,0:T(8,128)}) custom-call(bf16[2,128,512]{2,1,0:T(8,128)(2,1)} %q_ref.7, bf16[2,128,512]{2,1,0:T(8,128)(2,1)} %k_ref.7, bf16[2,128,512]{2,1,0:T(8,128)(2,1)} %v_ref.7), custom_call_target="tpu_custom_call" | custom-call | flops 67108864 | bytes 1572864 | tf_op jit(solution)/shard_map/pallas_call | solution.py:133
  30.2 1.0 %collective-permute-done.5.rest_2_ = f32[2,128,128]{2,1,0:T(8,128)S(1)} collective-permute-done((f32[2,128,128]{2,1,0:T(8,128)S(1)}, f32[2,128,128]{2,1,0:T(8,128)S(1)}, u32[]{:S(2)}, u32[]{:S(2)}) %collective-permute-start.5) | collective-permute-done | bytes 131104 | tf_op jit(solution)/shard_map/ppermute | solution.py:145
  31.9 2.4 %shard_map.86 = (f32[2,128,512]{2,1,0:T(8,128)}, bf16[2,128,512]{2,1,0:T(8,128)(2,1)}, f32[8,128]{1,0:T(8,128)}) custom-call(s32[1]{0:T(128)} %bitcast.place_ref, bf16[2,128,512]{2,1,0:T(8,128)(2,1)} %q_ref.7, f32[2,128,512]{2,1,0:T(8,128)} %get-tuple-element.24.loc_ref, bf16[2,128,512]{2,1,0:T(8,128)(2,1)} %g_ref.3, f32[2,512]{1,0:T(2,128)} %gain_ref.3, ...), custom_call_target="tpu_custom_call" | custom-call | flops 33554432 | bytes 2367492 | tf_op jit(solution)/shard_map/pallas_call | solution.py:133
  34.3 1.5 %collective-permute-start.8 = (f32[8,128]{1,0:T(8,128)}, f32[8,128]{1,0:T(8,128)S(1)}, u32[]{:S(2)}, u32[]{:S(2)}) collective-permute-start(f32[8,128]{1,0:T(8,128)} %get-tuple-element.30.rest_0_), channel_id=1, source_target_pairs={{0,2},{1,3},{2,0},{3,1},{4,6},{5,7},{6,4},{7,5},{8,10},{9,11},{10,... | collective-permute-start | bytes 12296 | tf_op jit(solution)/shard_map/ppermute | solution.py:202
  36.1 2.1 %collective-permute-done.8.rest_2_ = f32[8,128]{1,0:T(8,128)S(1)} collective-permute-done((f32[8,128]{1,0:T(8,128)}, f32[8,128]{1,0:T(8,128)S(1)}, u32[]{:S(2)}, u32[]{:S(2)}) %collective-permute-start.8) | collective-permute-done | bytes 4128 | tf_op jit(solution)/shard_map/ppermute | solution.py:202
  39.7 2.6 %shard_map.87 = (bf16[2,128,512]{2,1,0:T(8,128)(2,1)}, bf16[2,128,512]{2,1,0:T(8,128)(2,1)}, f32[2,128,128]{2,1,0:T(8,128)}, f32[2,128,128]{2,1,0:T(8,128)}, f32...) custom-call(s32[1]{0:T(128)} %bitcast.place_ref, f32[2,128,512]{2,1,0:T(8,128)} %get-tuple-element.29.attn_ref, ...), custom_call_target="tpu_custom_call" | custom-call | flops 33554432 | bytes 2117636 | tf_op jit(solution)/shard_map/pallas_call | solution.py:133
  42.9 2.2 %collective-permute-start.11 = (f32[2,128,128]{2,1,0:T(8,128)}, f32[2,128,128]{2,1,0:T(8,128)S(1)}, u32[]{:S(2)}, u32[]{:S(2)}) collective-permute-start(f32[2,128,128]{2,1,0:T(8,128)} %get-tuple-element.40), channel_id=1, source_target_pairs={{0,8},{4,12},{8,0},{12,4},{16,24},{20,28},{24,16},{28,20},{1,9},{5... | collective-permute-start | bytes 393224 | tf_op jit(solution)/shard_map/ppermute | solution.py:145
  45.8 3.1 %collective-permute-done.10 = f32[2,128,128]{2,1,0:T(8,128)S(1)} collective-permute-done((f32[2,128,128]{2,1,0:T(8,128)}, f32[2,128,128]{2,1,0:T(8,128)S(1)}, u32[]{:S(2)}, u32[]{:S(2)}) %collective-permute-start.10) | collective-permute-done | bytes 131104 | tf_op jit(solution)/shard_map/ppermute | solution.py:145
  49.2 2.0 %collective-permute-done.12 = f32[2,128,128]{2,1,0:T(8,128)S(1)} collective-permute-done((f32[2,128,128]{2,1,0:T(8,128)}, f32[2,128,128]{2,1,0:T(8,128)S(1)}, u32[]{:S(2)}, u32[]{:S(2)}) %collective-permute-start.12) | collective-permute-done | bytes 131104 | tf_op jit(solution)/shard_map/ppermute | solution.py:145
  52.2 1.3 %collective-permute-start.13 = (f32[2,128,128]{2,1,0:T(8,128)S(1)}, f32[2,128,128]{2,1,0:T(8,128)S(1)}, u32[]{:S(2)}, u32[]{:S(2)}) collective-permute-start(f32[2,128,128]{2,1,0:T(8,128)S(1)} %add_add_fusion), channel_id=1, source_target_pairs={{16,0},{20,4},{24,8},{28,12},{17,1},{21,5},{25,9},{29,13},{18,2},{... | collective-permute-start | bytes 393224 | tf_op jit(solution)/shard_map/ppermute | solution.py:152
  53.5 8.3 %collective-permute-done.13 = f32[2,128,128]{2,1,0:T(8,128)S(1)} collective-permute-done((f32[2,128,128]{2,1,0:T(8,128)S(1)}, f32[2,128,128]{2,1,0:T(8,128)S(1)}, u32[]{:S(2)}, u32[]{:S(2)}) %collective-permute-start.13) | collective-permute-done | bytes 131104 | tf_op jit(solution)/shard_map/ppermute | solution.py:152
  62.7 2.1 %collective-permute-start.15 = (f32[2,128,128]{2,1,0:T(8,128)S(1)}, f32[2,128,128]{2,1,0:T(8,128)S(1)}, u32[]{:S(2)}, u32[]{:S(2)}) collective-permute-start(f32[2,128,128]{2,1,0:T(8,128)S(1)} %get-tuple-element.45), channel_id=1, source_target_pairs={{0,8},{4,12},{8,0},{12,4},{16,24},{20,28},{24,16},{28,20},{1,9},{5... | collective-permute-start | bytes 393224 | tf_op jit(solution)/shard_map/ppermute | solution.py:145
  64.8 1.3 %collective-permute-start.14 = (f32[2,128,128]{2,1,0:T(8,128)S(1)}, f32[2,128,128]{2,1,0:T(8,128)S(1)}, u32[]{:S(2)}, u32[]{:S(2)}) collective-permute-start(f32[2,128,128]{2,1,0:T(8,128)S(1)} %get-tuple-element.46), channel_id=1, source_target_pairs={{0,4},{4,0},{8,12},{12,8},{16,20},{20,16},{24,28},{28,24},{1,5},{5... | collective-permute-start | bytes 393224 | tf_op jit(solution)/shard_map/ppermute | solution.py:145
  66.0 4.2 %shard_map.88 = (bf16[2,128,512]{2,1,0:T(8,128)(2,1)}, f32[2,128,512]{2,1,0:T(8,128)}, f32[2,128,512]{2,1,0:T(8,128)}) custom-call(bf16[2,128,512]{2,1,0:T(8,128)(2,1)} %q_ref.7, bf16[2,128,512]{2,1,0:T(8,128)(2,1)} %k_ref.7, bf16[2,128,512]{2,1,0:T(8,128)(2,1)} %v_ref.7, bf16[2,128,512]{2,1,0:T(8,128)(2,1)} %get-tuple-element.32.ga_ref, ...), custom_call_target="tpu_custom_call" | custom-call | flops 167772160 | bytes 2883584 | tf_op jit(solution)/shard_map/pallas_call | solution.py:133
  71.0 2.6 %shard_map.89 = (bf16[2,128,512]{2,1,0:T(8,128)(2,1)}, bf16[2,128,512]{2,1,0:T(8,128)(2,1)}) custom-call(s32[1]{0:T(128)} %bitcast.place_ref, bf16[2,128,512]{2,1,0:T(8,128)(2,1)} %k_ref.7, bf16[2,128,512]{2,1,0:T(8,128)(2,1)} %v_ref.7, f32[2,128,512]{2,1,0:T(8,128)} %get-tuple-element.36.gkl_ref, f32[2,128,512]{2,1,0:T(8,128)} %get-tuple-element.37.gvl_ref, ...), custom_call_target="tpu_custom_call" | custom-call | flops 67108864 | bytes 2621444 | tf_op jit(solution)/shard_map/pallas_call | solution.py:133
  (42 shorter events, 9.1 us)
Async XLA Ops:
  2.7 6.6 %collective-permute-start = (f32[2,128,128]{2,1,0:T(8,128)}, f32[2,128,128]{2,1,0:T(8,128)S(1)}, u32[]{:S(2)}, u32[]{:S(2)}) collective-permute-start(f32[2,128,128]{2,1,0:T(8,128)} %get-tuple-element.26), channel_id=1, source_target_pairs={{0,4},{4,0},{8,12},{12,8},{16,20},{20,16},{24,28},{28,24},{1,5},{5... | collective-permute-start | bytes 393224 | tf_op jit(solution)/shard_map/ppermute | solution.py:145
  5.6 6.6 %collective-permute-start.1 = (f32[2,128,128]{2,1,0:T(8,128)}, f32[2,128,128]{2,1,0:T(8,128)S(1)}, u32[]{:S(2)}, u32[]{:S(2)}) collective-permute-start(f32[2,128,128]{2,1,0:T(8,128)} %get-tuple-element.27), channel_id=1, source_target_pairs={{0,8},{4,12},{8,0},{12,4},{16,24},{20,28},{24,16},{28,20},{1,9},{5... | collective-permute-start | bytes 393224 | tf_op jit(solution)/shard_map/ppermute | solution.py:145
  7.2 6.2 %collective-permute-start.2 = (f32[2,128,128]{2,1,0:T(8,128)}, f32[2,128,128]{2,1,0:T(8,128)S(1)}, u32[]{:S(2)}, u32[]{:S(2)}) collective-permute-start(f32[2,128,128]{2,1,0:T(8,128)} %get-tuple-element.28), channel_id=1, source_target_pairs={{0,12},{4,8},{8,4},{12,0},{16,28},{20,24},{24,20},{28,16},{1,13},{... | collective-permute-start | bytes 393224 | tf_op jit(solution)/shard_map/ppermute | solution.py:145
  13.4 8.2 %copy-start.1 = (f32[2,128,128]{2,1,0:T(8,128)S(1)}, f32[2,128,128]{2,1,0:T(8,128)}, u32[]{:S(2)}) copy-start(f32[2,128,128]{2,1,0:T(8,128)} %get-tuple-element.25) | copy-start | bytes 393220
  14.4 7.2 %collective-permute-start.3 = (f32[2,128,128]{2,1,0:T(8,128)S(1)}, f32[2,128,128]{2,1,0:T(8,128)S(1)}, u32[]{:S(2)}, u32[]{:S(2)}) collective-permute-start(f32[2,128,128]{2,1,0:T(8,128)S(1)} %add_add_fusion.1), channel_id=1, source_target_pairs={{0,16},{4,20},{8,24},{12,28},{1,17},{5,21},{9,25},{13,29},{2,18},{... | collective-permute-start | bytes 393224 | tf_op jit(solution)/shard_map/ppermute | solution.py:152
  22.3 7.9 %collective-permute-start.6 = (f32[2,128,128]{2,1,0:T(8,128)S(1)}, f32[2,128,128]{2,1,0:T(8,128)S(1)}, u32[]{:S(2)}, u32[]{:S(2)}) collective-permute-start(f32[2,128,128]{2,1,0:T(8,128)S(1)} %get-tuple-element.48), channel_id=1, source_target_pairs={{0,12},{4,8},{8,4},{12,0},{16,28},{20,24},{24,20},{28,16},{1,13},{... | collective-permute-start | bytes 393224 | tf_op jit(solution)/shard_map/ppermute | solution.py:145
  26.3 5.0 %collective-permute-start.5 = (f32[2,128,128]{2,1,0:T(8,128)S(1)}, f32[2,128,128]{2,1,0:T(8,128)S(1)}, u32[]{:S(2)}, u32[]{:S(2)}) collective-permute-start(f32[2,128,128]{2,1,0:T(8,128)S(1)} %get-tuple-element.49), channel_id=1, source_target_pairs={{0,8},{4,12},{8,0},{12,4},{16,24},{20,28},{24,16},{28,20},{1,9},{5... | collective-permute-start | bytes 393224 | tf_op jit(solution)/shard_map/ppermute | solution.py:145
  26.3 5.0 %collective-permute-start.4 = (f32[2,128,128]{2,1,0:T(8,128)S(1)}, f32[2,128,128]{2,1,0:T(8,128)S(1)}, u32[]{:S(2)}, u32[]{:S(2)}) collective-permute-start(f32[2,128,128]{2,1,0:T(8,128)S(1)} %get-tuple-element.50), channel_id=1, source_target_pairs={{0,4},{4,0},{8,12},{12,8},{16,20},{20,16},{24,28},{28,24},{1,5},{5... | collective-permute-start | bytes 393224 | tf_op jit(solution)/shard_map/ppermute | solution.py:145
  30.2 1.0 %copy-start.4 = (f32[2,128,128]{2,1,0:T(8,128)}, f32[2,128,128]{2,1,0:T(8,128)S(1)}, u32[]{:S(2)}) copy-start(f32[2,128,128]{2,1,0:T(8,128)S(1)} %collective-permute-done.6.rest_3_) | copy-start | bytes 393220
  34.3 1.8 %collective-permute-start.9 = (f32[8,128]{1,0:T(8,128)}, f32[8,128]{1,0:T(8,128)S(1)}, u32[]{:S(2)}, u32[]{:S(2)}) collective-permute-start(f32[8,128]{1,0:T(8,128)} %get-tuple-element.30.rest_0_), channel_id=1, source_target_pairs={{0,3},{1,0},{2,1},{3,2},{4,7},{5,4},{6,5},{7,6},{8,11},{9,8},{10,9... | collective-permute-start | bytes 12296 | tf_op jit(solution)/shard_map/ppermute | solution.py:202
  34.3 3.8 %collective-permute-start.8 = (f32[8,128]{1,0:T(8,128)}, f32[8,128]{1,0:T(8,128)S(1)}, u32[]{:S(2)}, u32[]{:S(2)}) collective-permute-start(f32[8,128]{1,0:T(8,128)} %get-tuple-element.30.rest_0_), channel_id=1, source_target_pairs={{0,2},{1,3},{2,0},{3,1},{4,6},{5,7},{6,4},{7,5},{8,10},{9,11},{10,... | collective-permute-start | bytes 12296 | tf_op jit(solution)/shard_map/ppermute | solution.py:202
  35.9 3.2 %collective-permute-start.7 = (f32[8,128]{1,0:T(8,128)}, f32[8,128]{1,0:T(8,128)S(1)}, u32[]{:S(2)}, u32[]{:S(2)}) collective-permute-start(f32[8,128]{1,0:T(8,128)} %get-tuple-element.30.rest_0_), channel_id=1, source_target_pairs={{0,1},{1,2},{2,3},{3,0},{4,5},{5,6},{6,7},{7,4},{8,9},{9,10},{10,1... | collective-permute-start | bytes 12296 | tf_op jit(solution)/shard_map/ppermute | solution.py:202
  36.1 3.0 %copy-start.8 = (f32[8,128]{1,0:T(8,128)}, f32[8,128]{1,0:T(8,128)S(1)}, u32[]{:S(2)}) copy-start(f32[8,128]{1,0:T(8,128)S(1)} %collective-permute-done.9.rest_3_) | copy-start | bytes 12292
  38.2 1.0 %copy-start.9 = (f32[8,128]{1,0:T(8,128)}, f32[8,128]{1,0:T(8,128)S(1)}, u32[]{:S(2)}) copy-start(f32[8,128]{1,0:T(8,128)S(1)} %collective-permute-done.8.rest_2_) | copy-start | bytes 12292
  42.3 6.6 %collective-permute-start.10 = (f32[2,128,128]{2,1,0:T(8,128)}, f32[2,128,128]{2,1,0:T(8,128)S(1)}, u32[]{:S(2)}, u32[]{:S(2)}) collective-permute-start(f32[2,128,128]{2,1,0:T(8,128)} %get-tuple-element.39), channel_id=1, source_target_pairs={{0,4},{4,0},{8,12},{12,8},{16,20},{20,16},{24,28},{28,24},{1,5},{5... | collective-permute-start | bytes 393224 | tf_op jit(solution)/shard_map/ppermute | solution.py:145
  42.9 6.3 %collective-permute-start.11 = (f32[2,128,128]{2,1,0:T(8,128)}, f32[2,128,128]{2,1,0:T(8,128)S(1)}, u32[]{:S(2)}, u32[]{:S(2)}) collective-permute-start(f32[2,128,128]{2,1,0:T(8,128)} %get-tuple-element.40), channel_id=1, source_target_pairs={{0,8},{4,12},{8,0},{12,4},{16,24},{20,28},{24,16},{28,20},{1,9},{5... | collective-permute-start | bytes 393224 | tf_op jit(solution)/shard_map/ppermute | solution.py:145
  45.1 6.1 %collective-permute-start.12 = (f32[2,128,128]{2,1,0:T(8,128)}, f32[2,128,128]{2,1,0:T(8,128)S(1)}, u32[]{:S(2)}, u32[]{:S(2)}) collective-permute-start(f32[2,128,128]{2,1,0:T(8,128)} %get-tuple-element.41), channel_id=1, source_target_pairs={{0,12},{4,8},{8,4},{12,0},{16,28},{20,24},{24,20},{28,16},{1,13},{... | collective-permute-start | bytes 393224 | tf_op jit(solution)/shard_map/ppermute | solution.py:145
  51.2 10.6 %copy-start = (f32[2,128,128]{2,1,0:T(8,128)S(1)}, f32[2,128,128]{2,1,0:T(8,128)}, u32[]{:S(2)}) copy-start(f32[2,128,128]{2,1,0:T(8,128)} %get-tuple-element.38) | copy-start | bytes 393220
  52.2 9.6 %collective-permute-start.13 = (f32[2,128,128]{2,1,0:T(8,128)S(1)}, f32[2,128,128]{2,1,0:T(8,128)S(1)}, u32[]{:S(2)}, u32[]{:S(2)}) collective-permute-start(f32[2,128,128]{2,1,0:T(8,128)S(1)} %add_add_fusion), channel_id=1, source_target_pairs={{16,0},{20,4},{24,8},{28,12},{17,1},{21,5},{25,9},{29,13},{18,2},{... | collective-permute-start | bytes 393224 | tf_op jit(solution)/shard_map/ppermute | solution.py:152
  62.5 7.7 %collective-permute-start.16 = (f32[2,128,128]{2,1,0:T(8,128)S(1)}, f32[2,128,128]{2,1,0:T(8,128)S(1)}, u32[]{:S(2)}, u32[]{:S(2)}) collective-permute-start(f32[2,128,128]{2,1,0:T(8,128)S(1)} %get-tuple-element.44), channel_id=1, source_target_pairs={{0,12},{4,8},{8,4},{12,0},{16,28},{20,24},{24,20},{28,16},{1,13},{... | collective-permute-start | bytes 393224 | tf_op jit(solution)/shard_map/ppermute | solution.py:145
  62.7 7.6 %collective-permute-start.15 = (f32[2,128,128]{2,1,0:T(8,128)S(1)}, f32[2,128,128]{2,1,0:T(8,128)S(1)}, u32[]{:S(2)}, u32[]{:S(2)}) collective-permute-start(f32[2,128,128]{2,1,0:T(8,128)S(1)} %get-tuple-element.45), channel_id=1, source_target_pairs={{0,8},{4,12},{8,0},{12,4},{16,24},{20,28},{24,16},{28,20},{1,9},{5... | collective-permute-start | bytes 393224 | tf_op jit(solution)/shard_map/ppermute | solution.py:145
  64.8 5.5 %collective-permute-start.14 = (f32[2,128,128]{2,1,0:T(8,128)S(1)}, f32[2,128,128]{2,1,0:T(8,128)S(1)}, u32[]{:S(2)}, u32[]{:S(2)}) collective-permute-start(f32[2,128,128]{2,1,0:T(8,128)S(1)} %get-tuple-element.46), channel_id=1, source_target_pairs={{0,4},{4,0},{8,12},{12,8},{16,20},{20,16},{24,28},{28,24},{1,5},{5... | collective-permute-start | bytes 393224 | tf_op jit(solution)/shard_map/ppermute | solution.py:145
  70.2 0.7 copy-start.3
  70.3 0.7 copy-start.5
  (4 other events, 2.6 us)

commit v2 on v1

--- a/solution.py
+++ b/solution.py
@@ -128,11 +128,15 @@
             gv_ref[layer, :, at] = gv.astype(BF16)
 
 
-def call(body, outs, smem, flops, *args):
+def call(body, outs, smem, flops, *args, hbm=()):
     moved = sum(a.size * a.dtype.itemsize for a in [*args, *outs])
+    args = args[:smem] + tuple(
+        pltpu.with_memory_space_constraint(a, pltpu.VMEM) for a in args[smem:]
+    )
     return pl.pallas_call(
         body,
-        out_shape=outs,
+        out_shape=[a if i in hbm else pltpu.VMEM(a.shape, a.dtype) for i, a in enumerate(outs)],
+        compiler_params=pltpu.CompilerParams(vmem_limit_bytes=4 * 2**20),
         in_specs=[pl.BlockSpec(memory_space=pltpu.SMEM)] * smem
         + [pl.BlockSpec(memory_space=pltpu.VMEM)] * (len(args) - smem),
         out_specs=[pl.BlockSpec(memory_space=pltpu.VMEM)] * len(outs),
@@ -213,6 +217,7 @@
         out_gain,
         queries,
         *parts,
+        hbm=(0,),
     )
     later = carried(products, place, seq_count, True)
     grad_q, gk_local, gv_local = call(
@@ -226,6 +231,7 @@
         ga,
         s16,
         weights,
+        hbm=(0,),
     )
     grad_k, grad_v = call(
         outer_kernel,
@@ -238,6 +244,7 @@
         gk_local,
         gv_local,
         *later,
+        hbm=(0, 1),
     )
     return normed, grad_q, grad_k, grad_v
 

time: 74 us -> 63.1 us (0.85)
  Pallas kernels: 17.1 us -> 6.82 us
  other arithmetic: 3.53 us -> 0.27 us
  waiting for transfers between devices: 26.4 us -> 29 us
    pallas_call x6, Pallas kernels: 17.1 us -> 6.82 us  [call(): pl.pallas_call(body, out_shape=[a if i in hbm else pltpu.VMEM(a.shape, a....]
    ppermute x12, waiting for transfers between devices: 12.7 us -> 15.4 us  [swap(): return lax.ppermute(array, 'seq', [(i, i ^ turn) for i in range(count)])]
    add x2, other arithmetic: 2.01 us -> 0.06 us  [carried(): total = got[0] + got[1] + got[2] + got[3]]
    add x2, other arithmetic: 1.52 us -> 0.22 us  [carried(): value = value + jnp.where(reached, got[t], 0.0)]
    unnamed x22 -> x14, local copies, waits for them, and re-layouts: 2 us -> 1.92 us
  transfers between devices with their start and end apart: 17 -> 17, of which waited for: 11 -> 14; matrix products, arithmetic and copies ran while one was open for 0% -> 0% of each run, Pallas kernels for 10% -> 6%
where the time goes in v2:
time: 63.1 us; the launch traced here: 62.9 us
  waiting for transfers between devices  29 us (46%)
  starting transfers between devices  24 us (38%)
  Pallas kernels  6.82 us (11%)
  local copies, waits for them, and re-layouts  1.92 us (3%)
  between operations  0.8 us (1%)
    ppermute x12, starting transfers between devices, swap(): return lax.ppermute(array, 'seq', [(i, i ^ turn) for i in range(count)])  16.3 us
    ppermute x12, waiting for transfers between devices, swap(): return lax.ppermute(array, 'seq', [(i, i ^ turn) for i in range(count)])  15.4 us
    ppermute x2, waiting for transfers between devices, shift(): return lax.ppermute(array, 'seq', pairs)  10.8 us
    pallas_call x6, Pallas kernels, call(): pl.pallas_call(body, out_shape=[a if i in hbm else pltpu.VMEM(a.shape, a....  6.82 us
    ppermute x2, starting transfers between devices, shift(): return lax.ppermute(array, 'seq', pairs)  5.97 us
    ppermute x3, waiting for transfers between devices, per_device(): lax.ppermute(sums, 'head', [(i, (i + by) % head_count) for i in range(hea...  2.87 us
    unnamed x14, local copies, waits for them, and re-layouts  1.92 us
    ppermute x3, starting transfers between devices, per_device(): lax.ppermute(sums, 'head', [(i, (i + by) % head_count) for i in range(hea...  1.79 us
  transfers between devices with their start and end apart: 17, of which 14 were waited for; matrix products, arithmetic and copies ran while one was open for 0% of the time, Pallas kernels for 6%

profile of v2, /device:TPU:0, one launch (start us, length us, event | category | flops | bytes accessed | tf_op | source)
XLA Modules:
  0.0 62.9 jit_solution(18225480924352545642)
XLA Ops:
  1.6 0.9 %copy-done.2 = bf16[2,128,512]{2,1,0:T(8,128)(2,1)S(1)} copy-done((bf16[2,128,512]{2,1,0:T(8,128)(2,1)S(1)}, bf16[2,128,512]{2,1,0:T(8,128)(2,1)}, u32[]{:S(2)}) %copy-start.2) | copy-done | bytes 262168
  2.8 3.0 %collective-permute-start = (f32[2,128,128]{2,1,0:T(8,128)S(1)}, f32[2,128,128]{2,1,0:T(8,128)S(1)}, u32[]{:S(2)}, u32[]{:S(2)}) collective-permute-start(f32[2,128,128]{2,1,0:T(8,128)S(1)} %get-tuple-element.26), channel_id=1, source_target_pairs={{0,4},{4,0},{8,12},{12,8},{16,20},{20,16},{24,28},{28,24},{1,5},{5... | collective-permute-start | bytes 393224 | tf_op jit(solution)/shard_map/ppermute | solution.py:149
  5.8 1.6 %collective-permute-start.1 = (f32[2,128,128]{2,1,0:T(8,128)S(1)}, f32[2,128,128]{2,1,0:T(8,128)S(1)}, u32[]{:S(2)}, u32[]{:S(2)}) collective-permute-start(f32[2,128,128]{2,1,0:T(8,128)S(1)} %get-tuple-element.27), channel_id=1, source_target_pairs={{0,8},{4,12},{8,0},{12,4},{16,24},{20,28},{24,16},{28,20},{1,9},{5... | collective-permute-start | bytes 393224 | tf_op jit(solution)/shard_map/ppermute | solution.py:149
  7.4 1.9 %collective-permute-done = f32[2,128,128]{2,1,0:T(8,128)S(1)} collective-permute-done((f32[2,128,128]{2,1,0:T(8,128)S(1)}, f32[2,128,128]{2,1,0:T(8,128)S(1)}, u32[]{:S(2)}, u32[]{:S(2)}) %collective-permute-start) | collective-permute-done | bytes 131104 | tf_op jit(solution)/shard_map/ppermute | solution.py:149
  9.3 2.9 %collective-permute-done.1 = f32[2,128,128]{2,1,0:T(8,128)S(1)} collective-permute-done((f32[2,128,128]{2,1,0:T(8,128)S(1)}, f32[2,128,128]{2,1,0:T(8,128)S(1)}, u32[]{:S(2)}, u32[]{:S(2)}) %collective-permute-start.1) | collective-permute-done | bytes 131104 | tf_op jit(solution)/shard_map/ppermute | solution.py:149
  12.2 1.2 %collective-permute-done.2 = f32[2,128,128]{2,1,0:T(8,128)S(1)} collective-permute-done((f32[2,128,128]{2,1,0:T(8,128)S(1)}, f32[2,128,128]{2,1,0:T(8,128)S(1)}, u32[]{:S(2)}, u32[]{:S(2)}) %collective-permute-start.2) | collective-permute-done | bytes 131104 | tf_op jit(solution)/shard_map/ppermute | solution.py:149
  13.4 4.7 %collective-permute-start.3 = (f32[2,128,128]{2,1,0:T(8,128)S(1)}, f32[2,128,128]{2,1,0:T(8,128)S(1)}, u32[]{:S(2)}, u32[]{:S(2)}) collective-permute-start(f32[2,128,128]{2,1,0:T(8,128)S(1)} %add_add_fusion.1), channel_id=1, source_target_pairs={{0,16},{4,20},{8,24},{12,28},{1,17},{5,21},{9,25},{13,29},{2,18},{... | collective-permute-start | bytes 393224 | tf_op jit(solution)/shard_map/ppermute | solution.py:156
  18.2 2.4 %collective-permute-done.3 = f32[2,128,128]{2,1,0:T(8,128)S(1)} collective-permute-done((f32[2,128,128]{2,1,0:T(8,128)S(1)}, f32[2,128,128]{2,1,0:T(8,128)S(1)}, u32[]{:S(2)}, u32[]{:S(2)}) %collective-permute-start.3) | collective-permute-done | bytes 131104 | tf_op jit(solution)/shard_map/ppermute | solution.py:156
  20.7 4.0 %collective-permute-start.6 = (f32[2,128,128]{2,1,0:T(8,128)S(1)}, f32[2,128,128]{2,1,0:T(8,128)S(1)}, u32[]{:S(2)}, u32[]{:S(2)}) collective-permute-start(f32[2,128,128]{2,1,0:T(8,128)S(1)} %get-tuple-element.48), channel_id=1, source_target_pairs={{0,12},{4,8},{8,4},{12,0},{16,28},{20,24},{24,20},{28,16},{1,13},{... | collective-permute-start | bytes 393224 | tf_op jit(solution)/shard_map/ppermute | solution.py:149
  25.4 1.4 %shard_map.84 = (bf16[2,128,512]{2,1,0:T(8,128)(2,1)S(1)}, f32[2,128,512]{2,1,0:T(8,128)S(1)}) custom-call(bf16[2,128,512]{2,1,0:T(8,128)(2,1)S(1)} %copy-done.4, bf16[2,128,512]{2,1,0:T(8,128)(2,1)S(1)} %copy-done.1, bf16[2,128,512]{2,1,0:T(8,128)(2,1)S(1)} %copy-done.3), custom_call_target="tpu_custom_call" | custom-call | flops 67108864 | bytes 1572864 | tf_op jit(solution)/shard_map/pallas_call | solution.py:136
  27.6 2.0 %collective-permute-done.5.rest_2_ = f32[2,128,128]{2,1,0:T(8,128)S(1)} collective-permute-done((f32[2,128,128]{2,1,0:T(8,128)S(1)}, f32[2,128,128]{2,1,0:T(8,128)S(1)}, u32[]{:S(2)}, u32[]{:S(2)}) %collective-permute-start.5) | collective-permute-done | bytes 131104 | tf_op jit(solution)/shard_map/ppermute | solution.py:149
  30.1 1.6 %collective-permute-start.8 = (f32[8,128]{1,0:T(8,128)S(1)}, f32[8,128]{1,0:T(8,128)S(1)}, u32[]{:S(2)}, u32[]{:S(2)}) collective-permute-start(f32[8,128]{1,0:T(8,128)S(1)} %get-tuple-element.30.rest_0_), channel_id=1, source_target_pairs={{0,2},{1,3},{2,0},{3,1},{4,6},{5,7},{6,4},{7,5},{8,10},{9,11},{10,... | collective-permute-start | bytes 12296 | tf_op jit(solution)/shard_map/ppermute | solution.py:206
  31.9 1.9 %collective-permute-done.8.rest_2_ = f32[8,128]{1,0:T(8,128)S(1)} collective-permute-done((f32[8,128]{1,0:T(8,128)S(1)}, f32[8,128]{1,0:T(8,128)S(1)}, u32[]{:S(2)}, u32[]{:S(2)}) %collective-permute-start.8) | collective-permute-done | bytes 4128 | tf_op jit(solution)/shard_map/ppermute | solution.py:206
  33.8 1.0 %collective-permute-done.7.rest_1_ = f32[8,128]{1,0:T(8,128)S(1)} collective-permute-done((f32[8,128]{1,0:T(8,128)S(1)}, f32[8,128]{1,0:T(8,128)S(1)}, u32[]{:S(2)}, u32[]{:S(2)}) %collective-permute-start.7) | collective-permute-done | bytes 4128 | tf_op jit(solution)/shard_map/ppermute | solution.py:206
  34.8 1.1 %shard_map.87 = (bf16[2,128,512]{2,1,0:T(8,128)(2,1)}, bf16[2,128,512]{2,1,0:T(8,128)(2,1)S(1)}, f32[2,128,128]{2,1,0:T(8,128)S(1)}, f32[2,128,128]{2,1,0:T(8,12...) custom-call(s32[1]{0:T(128)} %bitcast.place_ref, f32[2,128,512]{2,1,0:T(8,128)S(1)} %get-tuple-element.29.attn_ref, ...), custom_call_target="tpu_custom_call" | custom-call | flops 33554432 | bytes 2117636 | tf_op jit(solution)/shard_map/pallas_call | solution.py:136
  36.5 2.2 %collective-permute-start.11 = (f32[2,128,128]{2,1,0:T(8,128)S(1)}, f32[2,128,128]{2,1,0:T(8,128)S(1)}, u32[]{:S(2)}, u32[]{:S(2)}) collective-permute-start(f32[2,128,128]{2,1,0:T(8,128)S(1)} %get-tuple-element.40), channel_id=1, source_target_pairs={{0,8},{4,12},{8,0},{12,4},{16,24},{20,28},{24,16},{28,20},{1,9},{5... | collective-permute-start | bytes 393224 | tf_op jit(solution)/shard_map/ppermute | solution.py:149
  39.4 2.9 %collective-permute-done.10 = f32[2,128,128]{2,1,0:T(8,128)S(1)} collective-permute-done((f32[2,128,128]{2,1,0:T(8,128)S(1)}, f32[2,128,128]{2,1,0:T(8,128)S(1)}, u32[]{:S(2)}, u32[]{:S(2)}) %collective-permute-start.10) | collective-permute-done | bytes 131104 | tf_op jit(solution)/shard_map/ppermute | solution.py:149
  42.6 2.0 %collective-permute-done.12 = f32[2,128,128]{2,1,0:T(8,128)S(1)} collective-permute-done((f32[2,128,128]{2,1,0:T(8,128)S(1)}, f32[2,128,128]{2,1,0:T(8,128)S(1)}, u32[]{:S(2)}, u32[]{:S(2)}) %collective-permute-start.12) | collective-permute-done | bytes 131104 | tf_op jit(solution)/shard_map/ppermute | solution.py:149
  44.6 1.3 %collective-permute-start.13 = (f32[2,128,128]{2,1,0:T(8,128)S(1)}, f32[2,128,128]{2,1,0:T(8,128)S(1)}, u32[]{:S(2)}, u32[]{:S(2)}) collective-permute-start(f32[2,128,128]{2,1,0:T(8,128)S(1)} %add_add_fusion), channel_id=1, source_target_pairs={{16,0},{20,4},{24,8},{28,12},{17,1},{21,5},{25,9},{29,13},{18,2},{... | collective-permute-start | bytes 393224 | tf_op jit(solution)/shard_map/ppermute | solution.py:156
  46.0 8.3 %collective-permute-done.13 = f32[2,128,128]{2,1,0:T(8,128)S(1)} collective-permute-done((f32[2,128,128]{2,1,0:T(8,128)S(1)}, f32[2,128,128]{2,1,0:T(8,128)S(1)}, u32[]{:S(2)}, u32[]{:S(2)}) %collective-permute-start.13) | collective-permute-done | bytes 131104 | tf_op jit(solution)/shard_map/ppermute | solution.py:156
  54.6 2.0 %collective-permute-start.15 = (f32[2,128,128]{2,1,0:T(8,128)S(1)}, f32[2,128,128]{2,1,0:T(8,128)S(1)}, u32[]{:S(2)}, u32[]{:S(2)}) collective-permute-start(f32[2,128,128]{2,1,0:T(8,128)S(1)} %get-tuple-element.45), channel_id=1, source_target_pairs={{0,8},{4,12},{8,0},{12,4},{16,24},{20,28},{24,16},{28,20},{1,9},{5... | collective-permute-start | bytes 393224 | tf_op jit(solution)/shard_map/ppermute | solution.py:149
  56.7 1.3 %collective-permute-start.14 = (f32[2,128,128]{2,1,0:T(8,128)S(1)}, f32[2,128,128]{2,1,0:T(8,128)S(1)}, u32[]{:S(2)}, u32[]{:S(2)}) collective-permute-start(f32[2,128,128]{2,1,0:T(8,128)S(1)} %get-tuple-element.46), channel_id=1, source_target_pairs={{0,4},{4,0},{8,12},{12,8},{16,20},{20,16},{24,28},{28,24},{1,5},{5... | collective-permute-start | bytes 393224 | tf_op jit(solution)/shard_map/ppermute | solution.py:149
  57.9 2.5 %shard_map.88 = (bf16[2,128,512]{2,1,0:T(8,128)(2,1)}, f32[2,128,512]{2,1,0:T(8,128)S(1)}, f32[2,128,512]{2,1,0:T(8,128)S(1)}) custom-call(bf16[2,128,512]{2,1,0:T(8,128)(2,1)S(1)} %copy-done.4, bf16[2,128,512]{2,1,0:T(8,128)(2,1)S(1)} %copy-done.1, bf16[2,128,512]{2,1,0:T(8,128)(2,1)S(1)} %copy-done.3, bf16[2,128,512]{2,1,0:T(8,128)(2,1)S(1)} %get-tuple-element.32.ga_ref, ...), custom_call_target="tpu_custom_call" | custom-call | flops 167772160 | bytes 2883584 | tf_op jit(solution)/shard_map/pallas_call | solution.py:136
  61.7 1.2 %shard_map.89 = (bf16[2,128,512]{2,1,0:T(8,128)(2,1)}, bf16[2,128,512]{2,1,0:T(8,128)(2,1)}) custom-call(s32[1]{0:T(128)} %bitcast.place_ref, bf16[2,128,512]{2,1,0:T(8,128)(2,1)S(1)} %copy-done.1, bf16[2,128,512]{2,1,0:T(8,128)(2,1)S(1)} %copy-done.3, f32[2,128,512]{2,1,0:T(8,128)S(1)} %get-tuple-element.36.gkl_ref, ...), custom_call_target="tpu_custom_call" | custom-call | flops 67108864 | bytes 2621444 | tf_op jit(solution)/shard_map/pallas_call | solution.py:136
  (34 shorter events, 6.8 us)
Async XLA Ops:
  0.6 1.0 %copy-start = (bf16[2,128,512]{2,1,0:T(8,128)(2,1)S(1)}, bf16[2,128,512]{2,1,0:T(8,128)(2,1)}, u32[]{:S(2)}) copy-start(bf16[2,128,512]{2,1,0:T(8,128)(2,1)} %k_ref.7) | copy-start | bytes 786436
  1.6 0.9 %copy-start.2 = (bf16[2,128,512]{2,1,0:T(8,128)(2,1)S(1)}, bf16[2,128,512]{2,1,0:T(8,128)(2,1)}, u32[]{:S(2)}) copy-start(bf16[2,128,512]{2,1,0:T(8,128)(2,1)} %v_ref.7) | copy-start | bytes 786436
  2.8 6.5 %collective-permute-start = (f32[2,128,128]{2,1,0:T(8,128)S(1)}, f32[2,128,128]{2,1,0:T(8,128)S(1)}, u32[]{:S(2)}, u32[]{:S(2)}) collective-permute-start(f32[2,128,128]{2,1,0:T(8,128)S(1)} %get-tuple-element.26), channel_id=1, source_target_pairs={{0,4},{4,0},{8,12},{12,8},{16,20},{20,16},{24,28},{28,24},{1,5},{5... | collective-permute-start | bytes 393224 | tf_op jit(solution)/shard_map/ppermute | solution.py:149
  5.8 6.4 %collective-permute-start.1 = (f32[2,128,128]{2,1,0:T(8,128)S(1)}, f32[2,128,128]{2,1,0:T(8,128)S(1)}, u32[]{:S(2)}, u32[]{:S(2)}) collective-permute-start(f32[2,128,128]{2,1,0:T(8,128)S(1)} %get-tuple-element.27), channel_id=1, source_target_pairs={{0,8},{4,12},{8,0},{12,4},{16,24},{20,28},{24,16},{28,20},{1,9},{5... | collective-permute-start | bytes 393224 | tf_op jit(solution)/shard_map/ppermute | solution.py:149
  7.4 6.0 %collective-permute-start.2 = (f32[2,128,128]{2,1,0:T(8,128)S(1)}, f32[2,128,128]{2,1,0:T(8,128)S(1)}, u32[]{:S(2)}, u32[]{:S(2)}) collective-permute-start(f32[2,128,128]{2,1,0:T(8,128)S(1)} %get-tuple-element.28), channel_id=1, source_target_pairs={{0,12},{4,8},{8,4},{12,0},{16,28},{20,24},{24,20},{28,16},{1,13},{... | collective-permute-start | bytes 393224 | tf_op jit(solution)/shard_map/ppermute | solution.py:149
  13.4 7.2 %collective-permute-start.3 = (f32[2,128,128]{2,1,0:T(8,128)S(1)}, f32[2,128,128]{2,1,0:T(8,128)S(1)}, u32[]{:S(2)}, u32[]{:S(2)}) collective-permute-start(f32[2,128,128]{2,1,0:T(8,128)S(1)} %add_add_fusion.1), channel_id=1, source_target_pairs={{0,16},{4,20},{8,24},{12,28},{1,17},{5,21},{9,25},{13,29},{2,18},{... | collective-permute-start | bytes 393224 | tf_op jit(solution)/shard_map/ppermute | solution.py:156
  18.1 7.2 %copy-start.1 = (bf16[2,128,512]{2,1,0:T(8,128)(2,1)S(1)}, bf16[2,128,512]{2,1,0:T(8,128)(2,1)}, u32[]{:S(2)}) copy-start(bf16[2,128,512]{2,1,0:T(8,128)(2,1)} %k_ref.7) | copy-start | bytes 786436
  18.1 7.2 %copy-start.3 = (bf16[2,128,512]{2,1,0:T(8,128)(2,1)S(1)}, bf16[2,128,512]{2,1,0:T(8,128)(2,1)}, u32[]{:S(2)}) copy-start(bf16[2,128,512]{2,1,0:T(8,128)(2,1)} %v_ref.7) | copy-start | bytes 786436
  18.1 7.2 %copy-start.4 = (bf16[2,128,512]{2,1,0:T(8,128)(2,1)S(1)}, bf16[2,128,512]{2,1,0:T(8,128)(2,1)}, u32[]{:S(2)}) copy-start(bf16[2,128,512]{2,1,0:T(8,128)(2,1)} %q_ref.7) | copy-start | bytes 786436
  20.7 6.9 %collective-permute-start.6 = (f32[2,128,128]{2,1,0:T(8,128)S(1)}, f32[2,128,128]{2,1,0:T(8,128)S(1)}, u32[]{:S(2)}, u32[]{:S(2)}) collective-permute-start(f32[2,128,128]{2,1,0:T(8,128)S(1)} %get-tuple-element.48), channel_id=1, source_target_pairs={{0,12},{4,8},{8,4},{12,0},{16,28},{20,24},{24,20},{28,16},{1,13},{... | collective-permute-start | bytes 393224 | tf_op jit(solution)/shard_map/ppermute | solution.py:149
  24.7 5.0 %collective-permute-start.5 = (f32[2,128,128]{2,1,0:T(8,128)S(1)}, f32[2,128,128]{2,1,0:T(8,128)S(1)}, u32[]{:S(2)}, u32[]{:S(2)}) collective-permute-start(f32[2,128,128]{2,1,0:T(8,128)S(1)} %get-tuple-element.49), channel_id=1, source_target_pairs={{0,8},{4,12},{8,0},{12,4},{16,24},{20,28},{24,16},{28,20},{1,9},{5... | collective-permute-start | bytes 393224 | tf_op jit(solution)/shard_map/ppermute | solution.py:149
  24.7 5.0 %copy-start.5 = (bf16[2,128,512]{2,1,0:T(8,128)(2,1)S(1)}, bf16[2,128,512]{2,1,0:T(8,128)(2,1)}, u32[]{:S(2)}) copy-start(bf16[2,128,512]{2,1,0:T(8,128)(2,1)} %g_ref.3) | copy-start | bytes 786436
  24.7 5.0 %collective-permute-start.4 = (f32[2,128,128]{2,1,0:T(8,128)S(1)}, f32[2,128,128]{2,1,0:T(8,128)S(1)}, u32[]{:S(2)}, u32[]{:S(2)}) collective-permute-start(f32[2,128,128]{2,1,0:T(8,128)S(1)} %get-tuple-element.50), channel_id=1, source_target_pairs={{0,4},{4,0},{8,12},{12,8},{16,20},{20,16},{24,28},{28,24},{1,5},{5... | collective-permute-start | bytes 393224 | tf_op jit(solution)/shard_map/ppermute | solution.py:149
  25.4 4.3 %copy-start.6 = (f32[2,512]{1,0:T(2,128)S(1)}, f32[2,512]{1,0:T(2,128)}, u32[]{:S(2)}) copy-start(f32[2,512]{1,0:T(2,128)} %gain_ref.3) | copy-start | bytes 12292
  30.1 1.8 %collective-permute-start.9 = (f32[8,128]{1,0:T(8,128)S(1)}, f32[8,128]{1,0:T(8,128)S(1)}, u32[]{:S(2)}, u32[]{:S(2)}) collective-permute-start(f32[8,128]{1,0:T(8,128)S(1)} %get-tuple-element.30.rest_0_), channel_id=1, source_target_pairs={{0,3},{1,0},{2,1},{3,2},{4,7},{5,4},{6,5},{7,6},{8,11},{9,8},{10,9... | collective-permute-start | bytes 12296 | tf_op jit(solution)/shard_map/ppermute | solution.py:206
  30.1 3.7 %collective-permute-start.8 = (f32[8,128]{1,0:T(8,128)S(1)}, f32[8,128]{1,0:T(8,128)S(1)}, u32[]{:S(2)}, u32[]{:S(2)}) collective-permute-start(f32[8,128]{1,0:T(8,128)S(1)} %get-tuple-element.30.rest_0_), channel_id=1, source_target_pairs={{0,2},{1,3},{2,0},{3,1},{4,6},{5,7},{6,4},{7,5},{8,10},{9,11},{10,... | collective-permute-start | bytes 12296 | tf_op jit(solution)/shard_map/ppermute | solution.py:206
  31.7 3.0 %collective-permute-start.7 = (f32[8,128]{1,0:T(8,128)S(1)}, f32[8,128]{1,0:T(8,128)S(1)}, u32[]{:S(2)}, u32[]{:S(2)}) collective-permute-start(f32[8,128]{1,0:T(8,128)S(1)} %get-tuple-element.30.rest_0_), channel_id=1, source_target_pairs={{0,1},{1,2},{2,3},{3,0},{4,5},{5,6},{6,7},{7,4},{8,9},{9,10},{10,1... | collective-permute-start | bytes 12296 | tf_op jit(solution)/shard_map/ppermute | solution.py:206
  35.9 6.4 %collective-permute-start.10 = (f32[2,128,128]{2,1,0:T(8,128)S(1)}, f32[2,128,128]{2,1,0:T(8,128)S(1)}, u32[]{:S(2)}, u32[]{:S(2)}) collective-permute-start(f32[2,128,128]{2,1,0:T(8,128)S(1)} %get-tuple-element.39), channel_id=1, source_target_pairs={{0,4},{4,0},{8,12},{12,8},{16,20},{20,16},{24,28},{28,24},{1,5},{5... | collective-permute-start | bytes 393224 | tf_op jit(solution)/shard_map/ppermute | solution.py:149
  36.5 6.0 %collective-permute-start.11 = (f32[2,128,128]{2,1,0:T(8,128)S(1)}, f32[2,128,128]{2,1,0:T(8,128)S(1)}, u32[]{:S(2)}, u32[]{:S(2)}) collective-permute-start(f32[2,128,128]{2,1,0:T(8,128)S(1)} %get-tuple-element.40), channel_id=1, source_target_pairs={{0,8},{4,12},{8,0},{12,4},{16,24},{20,28},{24,16},{28,20},{1,9},{5... | collective-permute-start | bytes 393224 | tf_op jit(solution)/shard_map/ppermute | solution.py:149
  38.7 5.9 %collective-permute-start.12 = (f32[2,128,128]{2,1,0:T(8,128)S(1)}, f32[2,128,128]{2,1,0:T(8,128)S(1)}, u32[]{:S(2)}, u32[]{:S(2)}) collective-permute-start(f32[2,128,128]{2,1,0:T(8,128)S(1)} %get-tuple-element.41), channel_id=1, source_target_pairs={{0,12},{4,8},{8,4},{12,0},{16,28},{20,24},{24,20},{28,16},{1,13},{... | collective-permute-start | bytes 393224 | tf_op jit(solution)/shard_map/ppermute | solution.py:149
  44.6 9.6 %collective-permute-start.13 = (f32[2,128,128]{2,1,0:T(8,128)S(1)}, f32[2,128,128]{2,1,0:T(8,128)S(1)}, u32[]{:S(2)}, u32[]{:S(2)}) collective-permute-start(f32[2,128,128]{2,1,0:T(8,128)S(1)} %add_add_fusion), channel_id=1, source_target_pairs={{16,0},{20,4},{24,8},{28,12},{17,1},{21,5},{25,9},{29,13},{18,2},{... | collective-permute-start | bytes 393224 | tf_op jit(solution)/shard_map/ppermute | solution.py:156
  54.4 6.1 %collective-permute-start.16 = (f32[2,128,128]{2,1,0:T(8,128)S(1)}, f32[2,128,128]{2,1,0:T(8,128)S(1)}, u32[]{:S(2)}, u32[]{:S(2)}) collective-permute-start(f32[2,128,128]{2,1,0:T(8,128)S(1)} %get-tuple-element.44), channel_id=1, source_target_pairs={{0,12},{4,8},{8,4},{12,0},{16,28},{20,24},{24,20},{28,16},{1,13},{... | collective-permute-start | bytes 393224 | tf_op jit(solution)/shard_map/ppermute | solution.py:149
  54.6 6.4 %collective-permute-start.15 = (f32[2,128,128]{2,1,0:T(8,128)S(1)}, f32[2,128,128]{2,1,0:T(8,128)S(1)}, u32[]{:S(2)}, u32[]{:S(2)}) collective-permute-start(f32[2,128,128]{2,1,0:T(8,128)S(1)} %get-tuple-element.45), channel_id=1, source_target_pairs={{0,8},{4,12},{8,0},{12,4},{16,24},{20,28},{24,16},{28,20},{1,9},{5... | collective-permute-start | bytes 393224 | tf_op jit(solution)/shard_map/ppermute | solution.py:149
  56.7 5.1 %collective-permute-start.14 = (f32[2,128,128]{2,1,0:T(8,128)S(1)}, f32[2,128,128]{2,1,0:T(8,128)S(1)}, u32[]{:S(2)}, u32[]{:S(2)}) collective-permute-start(f32[2,128,128]{2,1,0:T(8,128)S(1)} %get-tuple-element.46), channel_id=1, source_target_pairs={{0,4},{4,0},{8,12},{12,8},{16,20},{20,16},{24,28},{28,24},{1,5},{5... | collective-permute-start | bytes 393224 | tf_op jit(solution)/shard_map/ppermute | solution.py:149

commit v3 on v2

--- a/solution.py
+++ b/solution.py
@@ -10,6 +10,11 @@
 DH = 128
 CH = 128
 GROUP = 4
+ORDERS = ((1, 2, 3), (3, 2, 1), (1, 2, 3), (3, 2, 1))
+CYCLIC = True
+BARRIER = False
+AR = (3, 2, 1)
+RING = True
 
 EPSILON = 1e-06
 SCALE = DH ** (-0.5)
@@ -31,9 +36,9 @@
     return rows >= cols
 
 
-def kv_kernel(place_ref, k_ref, v_ref, *outs):
-    place = place_ref[0]
-    for turn, out in enumerate(outs):
+def kv_kernel(order, place_ref, k_ref, v_ref, *outs):
+    place = place_ref[0]
+    for turn, out in zip((0, *order), outs):
         at = lanes(lax.bitwise_xor(place, turn))
         for layer in range(k_ref.shape[0]):
             out[layer] = dot(k_ref[layer, :, at], v_ref[layer, :, at], 0, 0)
@@ -51,7 +56,21 @@
             loc_ref[layer, :, at] = dot(w, v_ref[layer, :, at], 1, 0)
 
 
-def attn_kernel(place_ref, q_ref, loc_ref, g_ref, gain_ref, *rest):
+def spread_kernel(reverse, order, order_back, place_ref, outside_ref, *refs):
+    got, outs = refs[:GROUP], refs[GROUP:]
+    place = place_ref[0]
+    for layer in range(outside_ref.shape[0]):
+        for turn, out in zip((0, *order_back), outs):
+            goal = lax.bitwise_xor(place, turn)
+            value = outside_ref[layer]
+            for t, ref in zip((0, *order), got):
+                source = lax.bitwise_xor(place, t)
+                reached = source > goal if reverse else source < goal
+                value = value + jnp.where(reached, ref[layer], 0.0)
+            out[layer] = value
+
+
+def attn_kernel(order, place_ref, q_ref, loc_ref, g_ref, gain_ref, *rest):
     states, (attn_ref, s16_ref, sums_ref) = rest[:GROUP], rest[GROUP:]
     place = place_ref[0]
     layers = q_ref.shape[0]
@@ -60,9 +79,9 @@
     for layer in range(layers):
         square = jnp.zeros((CH, DH), F32)
         cross = jnp.zeros((CH, DH), F32)
-        for turn in range(GROUP):
+        for turn, state in zip((0, *order), states):
             at = lanes(lax.bitwise_xor(place, turn))
-            s16 = states[turn][layer].astype(BF16)
+            s16 = state[layer].astype(BF16)
             s16_ref[layer, :, at] = s16
             attn = SCALE * dot(q_ref[layer, :, at], s16, 1, 0) + loc_ref[layer, :, at]
             attn_ref[layer, :, at] = attn
@@ -74,9 +93,9 @@
     sums_ref[...] = columns.T[: sums_ref.shape[0]]
 
 
-def grad_kernel(total_width, place_ref, attn_ref, g_ref, gain_ref, q_ref, *rest):
+def grad_kernel(total_width, order, place_ref, attn_ref, g_ref, gain_ref, q_ref, *rest):
     parts = rest[: len(rest) - GROUP - 2]
-    normed_ref, ga_ref = rest[len(parts) : len(parts) + 2]
+    ga_ref, inv_ref = rest[len(parts) : len(parts) + 2]
     outs = rest[len(parts) + 2 :]
     place = place_ref[0]
     layers = attn_ref.shape[0]
@@ -89,23 +108,24 @@
         cross = sums[:, 2 * layer + 1 : 2 * layer + 2] * (1.0 / total_width)
         inv = 1.0 / jnp.sqrt(square + EPSILON)
         back = cross * (inv * inv * inv)
-        for turn in range(GROUP):
+        inv_ref[layer] = jnp.broadcast_to(inv, inv_ref.shape[1:])
+        for turn, out in zip((0, *order), outs):
             at = lanes(lax.bitwise_xor(place, turn))
-            attn = attn_ref[layer, :, at]
-            gain = gain_ref[layer : layer + 1, at]
-            normed_ref[layer, :, at] = (attn * inv * gain).astype(BF16)
-            upper = gain * g_ref[layer, :, at].astype(F32)
-            ga = (upper * inv - attn * back).astype(BF16)
+            upper = gain_ref[layer : layer + 1, at] * g_ref[layer, :, at].astype(F32)
+            ga = (upper * inv - attn_ref[layer, :, at] * back).astype(BF16)
             ga_ref[layer, :, at] = ga
-            outs[turn][layer] = dot(q_ref[layer, :, at], ga, 0, 0)
-
-
-def inner_kernel(q_ref, k_ref, v_ref, ga_ref, s16_ref, w_ref, gq_ref, gkl_ref, gvl_ref):
+            out[layer] = dot(q_ref[layer, :, at], ga, 0, 0)
+
+
+def inner_kernel(q_ref, k_ref, v_ref, gain_ref, attn_ref, inv_ref, *rest):
+    ga_ref, s16_ref, w_ref, normed_ref, gq_ref, gkl_ref, gvl_ref = rest
     mask = causal_mask()
     layers, _, width = q_ref.shape
     for layer in range(layers):
         for head in range(width // DH):
             at = pl.ds(head * DH, DH)
+            gain = gain_ref[layer : layer + 1, at]
+            normed_ref[layer, :, at] = (attn_ref[layer, :, at] * inv_ref[layer] * gain).astype(BF16)
             ga = ga_ref[layer, :, at]
             dscores = dot(ga, v_ref[layer, :, at], 1, 1) * SCALE
             dw = jnp.where(mask, dscores, 0.0).astype(BF16)
@@ -115,13 +135,13 @@
             gvl_ref[layer, :, at] = dot(w_ref[layer, :, at], ga, 0, 0)
 
 
-def outer_kernel(place_ref, k_ref, v_ref, gkl_ref, gvl_ref, *rest):
+def outer_kernel(order, place_ref, k_ref, v_ref, gkl_ref, gvl_ref, *rest):
     backs, (gk_ref, gv_ref) = rest[:GROUP], rest[GROUP:]
     place = place_ref[0]
     for layer in range(k_ref.shape[0]):
-        for turn in range(GROUP):
+        for turn, back in zip((0, *order), backs):
             at = lanes(lax.bitwise_xor(place, turn))
-            b16 = (SCALE * backs[turn][layer]).astype(BF16)
+            b16 = (SCALE * back[layer]).astype(BF16)
             gk = dot(v_ref[layer, :, at], b16, 1, 1) + gkl_ref[layer, :, at]
             gv = dot(k_ref[layer, :, at], b16, 1, 0) + gvl_ref[layer, :, at]
             gk_ref[layer, :, at] = gk.astype(BF16)
@@ -144,34 +164,42 @@
     )(*args)
 
 
-def carried(chunks, place, count, reverse):
+def carried(chunks, place, count, reverse, beside, order, order_back):
     def swap(array, turn):
         return lax.ppermute(array, "seq", [(i, i ^ turn) for i in range(count)])
 
     def shift(array, by):
+        if CYCLIC:
+            step = -by if reverse else by
+            moved = lax.ppermute(array, "seq", [(i, (i + step) % count) for i in range(count)])
+            inside = place < count - by if reverse else place >= by
+            return jnp.where(inside, moved, 0.0)
+        pairs = [(i, i + by) for i in range(count - by)]
         if reverse:
-            pairs = [(i + by, i) for i in range(count - by)]
-        else:
-            pairs = [(i, i + by) for i in range(count - by)]
+            pairs = [(b, a) for a, b in pairs]
         return lax.ppermute(array, "seq", pairs)
 
-    got = [chunks[0]] + [swap(chunks[t], t) for t in range(1, GROUP)]
+    got = [chunks[0]] + [swap(chunks[1 + j], t) for j, t in enumerate(order)]
+    extra = beside()
+    if BARRIER:
+        got, extra = lax.optimization_barrier((got, extra))
     total = got[0] + got[1] + got[2] + got[3]
     outside = shift(total, GROUP)
     by = 1
     while by < count // GROUP - 1:
         outside = outside + shift(outside, by * GROUP)
         by *= 2
-    results = []
-    for turn in range(GROUP):
-        goal = lax.bitwise_xor(place, turn)
-        value = outside
-        for t in range(GROUP):
-            source = lax.bitwise_xor(place, t)
-            reached = source > goal if reverse else source < goal
-            value = value + jnp.where(reached, got[t], 0.0)
-        results.append(value)
-    return [results[0]] + [swap(results[t], t) for t in range(1, GROUP)]
+    own = lax.bitwise_and(place, GROUP - 1).astype(jnp.int32).reshape(1)
+    results = call(
+        functools.partial(spread_kernel, reverse, order, order_back),
+        [jax.ShapeDtypeStruct(total.shape, F32)] * GROUP,
+        1,
+        0,
+        own,
+        outside,
+        *got,
+    )
+    return [results[0]] + [swap(results[1 + j], t) for j, t in enumerate(order_back)], extra
 
 
 def per_device(seq_count, head_count, queries, keys, values, out_grad, out_gain):
@@ -179,19 +207,26 @@
     heads = width // DH
     assert tok_rows == CH and heads == GROUP and seq_count % GROUP == 0
     assert 2 * layers <= 8
-    place = lax.axis_index("seq") % GROUP
-    place_arg = place.astype(jnp.int32).reshape(1)
+    place = lax.axis_index("seq")
+    place_arg = lax.bitwise_and(place, GROUP - 1).astype(jnp.int32).reshape(1)
     wide = lambda dtype: jax.ShapeDtypeStruct((layers, CH, width), dtype)
     blocks = [jax.ShapeDtypeStruct((layers, DH, DH), F32)] * GROUP
     product = 2 * layers * heads * CH * DH * DH
 
-    kv = call(kv_kernel, blocks, 1, product, place_arg, keys, values)
-    states = carried(kv, place, seq_count, False)
-    weights, local = call(
-        local_kernel, [wide(BF16), wide(F32)], 0, 2 * product, queries, keys, values
+    kv = call(functools.partial(kv_kernel, ORDERS[0]), blocks, 1, product, place_arg, keys, values)
+    states, (weights, local) = carried(
+        kv,
+        place,
+        seq_count,
+        False,
+        lambda: call(
+            local_kernel, [wide(BF16), wide(F32)], 0, 2 * product, queries, keys, values
+        ),
+        ORDERS[0],
+        ORDERS[1],
     )
     attn, s16, sums = call(
-        attn_kernel,
+        functools.partial(attn_kernel, ORDERS[1]),
         [wide(F32), wide(BF16), jax.ShapeDtypeStruct((8, CH), F32)],
         1,
         product,
@@ -203,12 +238,12 @@
         *states,
     )
     parts = [sums] + [
-        lax.ppermute(sums, "head", [(i, (i + by) % head_count) for i in range(head_count)])
-        for by in range(1, head_count)
+        lax.ppermute(sums, "head", [(i, (i + by) % head_count if RING else i ^ by) for i in range(head_count)])
+        for by in AR
     ]
-    normed, ga, *products = call(
-        functools.partial(grad_kernel, width * head_count),
-        [wide(BF16), wide(BF16), *blocks],
+    ga, inv, *products = call(
+        functools.partial(grad_kernel, width * head_count, ORDERS[2]),
+        [wide(BF16), jax.ShapeDtypeStruct((layers, CH, DH), F32), *blocks],
         1,
         product,
         place_arg,
@@ -217,24 +252,33 @@
         out_gain,
         queries,
         *parts,
-        hbm=(0,),
-    )
-    later = carried(products, place, seq_count, True)
-    grad_q, gk_local, gv_local = call(
-        inner_kernel,
-        [wide(BF16), wide(F32), wide(F32)],
-        0,
-        5 * product,
-        queries,
-        keys,
-        values,
-        ga,
-        s16,
-        weights,
-        hbm=(0,),
+    )
+    later, (normed, grad_q, gk_local, gv_local) = carried(
+        products,
+        place,
+        seq_count,
+        True,
+        lambda: call(
+            inner_kernel,
+            [wide(BF16), wide(BF16), wide(F32), wide(F32)],
+            0,
+            5 * product,
+            queries,
+            keys,
+            values,
+            out_gain,
+            attn,
+            inv,
+            ga,
+            s16,
+            weights,
+            hbm=(0, 1),
+        ),
+        ORDERS[2],
+        ORDERS[3],
     )
     grad_k, grad_v = call(
-        outer_kernel,
+        functools.partial(outer_kernel, ORDERS[3]),
         [wide(BF16), wide(BF16)],
         1,
         2 * product,

time: 63.1 us -> 60.4 us (0.957)
  starting transfers between devices: 24 us -> 22 us
    ppermute x12, starting transfers between devices: 16.3 us -> 15.2 us  [swap(): return lax.ppermute(array, 'seq', [(i, i ^ turn) for i in range(count)])]
    ppermute x5, starting transfers between devices: 7.76 us -> 6.8 us  [the longest x2 5.03 us: shift(): lax.ppermute(array, 'seq', [(i, (i + step) % count) for i in range(count)])]
    pallas_call x6 -> x8, Pallas kernels: 6.82 us -> 6.56 us  [call(): pl.pallas_call(body, out_shape=[a if i in hbm else pltpu.VMEM(a.shape, a....]
  transfers between devices with their start and end apart: 17 -> 17, of which waited for: 14 -> 13; matrix products, arithmetic and copies ran while one was open for 0% -> 0% of each run, Pallas kernels for 6% -> 7%
where the time goes in v3:
time: 60.4 us; the launch traced here: 60.2 us
  waiting for transfers between devices  28.9 us (48%)
  starting transfers between devices  22 us (36%)
  Pallas kernels  6.56 us (11%)
  local copies, waits for them, and re-layouts  1.92 us (3%)
  between operations  0.72 us (1%)
    ppermute x12, waiting for transfers between devices, swap(): return lax.ppermute(array, 'seq', [(i, i ^ turn) for i in range(count)])  15.4 us
    ppermute x12, starting transfers between devices, swap(): return lax.ppermute(array, 'seq', [(i, i ^ turn) for i in range(count)])  15.2 us
    ppermute x2, waiting for transfers between devices, shift(): lax.ppermute(array, 'seq', [(i, (i + step) % count) for i in range(count)])  10.6 us
    pallas_call x8, Pallas kernels, call(): pl.pallas_call(body, out_shape=[a if i in hbm else pltpu.VMEM(a.shape, a....  6.56 us
    ppermute x2, starting transfers between devices, shift(): lax.ppermute(array, 'seq', [(i, (i + step) % count) for i in range(count)])  5.03 us
    ppermute x3, waiting for transfers between devices, per_device(): lax.ppermute(sums, 'head', [(i, (i + by) % head_count if RING else i ^ by...  2.87 us
    unnamed x14, local copies, waits for them, and re-layouts  1.92 us
    ppermute x3, starting transfers between devices, per_device(): lax.ppermute(sums, 'head', [(i, (i + by) % head_count if RING else i ^ by...  1.77 us
  transfers between devices with their start and end apart: 17, of which 13 were waited for; matrix products, arithmetic and copies ran while one was open for 0% of the time, Pallas kernels for 7%

profile of v3, /device:TPU:0, one launch (start us, length us, event | category | flops | bytes accessed | tf_op | source)
XLA Modules:
  0.0 60.2 jit_solution(3201853099400452179)
XLA Ops:
  2.8 3.0 %collective-permute-start = (f32[2,128,128]{2,1,0:T(8,128)S(1)}, f32[2,128,128]{2,1,0:T(8,128)S(1)}, u32[]{:S(2)}, u32[]{:S(2)}) collective-permute-start(f32[2,128,128]{2,1,0:T(8,128)S(1)} %get-tuple-element.35), channel_id=1, source_target_pairs={{0,4},{4,0},{8,12},{12,8},{16,20},{20,16},{24,28},{28,24},{1,5},{5... | collective-permute-start | bytes 393224 | tf_op jit(solution)/shard_map/ppermute | solution.py:169
  5.8 1.6 %collective-permute-start.1 = (f32[2,128,128]{2,1,0:T(8,128)S(1)}, f32[2,128,128]{2,1,0:T(8,128)S(1)}, u32[]{:S(2)}, u32[]{:S(2)}) collective-permute-start(f32[2,128,128]{2,1,0:T(8,128)S(1)} %get-tuple-element.36), channel_id=1, source_target_pairs={{0,8},{4,12},{8,0},{12,4},{16,24},{20,28},{24,16},{28,20},{1,9},{5... | collective-permute-start | bytes 393224 | tf_op jit(solution)/shard_map/ppermute | solution.py:169
  7.4 1.9 %collective-permute-done.refs_1_ = f32[2,128,128]{2,1,0:T(8,128)S(1)} collective-permute-done((f32[2,128,128]{2,1,0:T(8,128)S(1)}, f32[2,128,128]{2,1,0:T(8,128)S(1)}, u32[]{:S(2)}, u32[]{:S(2)}) %collective-permute-start) | collective-permute-done | bytes 131104 | tf_op jit(solution)/shard_map/ppermute | solution.py:169
  9.3 2.9 %collective-permute-done.1.refs_2_ = f32[2,128,128]{2,1,0:T(8,128)S(1)} collective-permute-done((f32[2,128,128]{2,1,0:T(8,128)S(1)}, f32[2,128,128]{2,1,0:T(8,128)S(1)}, u32[]{:S(2)}, u32[]{:S(2)}) %collective-permute-start.1) | collective-permute-done | bytes 131104 | tf_op jit(solution)/shard_map/ppermute | solution.py:169
  12.2 1.2 %collective-permute-done.2.refs_3_ = f32[2,128,128]{2,1,0:T(8,128)S(1)} collective-permute-done((f32[2,128,128]{2,1,0:T(8,128)S(1)}, f32[2,128,128]{2,1,0:T(8,128)S(1)}, u32[]{:S(2)}, u32[]{:S(2)}) %collective-permute-start.2) | collective-permute-done | bytes 131104 | tf_op jit(solution)/shard_map/ppermute | solution.py:169
  13.4 2.8 %collective-permute-start.3 = (f32[2,128,128]{2,1,0:T(8,128)S(1)}, f32[2,128,128]{2,1,0:T(8,128)S(1)}, u32[]{:S(2)}, u32[]{:S(2)}) collective-permute-start(f32[2,128,128]{2,1,0:T(8,128)S(1)} %add_add_fusion.1), channel_id=1, source_target_pairs={{0,16},{4,20},{8,24},{12,28},{16,0},{20,4},{24,8},{28,12},{1,17},{... | collective-permute-start | bytes 393224 | tf_op jit(solution)/shard_map/ppermute | solution.py:174
  16.2 5.4 %collective-permute-done.3 = f32[2,128,128]{2,1,0:T(8,128)S(1)} collective-permute-done((f32[2,128,128]{2,1,0:T(8,128)S(1)}, f32[2,128,128]{2,1,0:T(8,128)S(1)}, u32[]{:S(2)}, u32[]{:S(2)}) %collective-permute-start.3) | collective-permute-done | bytes 131104 | tf_op jit(solution)/shard_map/ppermute | solution.py:174
  21.8 1.1 %collective-permute-start.4 = (f32[2,128,128]{2,1,0:T(8,128)S(1)}, f32[2,128,128]{2,1,0:T(8,128)S(1)}, u32[]{:S(2)}, u32[]{:S(2)}) collective-permute-start(f32[2,128,128]{2,1,0:T(8,128)S(1)} %get-tuple-element.39), channel_id=1, source_target_pairs={{0,12},{4,8},{8,4},{12,0},{16,28},{20,24},{24,20},{28,16},{1,13},{... | collective-permute-start | bytes 393224 | tf_op jit(solution)/shard_map/ppermute | solution.py:169
  22.9 1.4 %collective-permute-start.5 = (f32[2,128,128]{2,1,0:T(8,128)S(1)}, f32[2,128,128]{2,1,0:T(8,128)S(1)}, u32[]{:S(2)}, u32[]{:S(2)}) collective-permute-start(f32[2,128,128]{2,1,0:T(8,128)S(1)} %get-tuple-element.40), channel_id=1, source_target_pairs={{0,8},{4,12},{8,0},{12,4},{16,24},{20,28},{24,16},{28,20},{1,9},{5... | collective-permute-start | bytes 393224 | tf_op jit(solution)/shard_map/ppermute | solution.py:169
  24.3 1.1 %collective-permute-start.6 = (f32[2,128,128]{2,1,0:T(8,128)S(1)}, f32[2,128,128]{2,1,0:T(8,128)S(1)}, u32[]{:S(2)}, u32[]{:S(2)}) collective-permute-start(f32[2,128,128]{2,1,0:T(8,128)S(1)} %get-tuple-element.41), channel_id=1, source_target_pairs={{0,4},{4,0},{8,12},{12,8},{16,20},{20,16},{24,28},{28,24},{1,5},{5... | collective-permute-start | bytes 393224 | tf_op jit(solution)/shard_map/ppermute | solution.py:169
  25.4 1.4 %shard_map.84 = (bf16[2,128,512]{2,1,0:T(8,128)(2,1)S(1)}, f32[2,128,512]{2,1,0:T(8,128)S(1)}) custom-call(bf16[2,128,512]{2,1,0:T(8,128)(2,1)S(1)} %copy-done.4, bf16[2,128,512]{2,1,0:T(8,128)(2,1)S(1)} %copy-done.1, bf16[2,128,512]{2,1,0:T(8,128)(2,1)S(1)} %copy-done.3), custom_call_target="tpu_custom_call" | custom-call | flops 67108864 | bytes 1572864 | tf_op jit(solution)/shard_map/pallas_call | solution.py:156
  26.7 2.3 %collective-permute-done.4.rest_1_ = f32[2,128,128]{2,1,0:T(8,128)S(1)} collective-permute-done((f32[2,128,128]{2,1,0:T(8,128)S(1)}, f32[2,128,128]{2,1,0:T(8,128)S(1)}, u32[]{:S(2)}, u32[]{:S(2)}) %collective-permute-start.4) | collective-permute-done | bytes 131104 | tf_op jit(solution)/shard_map/ppermute | solution.py:169
  29.1 1.4 %collective-permute-done.6.rest_3_ = f32[2,128,128]{2,1,0:T(8,128)S(1)} collective-permute-done((f32[2,128,128]{2,1,0:T(8,128)S(1)}, f32[2,128,128]{2,1,0:T(8,128)S(1)}, u32[]{:S(2)}, u32[]{:S(2)}) %collective-permute-start.6) | collective-permute-done | bytes 131104 | tf_op jit(solution)/shard_map/ppermute | solution.py:169
  31.2 1.3 %collective-permute-start.8 = (f32[8,128]{1,0:T(8,128)S(1)}, f32[8,128]{1,0:T(8,128)S(1)}, u32[]{:S(2)}, u32[]{:S(2)}) collective-permute-start(f32[8,128]{1,0:T(8,128)S(1)} %get-tuple-element.43.rest_0_), channel_id=1, source_target_pairs={{0,2},{1,3},{2,0},{3,1},{4,6},{5,7},{6,4},{7,5},{8,10},{9,11},{10,... | collective-permute-start | bytes 12296 | tf_op jit(solution)/shard_map/ppermute | solution.py:241
  32.7 2.1 %collective-permute-done.8.rest_2_ = f32[8,128]{1,0:T(8,128)S(1)} collective-permute-done((f32[8,128]{1,0:T(8,128)S(1)}, f32[8,128]{1,0:T(8,128)S(1)}, u32[]{:S(2)}, u32[]{:S(2)}) %collective-permute-start.8) | collective-permute-done | bytes 4128 | tf_op jit(solution)/shard_map/ppermute | solution.py:241
  37.1 2.6 %collective-permute-start.12 = (f32[2,128,128]{2,1,0:T(8,128)S(1)}, f32[2,128,128]{2,1,0:T(8,128)S(1)}, u32[]{:S(2)}, u32[]{:S(2)}) collective-permute-start(f32[2,128,128]{2,1,0:T(8,128)S(1)} %get-tuple-element.55), channel_id=1, source_target_pairs={{0,12},{4,8},{8,4},{12,0},{16,28},{20,24},{24,20},{28,16},{1,13},{... | collective-permute-start | bytes 393224 | tf_op jit(solution)/shard_map/ppermute | solution.py:169
  39.6 2.9 %collective-permute-done.10.refs_1_ = f32[2,128,128]{2,1,0:T(8,128)S(1)} collective-permute-done((f32[2,128,128]{2,1,0:T(8,128)S(1)}, f32[2,128,128]{2,1,0:T(8,128)S(1)}, u32[]{:S(2)}, u32[]{:S(2)}) %collective-permute-start.10) | collective-permute-done | bytes 131104 | tf_op jit(solution)/shard_map/ppermute | solution.py:169
  42.5 1.6 %collective-permute-done.12.refs_3_ = f32[2,128,128]{2,1,0:T(8,128)S(1)} collective-permute-done((f32[2,128,128]{2,1,0:T(8,128)S(1)}, f32[2,128,128]{2,1,0:T(8,128)S(1)}, u32[]{:S(2)}, u32[]{:S(2)}) %collective-permute-start.12) | collective-permute-done | bytes 131104 | tf_op jit(solution)/shard_map/ppermute | solution.py:169
  44.2 2.2 %collective-permute-start.13 = (f32[2,128,128]{2,1,0:T(8,128)S(1)}, f32[2,128,128]{2,1,0:T(8,128)S(1)}, u32[]{:S(2)}, u32[]{:S(2)}) collective-permute-start(f32[2,128,128]{2,1,0:T(8,128)S(1)} %add_add_fusion), channel_id=1, source_target_pairs={{0,16},{4,20},{8,24},{12,28},{16,0},{20,4},{24,8},{28,12},{1,17},{... | collective-permute-start | bytes 393224 | tf_op jit(solution)/shard_map/ppermute | solution.py:174
  46.4 5.2 %collective-permute-done.13 = f32[2,128,128]{2,1,0:T(8,128)S(1)} collective-permute-done((f32[2,128,128]{2,1,0:T(8,128)S(1)}, f32[2,128,128]{2,1,0:T(8,128)S(1)}, u32[]{:S(2)}, u32[]{:S(2)}) %collective-permute-start.13) | collective-permute-done | bytes 131104 | tf_op jit(solution)/shard_map/ppermute | solution.py:174
  51.9 2.2 %collective-permute-start.15 = (f32[2,128,128]{2,1,0:T(8,128)S(1)}, f32[2,128,128]{2,1,0:T(8,128)S(1)}, u32[]{:S(2)}, u32[]{:S(2)}) collective-permute-start(f32[2,128,128]{2,1,0:T(8,128)S(1)} %get-tuple-element.58), channel_id=1, source_target_pairs={{0,8},{4,12},{8,0},{12,4},{16,24},{20,28},{24,16},{28,20},{1,9},{5... | collective-permute-start | bytes 393224 | tf_op jit(solution)/shard_map/ppermute | solution.py:169
  54.1 1.2 %collective-permute-start.16 = (f32[2,128,128]{2,1,0:T(8,128)S(1)}, f32[2,128,128]{2,1,0:T(8,128)S(1)}, u32[]{:S(2)}, u32[]{:S(2)}) collective-permute-start(f32[2,128,128]{2,1,0:T(8,128)S(1)} %get-tuple-element.59), channel_id=1, source_target_pairs={{0,4},{4,0},{8,12},{12,8},{16,20},{20,16},{24,28},{28,24},{1,5},{5... | collective-permute-start | bytes 393224 | tf_op jit(solution)/shard_map/ppermute | solution.py:169
  55.3 2.6 %shard_map.89 = (bf16[2,128,512]{2,1,0:T(8,128)(2,1)}, bf16[2,128,512]{2,1,0:T(8,128)(2,1)}, f32[2,128,512]{2,1,0:T(8,128)S(1)}, f32[2,128,512]{2,1,0:T(8,128)S(1)}) custom-call(bf16[2,128,512]{2,1,0:T(8,128)(2,1)S(1)} %copy-done.4, bf16[2,128,512]{2,1,0:T(8,128)(2,1)S(1)} %copy-done.1, bf16[2,128,512]{2,1,0:T(8,128)(2,1)S(1)} %copy-done.3, ...), custom_call_target="tpu_custom_call" | custom-call | flops 167772160 | bytes 3805184 | tf_op jit(solution)/shard_map/pallas_call | solution.py:156
  59.1 1.2 %shard_map.91 = (bf16[2,128,512]{2,1,0:T(8,128)(2,1)}, bf16[2,128,512]{2,1,0:T(8,128)(2,1)}) custom-call(s32[1]{0:T(128)} %bitcast.place_ref, bf16[2,128,512]{2,1,0:T(8,128)(2,1)S(1)} %copy-done.1, bf16[2,128,512]{2,1,0:T(8,128)(2,1)S(1)} %copy-done.3, f32[2,128,512]{2,1,0:T(8,128)S(1)} %get-tuple-element.50.gkl_ref, ...), custom_call_target="tpu_custom_call" | custom-call | flops 67108864 | bytes 2621444 | tf_op jit(solution)/shard_map/pallas_call | solution.py:156
  (36 shorter events, 6.9 us)
Async XLA Ops:
  0.6 1.0 %copy-start = (bf16[2,128,512]{2,1,0:T(8,128)(2,1)S(1)}, bf16[2,128,512]{2,1,0:T(8,128)(2,1)}, u32[]{:S(2)}) copy-start(bf16[2,128,512]{2,1,0:T(8,128)(2,1)} %k_ref.7) | copy-start | bytes 786436
  1.6 0.9 %copy-start.2 = (bf16[2,128,512]{2,1,0:T(8,128)(2,1)S(1)}, bf16[2,128,512]{2,1,0:T(8,128)(2,1)}, u32[]{:S(2)}) copy-start(bf16[2,128,512]{2,1,0:T(8,128)(2,1)} %v_ref.7) | copy-start | bytes 786436
  2.8 6.5 %collective-permute-start = (f32[2,128,128]{2,1,0:T(8,128)S(1)}, f32[2,128,128]{2,1,0:T(8,128)S(1)}, u32[]{:S(2)}, u32[]{:S(2)}) collective-permute-start(f32[2,128,128]{2,1,0:T(8,128)S(1)} %get-tuple-element.35), channel_id=1, source_target_pairs={{0,4},{4,0},{8,12},{12,8},{16,20},{20,16},{24,28},{28,24},{1,5},{5... | collective-permute-start | bytes 393224 | tf_op jit(solution)/shard_map/ppermute | solution.py:169
  5.8 6.4 %collective-permute-start.1 = (f32[2,128,128]{2,1,0:T(8,128)S(1)}, f32[2,128,128]{2,1,0:T(8,128)S(1)}, u32[]{:S(2)}, u32[]{:S(2)}) collective-permute-start(f32[2,128,128]{2,1,0:T(8,128)S(1)} %get-tuple-element.36), channel_id=1, source_target_pairs={{0,8},{4,12},{8,0},{12,4},{16,24},{20,28},{24,16},{28,20},{1,9},{5... | collective-permute-start | bytes 393224 | tf_op jit(solution)/shard_map/ppermute | solution.py:169
  7.4 6.0 %collective-permute-start.2 = (f32[2,128,128]{2,1,0:T(8,128)S(1)}, f32[2,128,128]{2,1,0:T(8,128)S(1)}, u32[]{:S(2)}, u32[]{:S(2)}) collective-permute-start(f32[2,128,128]{2,1,0:T(8,128)S(1)} %get-tuple-element.37), channel_id=1, source_target_pairs={{0,12},{4,8},{8,4},{12,0},{16,28},{20,24},{24,20},{28,16},{1,13},{... | collective-permute-start | bytes 393224 | tf_op jit(solution)/shard_map/ppermute | solution.py:169
  13.4 8.2 %collective-permute-start.3 = (f32[2,128,128]{2,1,0:T(8,128)S(1)}, f32[2,128,128]{2,1,0:T(8,128)S(1)}, u32[]{:S(2)}, u32[]{:S(2)}) collective-permute-start(f32[2,128,128]{2,1,0:T(8,128)S(1)} %add_add_fusion.1), channel_id=1, source_target_pairs={{0,16},{4,20},{8,24},{12,28},{16,0},{20,4},{24,8},{28,12},{1,17},{... | collective-permute-start | bytes 393224 | tf_op jit(solution)/shard_map/ppermute | solution.py:174
  21.7 3.7 %copy-start.4 = (bf16[2,128,512]{2,1,0:T(8,128)(2,1)S(1)}, bf16[2,128,512]{2,1,0:T(8,128)(2,1)}, u32[]{:S(2)}) copy-start(bf16[2,128,512]{2,1,0:T(8,128)(2,1)} %q_ref.7) | copy-start | bytes 786436
  21.7 3.7 %copy-start.1 = (bf16[2,128,512]{2,1,0:T(8,128)(2,1)S(1)}, bf16[2,128,512]{2,1,0:T(8,128)(2,1)}, u32[]{:S(2)}) copy-start(bf16[2,128,512]{2,1,0:T(8,128)(2,1)} %k_ref.7) | copy-start | bytes 786436
  21.7 3.7 %copy-start.3 = (bf16[2,128,512]{2,1,0:T(8,128)(2,1)S(1)}, bf16[2,128,512]{2,1,0:T(8,128)(2,1)}, u32[]{:S(2)}) copy-start(bf16[2,128,512]{2,1,0:T(8,128)(2,1)} %v_ref.7) | copy-start | bytes 786436
  21.8 7.3 %collective-permute-start.4 = (f32[2,128,128]{2,1,0:T(8,128)S(1)}, f32[2,128,128]{2,1,0:T(8,128)S(1)}, u32[]{:S(2)}, u32[]{:S(2)}) collective-permute-start(f32[2,128,128]{2,1,0:T(8,128)S(1)} %get-tuple-element.39), channel_id=1, source_target_pairs={{0,12},{4,8},{8,4},{12,0},{16,28},{20,24},{24,20},{28,16},{1,13},{... | collective-permute-start | bytes 393224 | tf_op jit(solution)/shard_map/ppermute | solution.py:169
  22.9 6.2 %collective-permute-start.5 = (f32[2,128,128]{2,1,0:T(8,128)S(1)}, f32[2,128,128]{2,1,0:T(8,128)S(1)}, u32[]{:S(2)}, u32[]{:S(2)}) collective-permute-start(f32[2,128,128]{2,1,0:T(8,128)S(1)} %get-tuple-element.40), channel_id=1, source_target_pairs={{0,8},{4,12},{8,0},{12,4},{16,24},{20,28},{24,16},{28,20},{1,9},{5... | collective-permute-start | bytes 393224 | tf_op jit(solution)/shard_map/ppermute | solution.py:169
  24.3 6.2 %copy-start.5 = (bf16[2,128,512]{2,1,0:T(8,128)(2,1)S(1)}, bf16[2,128,512]{2,1,0:T(8,128)(2,1)}, u32[]{:S(2)}) copy-start(bf16[2,128,512]{2,1,0:T(8,128)(2,1)} %g_ref.3) | copy-start | bytes 786436
  24.3 6.2 %collective-permute-start.6 = (f32[2,128,128]{2,1,0:T(8,128)S(1)}, f32[2,128,128]{2,1,0:T(8,128)S(1)}, u32[]{:S(2)}, u32[]{:S(2)}) collective-permute-start(f32[2,128,128]{2,1,0:T(8,128)S(1)} %get-tuple-element.41), channel_id=1, source_target_pairs={{0,4},{4,0},{8,12},{12,8},{16,20},{20,16},{24,28},{28,24},{1,5},{5... | collective-permute-start | bytes 393224 | tf_op jit(solution)/shard_map/ppermute | solution.py:169
  25.4 5.1 %copy-start.6 = (f32[2,512]{1,0:T(2,128)S(1)}, f32[2,512]{1,0:T(2,128)}, u32[]{:S(2)}) copy-start(f32[2,512]{1,0:T(2,128)} %gain_ref.5) | copy-start | bytes 12292
  30.9 1.8 %collective-permute-start.7 = (f32[8,128]{1,0:T(8,128)S(1)}, f32[8,128]{1,0:T(8,128)S(1)}, u32[]{:S(2)}, u32[]{:S(2)}) collective-permute-start(f32[8,128]{1,0:T(8,128)S(1)} %get-tuple-element.43.rest_0_), channel_id=1, source_target_pairs={{0,3},{1,0},{2,1},{3,2},{4,7},{5,4},{6,5},{7,6},{8,11},{9,8},{10,9... | collective-permute-start | bytes 12296 | tf_op jit(solution)/shard_map/ppermute | solution.py:241
  31.2 3.6 %collective-permute-start.8 = (f32[8,128]{1,0:T(8,128)S(1)}, f32[8,128]{1,0:T(8,128)S(1)}, u32[]{:S(2)}, u32[]{:S(2)}) collective-permute-start(f32[8,128]{1,0:T(8,128)S(1)} %get-tuple-element.43.rest_0_), channel_id=1, source_target_pairs={{0,2},{1,3},{2,0},{3,1},{4,6},{5,7},{6,4},{7,5},{8,10},{9,11},{10,... | collective-permute-start | bytes 12296 | tf_op jit(solution)/shard_map/ppermute | solution.py:241
  32.5 3.0 %collective-permute-start.9 = (f32[8,128]{1,0:T(8,128)S(1)}, f32[8,128]{1,0:T(8,128)S(1)}, u32[]{:S(2)}, u32[]{:S(2)}) collective-permute-start(f32[8,128]{1,0:T(8,128)S(1)} %get-tuple-element.43.rest_0_), channel_id=1, source_target_pairs={{0,1},{1,2},{2,3},{3,0},{4,5},{5,6},{6,7},{7,4},{8,9},{9,10},{10,1... | collective-permute-start | bytes 12296 | tf_op jit(solution)/shard_map/ppermute | solution.py:241
  36.1 6.4 %collective-permute-start.10 = (f32[2,128,128]{2,1,0:T(8,128)S(1)}, f32[2,128,128]{2,1,0:T(8,128)S(1)}, u32[]{:S(2)}, u32[]{:S(2)}) collective-permute-start(f32[2,128,128]{2,1,0:T(8,128)S(1)} %get-tuple-element.53), channel_id=1, source_target_pairs={{0,4},{4,0},{8,12},{12,8},{16,20},{20,16},{24,28},{28,24},{1,5},{5... | collective-permute-start | bytes 393224 | tf_op jit(solution)/shard_map/ppermute | solution.py:169
  36.8 5.8 %collective-permute-start.11 = (f32[2,128,128]{2,1,0:T(8,128)S(1)}, f32[2,128,128]{2,1,0:T(8,128)S(1)}, u32[]{:S(2)}, u32[]{:S(2)}) collective-permute-start(f32[2,128,128]{2,1,0:T(8,128)S(1)} %get-tuple-element.54), channel_id=1, source_target_pairs={{0,8},{4,12},{8,0},{12,4},{16,24},{20,28},{24,16},{28,20},{1,9},{5... | collective-permute-start | bytes 393224 | tf_op jit(solution)/shard_map/ppermute | solution.py:169
  37.1 7.1 %collective-permute-start.12 = (f32[2,128,128]{2,1,0:T(8,128)S(1)}, f32[2,128,128]{2,1,0:T(8,128)S(1)}, u32[]{:S(2)}, u32[]{:S(2)}) collective-permute-start(f32[2,128,128]{2,1,0:T(8,128)S(1)} %get-tuple-element.55), channel_id=1, source_target_pairs={{0,12},{4,8},{8,4},{12,0},{16,28},{20,24},{24,20},{28,16},{1,13},{... | collective-permute-start | bytes 393224 | tf_op jit(solution)/shard_map/ppermute | solution.py:169
  44.2 7.4 %collective-permute-start.13 = (f32[2,128,128]{2,1,0:T(8,128)S(1)}, f32[2,128,128]{2,1,0:T(8,128)S(1)}, u32[]{:S(2)}, u32[]{:S(2)}) collective-permute-start(f32[2,128,128]{2,1,0:T(8,128)S(1)} %add_add_fusion), channel_id=1, source_target_pairs={{0,16},{4,20},{8,24},{12,28},{16,0},{20,4},{24,8},{28,12},{1,17},{... | collective-permute-start | bytes 393224 | tf_op jit(solution)/shard_map/ppermute | solution.py:174
  51.7 6.2 %collective-permute-start.14 = (f32[2,128,128]{2,1,0:T(8,128)S(1)}, f32[2,128,128]{2,1,0:T(8,128)S(1)}, u32[]{:S(2)}, u32[]{:S(2)}) collective-permute-start(f32[2,128,128]{2,1,0:T(8,128)S(1)} %get-tuple-element.57), channel_id=1, source_target_pairs={{0,12},{4,8},{8,4},{12,0},{16,28},{20,24},{24,20},{28,16},{1,13},{... | collective-permute-start | bytes 393224 | tf_op jit(solution)/shard_map/ppermute | solution.py:169
  51.9 6.5 %collective-permute-start.15 = (f32[2,128,128]{2,1,0:T(8,128)S(1)}, f32[2,128,128]{2,1,0:T(8,128)S(1)}, u32[]{:S(2)}, u32[]{:S(2)}) collective-permute-start(f32[2,128,128]{2,1,0:T(8,128)S(1)} %get-tuple-element.58), channel_id=1, source_target_pairs={{0,8},{4,12},{8,0},{12,4},{16,24},{20,28},{24,16},{28,20},{1,9},{5... | collective-permute-start | bytes 393224 | tf_op jit(solution)/shard_map/ppermute | solution.py:169
  54.1 5.0 %collective-permute-start.16 = (f32[2,128,128]{2,1,0:T(8,128)S(1)}, f32[2,128,128]{2,1,0:T(8,128)S(1)}, u32[]{:S(2)}, u32[]{:S(2)}) collective-permute-start(f32[2,128,128]{2,1,0:T(8,128)S(1)} %get-tuple-element.59), channel_id=1, source_target_pairs={{0,4},{4,0},{8,12},{12,8},{16,20},{20,16},{24,28},{28,24},{1,5},{5... | collective-permute-start | bytes 393224 | tf_op jit(solution)/shard_map/ppermute | solution.py:169

commit v4 on v3

--- a/solution.py
+++ b/solution.py
@@ -10,11 +10,7 @@
 DH = 128
 CH = 128
 GROUP = 4
-ORDERS = ((1, 2, 3), (3, 2, 1), (1, 2, 3), (3, 2, 1))
-CYCLIC = True
-BARRIER = False
-AR = (3, 2, 1)
-RING = True
+ORDERS = ((2, 1, 3), (3, 1, 2), (1, 3, 2), (3, 1, 2))
 
 EPSILON = 1e-06
 SCALE = DH ** (-0.5)
@@ -36,7 +32,17 @@
     return rows >= cols
 
 
-def kv_kernel(order, place_ref, k_ref, v_ref, *outs):
+def kv_kernel(order, place_ref, k_hbm, v_hbm, k_ref, v_ref, *rest):
+    outs, sems = rest[:GROUP], rest[GROUP]
+    loads = [
+        pltpu.make_async_copy(src.at[layer], dst.at[layer], sems.at[i, layer])
+        for layer in range(k_ref.shape[0])
+        for i, (src, dst) in enumerate(((k_hbm, k_ref), (v_hbm, v_ref)))
+    ]
+    for load in loads:
+        load.start()
+    for load in loads:
+        load.wait()
     place = place_ref[0]
     for turn, out in zip((0, *order), outs):
         at = lanes(lax.bitwise_xor(place, turn))
@@ -136,8 +142,9 @@
 
 
 def outer_kernel(order, place_ref, k_ref, v_ref, gkl_ref, gvl_ref, *rest):
-    backs, (gk_ref, gv_ref) = rest[:GROUP], rest[GROUP:]
-    place = place_ref[0]
+    backs, (gk_hbm, gv_hbm, gk_ref, gv_ref, sems) = rest[:GROUP], rest[GROUP:]
+    place = place_ref[0]
+    stores = []
     for layer in range(k_ref.shape[0]):
         for turn, back in zip((0, *order), backs):
             at = lanes(lax.bitwise_xor(place, turn))
@@ -146,22 +153,33 @@
             gv = dot(k_ref[layer, :, at], b16, 1, 0) + gvl_ref[layer, :, at]
             gk_ref[layer, :, at] = gk.astype(BF16)
             gv_ref[layer, :, at] = gv.astype(BF16)
-
-
-def call(body, outs, smem, flops, *args, hbm=()):
-    moved = sum(a.size * a.dtype.itemsize for a in [*args, *outs])
-    args = args[:smem] + tuple(
-        pltpu.with_memory_space_constraint(a, pltpu.VMEM) for a in args[smem:]
-    )
+        for i, (src, dst) in enumerate(((gk_ref, gk_hbm), (gv_ref, gv_hbm))):
+            store = pltpu.make_async_copy(src.at[layer], dst.at[layer], sems.at[i, layer])
+            store.start()
+            stores.append(store)
+    for store in stores:
+        store.wait()
+
+
+def call(body, outs, smem, flops, *args, hbm=(), held=(), scratch=(), manual=False):
+    moved = sum(a.size * a.dtype.itemsize for a in [*args, *held, *outs])
+    inputs = [pltpu.with_memory_space_constraint(a, pltpu.VMEM) for a in args[smem:]]
+    spec = lambda space: pl.BlockSpec(memory_space=space)
     return pl.pallas_call(
         body,
-        out_shape=[a if i in hbm else pltpu.VMEM(a.shape, a.dtype) for i, a in enumerate(outs)],
+        out_shape=[
+            a if i in hbm else pltpu.VMEM(a.shape, a.dtype) for i, a in enumerate(outs)
+        ],
+        in_specs=[spec(pltpu.SMEM)] * smem
+        + [spec(pltpu.VMEM)] * len(inputs)
+        + [spec(pltpu.HBM)] * len(held),
+        out_specs=[
+            spec(pltpu.HBM if manual and i in hbm else pltpu.VMEM) for i in range(len(outs))
+        ],
+        scratch_shapes=scratch,
         compiler_params=pltpu.CompilerParams(vmem_limit_bytes=4 * 2**20),
-        in_specs=[pl.BlockSpec(memory_space=pltpu.SMEM)] * smem
-        + [pl.BlockSpec(memory_space=pltpu.VMEM)] * (len(args) - smem),
-        out_specs=[pl.BlockSpec(memory_space=pltpu.VMEM)] * len(outs),
         cost_estimate=pl.CostEstimate(flops=flops, bytes_accessed=moved, transcendentals=0),
-    )(*args)
+    )(*args[:smem], *inputs, *[pltpu.with_memory_space_constraint(a, pltpu.HBM) for a in held])
 
 
 def carried(chunks, place, count, reverse, beside, order, order_back):
@@ -169,20 +187,13 @@
         return lax.ppermute(array, "seq", [(i, i ^ turn) for i in range(count)])
 
     def shift(array, by):
-        if CYCLIC:
-            step = -by if reverse else by
-            moved = lax.ppermute(array, "seq", [(i, (i + step) % count) for i in range(count)])
-            inside = place < count - by if reverse else place >= by
-            return jnp.where(inside, moved, 0.0)
-        pairs = [(i, i + by) for i in range(count - by)]
-        if reverse:
-            pairs = [(b, a) for a, b in pairs]
-        return lax.ppermute(array, "seq", pairs)
+        step = -by if reverse else by
+        moved = lax.ppermute(array, "seq", [(i, (i + step) % count) for i in range(count)])
+        inside = place < count - by if reverse else place >= by
+        return jnp.where(inside, moved, 0.0)
 
     got = [chunks[0]] + [swap(chunks[1 + j], t) for j, t in enumerate(order)]
     extra = beside()
-    if BARRIER:
-        got, extra = lax.optimization_barrier((got, extra))
     total = got[0] + got[1] + got[2] + got[3]
     outside = shift(total, GROUP)
     by = 1
@@ -213,7 +224,16 @@
     blocks = [jax.ShapeDtypeStruct((layers, DH, DH), F32)] * GROUP
     product = 2 * layers * heads * CH * DH * DH
 
-    kv = call(functools.partial(kv_kernel, ORDERS[0]), blocks, 1, product, place_arg, keys, values)
+    keys, values, *kv = call(
+        functools.partial(kv_kernel, ORDERS[0]),
+        [wide(BF16), wide(BF16), *blocks],
+        1,
+        product,
+        place_arg,
+        held=(keys, values),
+        scratch=[pltpu.SemaphoreType.DMA((2, layers))],
+    )
+    queries, out_grad, kv = lax.optimization_barrier((queries, out_grad, kv))
     states, (weights, local) = carried(
         kv,
         place,
@@ -237,10 +257,11 @@
         out_gain,
         *states,
     )
-    parts = [sums] + [
-        lax.ppermute(sums, "head", [(i, (i + by) % head_count if RING else i ^ by) for i in range(head_count)])
-        for by in AR
-    ]
+    def across(array, by):
+        pairs = [(i, (i + by) % head_count) for i in range(head_count)]
+        return lax.ppermute(array, "head", pairs)
+
+    parts = [sums] + [across(sums, by) for by in range(head_count - 1, 0, -1)]
     ga, inv, *products = call(
         functools.partial(grad_kernel, width * head_count, ORDERS[2]),
         [wide(BF16), jax.ShapeDtypeStruct((layers, CH, DH), F32), *blocks],
@@ -277,6 +298,7 @@
         ORDERS[2],
         ORDERS[3],
     )
+    tile = pltpu.VMEM(queries.shape, BF16)
     grad_k, grad_v = call(
         functools.partial(outer_kernel, ORDERS[3]),
         [wide(BF16), wide(BF16)],
@@ -289,6 +311,8 @@
         gv_local,
         *later,
         hbm=(0, 1),
+        scratch=[tile, tile, pltpu.SemaphoreType.DMA((2, layers))],
+        manual=True,
     )
     return normed, grad_q, grad_k, grad_v
 

time: 60.4 us -> 58.2 us (0.964)
  waiting for transfers between devices: 28.9 us -> 26 us
  local copies, waits for them, and re-layouts: 1.92 us -> 0.01 us
  starting transfers between devices: 22 us -> 23.6 us
  Pallas kernels: 6.56 us -> 7.64 us
    unnamed x14 -> x6, local copies, waits for them, and re-layouts: 1.92 us -> 0.01 us
    ppermute x2, waiting for transfers between devices: 10.6 us -> 9.07 us  [shift(): lax.ppermute(array, 'seq', [(i, (i + step) % count) for i in range(count)])]
    ppermute x2, starting transfers between devices: 5.03 us -> 6.5 us  [shift(): lax.ppermute(array, 'seq', [(i, (i + step) % count) for i in range(count)])]
    ppermute x12, waiting for transfers between devices: 15.4 us -> 14.1 us  [swap(): return lax.ppermute(array, 'seq', [(i, i ^ turn) for i in range(count)])]
    pallas_call x8, Pallas kernels: 6.56 us -> 7.64 us  [call(): pl.pallas_call(body, out_shape=[a if i in hbm else pltpu.VMEM(a.shape, a....]
where the time goes in v4:
time: 58.2 us; the launch traced here: 58.1 us
  waiting for transfers between devices  26 us (45%)
  starting transfers between devices  23.6 us (41%)
  Pallas kernels  7.64 us (13%)
  between operations  0.71 us (1%)
    ppermute x12, starting transfers between devices, swap(): return lax.ppermute(array, 'seq', [(i, i ^ turn) for i in range(count)])  15.3 us
    ppermute x12, waiting for transfers between devices, swap(): return lax.ppermute(array, 'seq', [(i, i ^ turn) for i in range(count)])  14.1 us
    ppermute x2, waiting for transfers between devices, shift(): lax.ppermute(array, 'seq', [(i, (i + step) % count) for i in range(count)])  9.07 us
    pallas_call x8, Pallas kernels, call(): pl.pallas_call(body, out_shape=[a if i in hbm else pltpu.VMEM(a.shape, a....  7.64 us
    ppermute x2, starting transfers between devices, shift(): lax.ppermute(array, 'seq', [(i, (i + step) % count) for i in range(count)])  6.5 us
    ppermute x3, waiting for transfers between devices, across(): return lax.ppermute(array, 'head', pairs)  2.87 us
    ppermute x3, starting transfers between devices, across(): return lax.ppermute(array, 'head', pairs)  1.79 us
  transfers between devices with their start and end apart: 17, of which 13 were waited for; matrix products, arithmetic and copies ran while one was open for 0% of the time, Pallas kernels for 7%

profile of v4, /device:TPU:0, one launch (start us, length us, event | category | flops | bytes accessed | tf_op | source)
XLA Modules:
  0.0 58.1 jit_solution(2491979762513538484)
XLA Ops:
  0.6 1.4 %shard_map.84 = (bf16[2,128,512]{2,1,0:T(8,128)(2,1)S(1)}, bf16[2,128,512]{2,1,0:T(8,128)(2,1)S(1)}, f32[2,128,128]{2,1,0:T(8,128)S(1)}, f32[2,128,128]{2,1,0:T(...) custom-call(s32[1]{0:T(128)} %bitcast.place_ref, bf16[2,128,512]{2,1,0:T(8,128)(2,1)} %k_hbm.1, ...), custom_call_target="tpu_custom_call" | custom-call | flops 33554432 | bytes 1572868 | tf_op jit(solution)/shard_map/pallas_call | solution.py:168
  2.0 3.1 %collective-permute-start = (f32[2,128,128]{2,1,0:T(8,128)S(1)}, f32[2,128,128]{2,1,0:T(8,128)S(1)}, u32[]{:S(2)}, u32[]{:S(2)}) collective-permute-start(f32[2,128,128]{2,1,0:T(8,128)S(1)} %get-tuple-element.51), channel_id=1, source_target_pairs={{0,8},{4,12},{8,0},{12,4},{16,24},{20,28},{24,16},{28,20},{1,9},{5... | collective-permute-start | bytes 393224 | tf_op jit(solution)/shard_map/ppermute | solution.py:187
  5.1 1.5 %collective-permute-start.1 = (f32[2,128,128]{2,1,0:T(8,128)S(1)}, f32[2,128,128]{2,1,0:T(8,128)S(1)}, u32[]{:S(2)}, u32[]{:S(2)}) collective-permute-start(f32[2,128,128]{2,1,0:T(8,128)S(1)} %get-tuple-element.52), channel_id=1, source_target_pairs={{0,4},{4,0},{8,12},{12,8},{16,20},{20,16},{24,28},{28,24},{1,5},{5... | collective-permute-start | bytes 393224 | tf_op jit(solution)/shard_map/ppermute | solution.py:187
  6.7 2.4 %collective-permute-done.refs_1_ = f32[2,128,128]{2,1,0:T(8,128)S(1)} collective-permute-done((f32[2,128,128]{2,1,0:T(8,128)S(1)}, f32[2,128,128]{2,1,0:T(8,128)S(1)}, u32[]{:S(2)}, u32[]{:S(2)}) %collective-permute-start) | collective-permute-done | bytes 131104 | tf_op jit(solution)/shard_map/ppermute | solution.py:187
  9.0 3.9 %collective-permute-done.1.refs_2_ = f32[2,128,128]{2,1,0:T(8,128)S(1)} collective-permute-done((f32[2,128,128]{2,1,0:T(8,128)S(1)}, f32[2,128,128]{2,1,0:T(8,128)S(1)}, u32[]{:S(2)}, u32[]{:S(2)}) %collective-permute-start.1) | collective-permute-done | bytes 131104 | tf_op jit(solution)/shard_map/ppermute | solution.py:187
  12.9 2.7 %collective-permute-start.3 = (f32[2,128,128]{2,1,0:T(8,128)S(1)}, f32[2,128,128]{2,1,0:T(8,128)S(1)}, u32[]{:S(2)}, u32[]{:S(2)}) collective-permute-start(f32[2,128,128]{2,1,0:T(8,128)S(1)} %add_add_fusion.1), channel_id=1, source_target_pairs={{0,16},{4,20},{8,24},{12,28},{16,0},{20,4},{24,8},{28,12},{1,17},{... | collective-permute-start | bytes 393224 | tf_op jit(solution)/shard_map/ppermute | solution.py:191
  15.6 4.9 %collective-permute-done.3 = f32[2,128,128]{2,1,0:T(8,128)S(1)} collective-permute-done((f32[2,128,128]{2,1,0:T(8,128)S(1)}, f32[2,128,128]{2,1,0:T(8,128)S(1)}, u32[]{:S(2)}, u32[]{:S(2)}) %collective-permute-start.3) | collective-permute-done | bytes 131104 | tf_op jit(solution)/shard_map/ppermute | solution.py:191
  21.4 1.4 %collective-permute-start.5 = (f32[2,128,128]{2,1,0:T(8,128)S(1)}, f32[2,128,128]{2,1,0:T(8,128)S(1)}, u32[]{:S(2)}, u32[]{:S(2)}) collective-permute-start(f32[2,128,128]{2,1,0:T(8,128)S(1)} %get-tuple-element.56), channel_id=1, source_target_pairs={{0,4},{4,0},{8,12},{12,8},{16,20},{20,16},{24,28},{28,24},{1,5},{5... | collective-permute-start | bytes 393224 | tf_op jit(solution)/shard_map/ppermute | solution.py:187
  22.8 1.4 %collective-permute-start.6 = (f32[2,128,128]{2,1,0:T(8,128)S(1)}, f32[2,128,128]{2,1,0:T(8,128)S(1)}, u32[]{:S(2)}, u32[]{:S(2)}) collective-permute-start(f32[2,128,128]{2,1,0:T(8,128)S(1)} %get-tuple-element.57), channel_id=1, source_target_pairs={{0,8},{4,12},{8,0},{12,4},{16,24},{20,28},{24,16},{28,20},{1,9},{5... | collective-permute-start | bytes 393224 | tf_op jit(solution)/shard_map/ppermute | solution.py:187
  24.2 1.4 %shard_map.85 = (bf16[2,128,512]{2,1,0:T(8,128)(2,1)S(1)}, f32[2,128,512]{2,1,0:T(8,128)S(1)}) custom-call(bf16[2,128,512]{2,1,0:T(8,128)(2,1)S(1)} %copy-done, bf16[2,128,512]{2,1,0:T(8,128)(2,1)S(1)} %get-tuple-element.46.k_ref, bf16[2,128,512]{2,1,0:T(8,128)(2,1)S(1)} %get-tuple-element.47.v_ref), custom_call_target="tpu_custom_call" | custom-call | flops 67108864 | bytes 1572864 | tf_op jit(solution)/shard_map/pallas_call | solution.py:168
  25.6 1.1 %collective-permute-done.4.rest_1_ = f32[2,128,128]{2,1,0:T(8,128)S(1)} collective-permute-done((f32[2,128,128]{2,1,0:T(8,128)S(1)}, f32[2,128,128]{2,1,0:T(8,128)S(1)}, u32[]{:S(2)}, u32[]{:S(2)}) %collective-permute-start.4) | collective-permute-done | bytes 131104 | tf_op jit(solution)/shard_map/ppermute | solution.py:187
  26.7 1.1 %collective-permute-done.5.rest_2_ = f32[2,128,128]{2,1,0:T(8,128)S(1)} collective-permute-done((f32[2,128,128]{2,1,0:T(8,128)S(1)}, f32[2,128,128]{2,1,0:T(8,128)S(1)}, u32[]{:S(2)}, u32[]{:S(2)}) %collective-permute-start.5) | collective-permute-done | bytes 131104 | tf_op jit(solution)/shard_map/ppermute | solution.py:187
  28.6 1.6 %collective-permute-start.8 = (f32[8,128]{1,0:T(8,128)S(1)}, f32[8,128]{1,0:T(8,128)S(1)}, u32[]{:S(2)}, u32[]{:S(2)}) collective-permute-start(f32[8,128]{1,0:T(8,128)S(1)} %get-tuple-element.59.rest_0_), channel_id=1, source_target_pairs={{0,2},{1,3},{2,0},{3,1},{4,6},{5,7},{6,4},{7,5},{8,10},{9,11},{10,... | collective-permute-start | bytes 12296 | tf_op jit(solution)/shard_map/ppermute | solution.py:262
  30.3 1.9 %collective-permute-done.8.rest_2_ = f32[8,128]{1,0:T(8,128)S(1)} collective-permute-done((f32[8,128]{1,0:T(8,128)S(1)}, f32[8,128]{1,0:T(8,128)S(1)}, u32[]{:S(2)}, u32[]{:S(2)}) %collective-permute-start.8) | collective-permute-done | bytes 4128 | tf_op jit(solution)/shard_map/ppermute | solution.py:262
  32.2 1.0 %collective-permute-done.9.rest_3_ = f32[8,128]{1,0:T(8,128)S(1)} collective-permute-done((f32[8,128]{1,0:T(8,128)S(1)}, f32[8,128]{1,0:T(8,128)S(1)}, u32[]{:S(2)}, u32[]{:S(2)}) %collective-permute-start.9) | collective-permute-done | bytes 4128 | tf_op jit(solution)/shard_map/ppermute | solution.py:262
  33.8 1.1 %collective-permute-start.10 = (f32[2,128,128]{2,1,0:T(8,128)S(1)}, f32[2,128,128]{2,1,0:T(8,128)S(1)}, u32[]{:S(2)}, u32[]{:S(2)}) collective-permute-start(f32[2,128,128]{2,1,0:T(8,128)S(1)} %get-tuple-element.69), channel_id=1, source_target_pairs={{0,4},{4,0},{8,12},{12,8},{16,20},{20,16},{24,28},{28,24},{1,5},{5... | collective-permute-start | bytes 393224 | tf_op jit(solution)/shard_map/ppermute | solution.py:187
  34.9 1.5 %collective-permute-start.11 = (f32[2,128,128]{2,1,0:T(8,128)S(1)}, f32[2,128,128]{2,1,0:T(8,128)S(1)}, u32[]{:S(2)}, u32[]{:S(2)}) collective-permute-start(f32[2,128,128]{2,1,0:T(8,128)S(1)} %get-tuple-element.70), channel_id=1, source_target_pairs={{0,12},{4,8},{8,4},{12,0},{16,28},{20,24},{24,20},{28,16},{1,13},{... | collective-permute-start | bytes 393224 | tf_op jit(solution)/shard_map/ppermute | solution.py:187
  37.3 1.9 %collective-permute-done.10.refs_1_ = f32[2,128,128]{2,1,0:T(8,128)S(1)} collective-permute-done((f32[2,128,128]{2,1,0:T(8,128)S(1)}, f32[2,128,128]{2,1,0:T(8,128)S(1)}, u32[]{:S(2)}, u32[]{:S(2)}) %collective-permute-start.10) | collective-permute-done | bytes 131104 | tf_op jit(solution)/shard_map/ppermute | solution.py:187
  39.2 1.5 %collective-permute-done.11.refs_2_ = f32[2,128,128]{2,1,0:T(8,128)S(1)} collective-permute-done((f32[2,128,128]{2,1,0:T(8,128)S(1)}, f32[2,128,128]{2,1,0:T(8,128)S(1)}, u32[]{:S(2)}, u32[]{:S(2)}) %collective-permute-start.11) | collective-permute-done | bytes 131104 | tf_op jit(solution)/shard_map/ppermute | solution.py:187
  41.7 3.8 %collective-permute-start.13 = (f32[2,128,128]{2,1,0:T(8,128)S(1)}, f32[2,128,128]{2,1,0:T(8,128)S(1)}, u32[]{:S(2)}, u32[]{:S(2)}) collective-permute-start(f32[2,128,128]{2,1,0:T(8,128)S(1)} %add_add_fusion), channel_id=1, source_target_pairs={{0,16},{4,20},{8,24},{12,28},{16,0},{20,4},{24,8},{28,12},{1,17},{... | collective-permute-start | bytes 393224 | tf_op jit(solution)/shard_map/ppermute | solution.py:191
  45.5 4.2 %collective-permute-done.13 = f32[2,128,128]{2,1,0:T(8,128)S(1)} collective-permute-done((f32[2,128,128]{2,1,0:T(8,128)S(1)}, f32[2,128,128]{2,1,0:T(8,128)S(1)}, u32[]{:S(2)}, u32[]{:S(2)}) %collective-permute-start.13) | collective-permute-done | bytes 131104 | tf_op jit(solution)/shard_map/ppermute | solution.py:191
  51.0 2.4 %collective-permute-start.16 = (f32[2,128,128]{2,1,0:T(8,128)S(1)}, f32[2,128,128]{2,1,0:T(8,128)S(1)}, u32[]{:S(2)}, u32[]{:S(2)}) collective-permute-start(f32[2,128,128]{2,1,0:T(8,128)S(1)} %get-tuple-element.75), channel_id=1, source_target_pairs={{0,8},{4,12},{8,0},{12,4},{16,24},{20,28},{24,16},{28,20},{1,9},{5... | collective-permute-start | bytes 393224 | tf_op jit(solution)/shard_map/ppermute | solution.py:187
  53.4 2.6 %shard_map.89 = (bf16[2,128,512]{2,1,0:T(8,128)(2,1)}, bf16[2,128,512]{2,1,0:T(8,128)(2,1)}, f32[2,128,512]{2,1,0:T(8,128)S(1)}, f32[2,128,512]{2,1,0:T(8,128)S(1)}) custom-call(bf16[2,128,512]{2,1,0:T(8,128)(2,1)S(1)} %copy-done, bf16[2,128,512]{2,1,0:T(8,128)(2,1)S(1)} %get-tuple-element.46.k_ref, bf16[2,128,512]{2,1,0:T(8,128)(2,1)S(1)} %get-tuple-element.47.v_ref, ...), custom_call_target="tpu_custom_call" | custom-call | flops 167772160 | bytes 3805184 | tf_op jit(solution)/shard_map/pallas_call | solution.py:168
  57.0 1.1 %shard_map.91 = (bf16[2,128,512]{2,1,0:T(8,128)(2,1)}, bf16[2,128,512]{2,1,0:T(8,128)(2,1)}) custom-call(s32[1]{0:T(128)} %bitcast.place_ref, bf16[2,128,512]{2,1,0:T(8,128)(2,1)S(1)} %get-tuple-element.46.k_ref, bf16[2,128,512]{2,1,0:T(8,128)(2,1)S(1)} %get-tuple-element.47.v_ref, f32[2,128,512]{2,1,0:T(8,128)S(1)} %get-tuple-element.66.gkl_ref, ...), custom_call_target="tpu_custom_call" | custom-call | flops 67108864 | bytes 2621444 | tf_op jit(solution)/shard_map/pallas_call | solution.py:168
  (28 shorter events, 6.6 us)
Async XLA Ops:
  2.0 7.0 %collective-permute-start = (f32[2,128,128]{2,1,0:T(8,128)S(1)}, f32[2,128,128]{2,1,0:T(8,128)S(1)}, u32[]{:S(2)}, u32[]{:S(2)}) collective-permute-start(f32[2,128,128]{2,1,0:T(8,128)S(1)} %get-tuple-element.51), channel_id=1, source_target_pairs={{0,8},{4,12},{8,0},{12,4},{16,24},{20,28},{24,16},{28,20},{1,9},{5... | collective-permute-start | bytes 393224 | tf_op jit(solution)/shard_map/ppermute | solution.py:187
  5.1 7.8 %collective-permute-start.1 = (f32[2,128,128]{2,1,0:T(8,128)S(1)}, f32[2,128,128]{2,1,0:T(8,128)S(1)}, u32[]{:S(2)}, u32[]{:S(2)}) collective-permute-start(f32[2,128,128]{2,1,0:T(8,128)S(1)} %get-tuple-element.52), channel_id=1, source_target_pairs={{0,4},{4,0},{8,12},{12,8},{16,20},{20,16},{24,28},{28,24},{1,5},{5... | collective-permute-start | bytes 393224 | tf_op jit(solution)/shard_map/ppermute | solution.py:187
  6.6 6.3 %collective-permute-start.2 = (f32[2,128,128]{2,1,0:T(8,128)S(1)}, f32[2,128,128]{2,1,0:T(8,128)S(1)}, u32[]{:S(2)}, u32[]{:S(2)}) collective-permute-start(f32[2,128,128]{2,1,0:T(8,128)S(1)} %get-tuple-element.53), channel_id=1, source_target_pairs={{0,12},{4,8},{8,4},{12,0},{16,28},{20,24},{24,20},{28,16},{1,13},{... | collective-permute-start | bytes 393224 | tf_op jit(solution)/shard_map/ppermute | solution.py:187
  12.9 7.6 %collective-permute-start.3 = (f32[2,128,128]{2,1,0:T(8,128)S(1)}, f32[2,128,128]{2,1,0:T(8,128)S(1)}, u32[]{:S(2)}, u32[]{:S(2)}) collective-permute-start(f32[2,128,128]{2,1,0:T(8,128)S(1)} %add_add_fusion.1), channel_id=1, source_target_pairs={{0,16},{4,20},{8,24},{12,28},{16,0},{20,4},{24,8},{28,12},{1,17},{... | collective-permute-start | bytes 393224 | tf_op jit(solution)/shard_map/ppermute | solution.py:191
  20.5 3.7 %copy-start = (bf16[2,128,512]{2,1,0:T(8,128)(2,1)S(1)}, bf16[2,128,512]{2,1,0:T(8,128)(2,1)}, u32[]{:S(2)}) copy-start(bf16[2,128,512]{2,1,0:T(8,128)(2,1)} %q_ref.3) | copy-start | bytes 786436
  20.6 6.0 %collective-permute-start.4 = (f32[2,128,128]{2,1,0:T(8,128)S(1)}, f32[2,128,128]{2,1,0:T(8,128)S(1)}, u32[]{:S(2)}, u32[]{:S(2)}) collective-permute-start(f32[2,128,128]{2,1,0:T(8,128)S(1)} %get-tuple-element.55), channel_id=1, source_target_pairs={{0,12},{4,8},{8,4},{12,0},{16,28},{20,24},{24,20},{28,16},{1,13},{... | collective-permute-start | bytes 393224 | tf_op jit(solution)/shard_map/ppermute | solution.py:187
  21.4 6.4 %collective-permute-start.5 = (f32[2,128,128]{2,1,0:T(8,128)S(1)}, f32[2,128,128]{2,1,0:T(8,128)S(1)}, u32[]{:S(2)}, u32[]{:S(2)}) collective-permute-start(f32[2,128,128]{2,1,0:T(8,128)S(1)} %get-tuple-element.56), channel_id=1, source_target_pairs={{0,4},{4,0},{8,12},{12,8},{16,20},{20,16},{24,28},{28,24},{1,5},{5... | collective-permute-start | bytes 393224 | tf_op jit(solution)/shard_map/ppermute | solution.py:187
  22.8 5.3 %collective-permute-start.6 = (f32[2,128,128]{2,1,0:T(8,128)S(1)}, f32[2,128,128]{2,1,0:T(8,128)S(1)}, u32[]{:S(2)}, u32[]{:S(2)}) collective-permute-start(f32[2,128,128]{2,1,0:T(8,128)S(1)} %get-tuple-element.57), channel_id=1, source_target_pairs={{0,8},{4,12},{8,0},{12,4},{16,24},{20,28},{24,16},{28,20},{1,9},{5... | collective-permute-start | bytes 393224 | tf_op jit(solution)/shard_map/ppermute | solution.py:187
  24.2 3.9 %copy-start.1 = (bf16[2,128,512]{2,1,0:T(8,128)(2,1)S(1)}, bf16[2,128,512]{2,1,0:T(8,128)(2,1)}, u32[]{:S(2)}) copy-start(bf16[2,128,512]{2,1,0:T(8,128)(2,1)} %g_ref.1) | copy-start | bytes 786436
  24.2 3.9 %copy-start.2 = (f32[2,512]{1,0:T(2,128)S(1)}, f32[2,512]{1,0:T(2,128)}, u32[]{:S(2)}) copy-start(f32[2,512]{1,0:T(2,128)} %gain_ref.5) | copy-start | bytes 12292
  28.5 1.8 %collective-permute-start.7 = (f32[8,128]{1,0:T(8,128)S(1)}, f32[8,128]{1,0:T(8,128)S(1)}, u32[]{:S(2)}, u32[]{:S(2)}) collective-permute-start(f32[8,128]{1,0:T(8,128)S(1)} %get-tuple-element.59.rest_0_), channel_id=1, source_target_pairs={{0,3},{1,0},{2,1},{3,2},{4,7},{5,4},{6,5},{7,6},{8,11},{9,8},{10,9... | collective-permute-start | bytes 12296 | tf_op jit(solution)/shard_map/ppermute | solution.py:262
  28.6 3.7 %collective-permute-start.8 = (f32[8,128]{1,0:T(8,128)S(1)}, f32[8,128]{1,0:T(8,128)S(1)}, u32[]{:S(2)}, u32[]{:S(2)}) collective-permute-start(f32[8,128]{1,0:T(8,128)S(1)} %get-tuple-element.59.rest_0_), channel_id=1, source_target_pairs={{0,2},{1,3},{2,0},{3,1},{4,6},{5,7},{6,4},{7,5},{8,10},{9,11},{10,... | collective-permute-start | bytes 12296 | tf_op jit(solution)/shard_map/ppermute | solution.py:262
  30.2 3.0 %collective-permute-start.9 = (f32[8,128]{1,0:T(8,128)S(1)}, f32[8,128]{1,0:T(8,128)S(1)}, u32[]{:S(2)}, u32[]{:S(2)}) collective-permute-start(f32[8,128]{1,0:T(8,128)S(1)} %get-tuple-element.59.rest_0_), channel_id=1, source_target_pairs={{0,1},{1,2},{2,3},{3,0},{4,5},{5,6},{6,7},{7,4},{8,9},{9,10},{10,1... | collective-permute-start | bytes 12296 | tf_op jit(solution)/shard_map/ppermute | solution.py:262
  33.8 5.5 %collective-permute-start.10 = (f32[2,128,128]{2,1,0:T(8,128)S(1)}, f32[2,128,128]{2,1,0:T(8,128)S(1)}, u32[]{:S(2)}, u32[]{:S(2)}) collective-permute-start(f32[2,128,128]{2,1,0:T(8,128)S(1)} %get-tuple-element.69), channel_id=1, source_target_pairs={{0,4},{4,0},{8,12},{12,8},{16,20},{20,16},{24,28},{28,24},{1,5},{5... | collective-permute-start | bytes 393224 | tf_op jit(solution)/shard_map/ppermute | solution.py:187
  34.9 5.9 %collective-permute-start.11 = (f32[2,128,128]{2,1,0:T(8,128)S(1)}, f32[2,128,128]{2,1,0:T(8,128)S(1)}, u32[]{:S(2)}, u32[]{:S(2)}) collective-permute-start(f32[2,128,128]{2,1,0:T(8,128)S(1)} %get-tuple-element.70), channel_id=1, source_target_pairs={{0,12},{4,8},{8,4},{12,0},{16,28},{20,24},{24,20},{28,16},{1,13},{... | collective-permute-start | bytes 393224 | tf_op jit(solution)/shard_map/ppermute | solution.py:187
  36.4 5.3 %collective-permute-start.12 = (f32[2,128,128]{2,1,0:T(8,128)S(1)}, f32[2,128,128]{2,1,0:T(8,128)S(1)}, u32[]{:S(2)}, u32[]{:S(2)}) collective-permute-start(f32[2,128,128]{2,1,0:T(8,128)S(1)} %get-tuple-element.71), channel_id=1, source_target_pairs={{0,8},{4,12},{8,0},{12,4},{16,24},{20,28},{24,16},{28,20},{1,9},{5... | collective-permute-start | bytes 393224 | tf_op jit(solution)/shard_map/ppermute | solution.py:187
  41.7 8.0 %collective-permute-start.13 = (f32[2,128,128]{2,1,0:T(8,128)S(1)}, f32[2,128,128]{2,1,0:T(8,128)S(1)}, u32[]{:S(2)}, u32[]{:S(2)}) collective-permute-start(f32[2,128,128]{2,1,0:T(8,128)S(1)} %add_add_fusion), channel_id=1, source_target_pairs={{0,16},{4,20},{8,24},{12,28},{16,0},{20,4},{24,8},{28,12},{1,17},{... | collective-permute-start | bytes 393224 | tf_op jit(solution)/shard_map/ppermute | solution.py:191
  49.8 6.2 %collective-permute-start.14 = (f32[2,128,128]{2,1,0:T(8,128)S(1)}, f32[2,128,128]{2,1,0:T(8,128)S(1)}, u32[]{:S(2)}, u32[]{:S(2)}) collective-permute-start(f32[2,128,128]{2,1,0:T(8,128)S(1)} %get-tuple-element.73), channel_id=1, source_target_pairs={{0,12},{4,8},{8,4},{12,0},{16,28},{20,24},{24,20},{28,16},{1,13},{... | collective-permute-start | bytes 393224 | tf_op jit(solution)/shard_map/ppermute | solution.py:187
  50.6 6.4 %collective-permute-start.15 = (f32[2,128,128]{2,1,0:T(8,128)S(1)}, f32[2,128,128]{2,1,0:T(8,128)S(1)}, u32[]{:S(2)}, u32[]{:S(2)}) collective-permute-start(f32[2,128,128]{2,1,0:T(8,128)S(1)} %get-tuple-element.74), channel_id=1, source_target_pairs={{0,4},{4,0},{8,12},{12,8},{16,20},{20,16},{24,28},{28,24},{1,5},{5... | collective-permute-start | bytes 393224 | tf_op jit(solution)/shard_map/ppermute | solution.py:187
  51.0 6.0 %collective-permute-start.16 = (f32[2,128,128]{2,1,0:T(8,128)S(1)}, f32[2,128,128]{2,1,0:T(8,128)S(1)}, u32[]{:S(2)}, u32[]{:S(2)}) collective-permute-start(f32[2,128,128]{2,1,0:T(8,128)S(1)} %get-tuple-element.75), channel_id=1, source_target_pairs={{0,8},{4,12},{8,0},{12,4},{16,24},{20,28},{24,16},{28,20},{1,9},{5... | collective-permute-start | bytes 393224 | tf_op jit(solution)/shard_map/ppermute | solution.py:187

commit v5 on v4

--- a/solution.py
+++ b/solution.py
@@ -10,6 +10,7 @@
 DH = 128
 CH = 128
 GROUP = 4
+EARLY = 2
 ORDERS = ((2, 1, 3), (3, 1, 2), (1, 3, 2), (3, 1, 2))
 
 EPSILON = 1e-06
@@ -32,34 +33,56 @@
     return rows >= cols
 
 
-def kv_kernel(order, place_ref, k_hbm, v_hbm, k_ref, v_ref, *rest):
-    outs, sems = rest[:GROUP], rest[GROUP]
+def local_part(early, q_ref, k_ref, v_ref, w_ref, loc_ref):
+    mask = causal_mask()
+    layers, _, width = q_ref.shape
+    every = [(layer, head) for layer in range(layers) for head in range(width // DH)]
+    for layer, head in every[:EARLY] if early else every[EARLY:]:
+        at = pl.ds(head * DH, DH)
+        scores = dot(q_ref[layer, :, at], k_ref[layer, :, at], 1, 1) * SCALE
+        w = jnp.where(mask, scores, 0.0).astype(BF16)
+        w_ref[layer, :, at] = w
+        loc_ref[layer, :, at] = dot(w, v_ref[layer, :, at], 1, 0)
+
+
+def held_back():
+    return lax.rem(lax.axis_index("head"), 2) == 0
+
+
+def kv_kernel(order, place_ref, *refs):
+    sources, (q_ref, k_ref, v_ref) = refs[:3], refs[3:6]
+    w_ref, loc_ref = refs[6:8]
+    outs, sems = refs[8:-1], refs[-1]
     loads = [
-        pltpu.make_async_copy(src.at[layer], dst.at[layer], sems.at[i, layer])
-        for layer in range(k_ref.shape[0])
-        for i, (src, dst) in enumerate(((k_hbm, k_ref), (v_hbm, v_ref)))
+        [
+            pltpu.make_async_copy(src.at[layer], dst.at[layer], sems.at[i, layer])
+            for layer in range(k_ref.shape[0])
+        ]
+        for i, (src, dst) in enumerate(zip(sources, (q_ref, k_ref, v_ref)))
     ]
-    for load in loads:
+    for load in loads[1] + loads[2] + loads[0]:
         load.start()
-    for load in loads:
+    for load in loads[1] + loads[2]:
         load.wait()
     place = place_ref[0]
     for turn, out in zip((0, *order), outs):
         at = lanes(lax.bitwise_xor(place, turn))
         for layer in range(k_ref.shape[0]):
             out[layer] = dot(k_ref[layer, :, at], v_ref[layer, :, at], 0, 0)
-
-
-def local_kernel(q_ref, k_ref, v_ref, w_ref, loc_ref):
-    mask = causal_mask()
-    layers, _, width = q_ref.shape
-    for layer in range(layers):
-        for head in range(width // DH):
-            at = pl.ds(head * DH, DH)
-            scores = dot(q_ref[layer, :, at], k_ref[layer, :, at], 1, 1) * SCALE
-            w = jnp.where(mask, scores, 0.0).astype(BF16)
-            w_ref[layer, :, at] = w
-            loc_ref[layer, :, at] = dot(w, v_ref[layer, :, at], 1, 0)
+    for load in loads[0]:
+        load.wait()
+
+    @pl.when(held_back())
+    def _():
+        local_part(True, q_ref, k_ref, v_ref, w_ref, loc_ref)
+
+
+def local_kernel(q_ref, k_ref, v_ref, w_in, loc_in, w_ref, loc_ref):
+    local_part(False, q_ref, k_ref, v_ref, w_ref, loc_ref)
+
+    @pl.when(jnp.logical_not(held_back()))
+    def _():
+        local_part(True, q_ref, k_ref, v_ref, w_ref, loc_ref)
 
 
 def spread_kernel(reverse, order, order_back, place_ref, outside_ref, *refs):
@@ -161,7 +184,7 @@
         store.wait()
 
 
-def call(body, outs, smem, flops, *args, hbm=(), held=(), scratch=(), manual=False):
+def call(body, outs, smem, flops, *args, hbm=(), held=(), scratch=(), manual=False, alias={}):
     moved = sum(a.size * a.dtype.itemsize for a in [*args, *held, *outs])
     inputs = [pltpu.with_memory_space_constraint(a, pltpu.VMEM) for a in args[smem:]]
     spec = lambda space: pl.BlockSpec(memory_space=space)
@@ -177,6 +200,7 @@
             spec(pltpu.HBM if manual and i in hbm else pltpu.VMEM) for i in range(len(outs))
         ],
         scratch_shapes=scratch,
+        input_output_aliases=alias,
         compiler_params=pltpu.CompilerParams(vmem_limit_bytes=4 * 2**20),
         cost_estimate=pl.CostEstimate(flops=flops, bytes_accessed=moved, transcendentals=0),
     )(*args[:smem], *inputs, *[pltpu.with_memory_space_constraint(a, pltpu.HBM) for a in held])
@@ -224,23 +248,32 @@
     blocks = [jax.ShapeDtypeStruct((layers, DH, DH), F32)] * GROUP
     product = 2 * layers * heads * CH * DH * DH
 
-    keys, values, *kv = call(
+    queries, keys, values, weights, local, *kv = call(
         functools.partial(kv_kernel, ORDERS[0]),
-        [wide(BF16), wide(BF16), *blocks],
-        1,
-        product,
+        [wide(BF16)] * 4 + [wide(F32), *blocks],
+        1,
+        3 * product,
         place_arg,
-        held=(keys, values),
-        scratch=[pltpu.SemaphoreType.DMA((2, layers))],
-    )
-    queries, out_grad, kv = lax.optimization_barrier((queries, out_grad, kv))
+        held=(queries, keys, values),
+        scratch=[pltpu.SemaphoreType.DMA((3, layers))],
+    )
+    out_grad, kv = lax.optimization_barrier((out_grad, kv))
     states, (weights, local) = carried(
         kv,
         place,
         seq_count,
         False,
         lambda: call(
-            local_kernel, [wide(BF16), wide(F32)], 0, 2 * product, queries, keys, values
+            local_kernel,
+            [wide(BF16), wide(F32)],
+            0,
+            2 * product,
+            queries,
+            keys,
+            values,
+            weights,
+            local,
+            alias={3: 0, 4: 1},
         ),
         ORDERS[0],
         ORDERS[1],
@@ -298,7 +331,7 @@
         ORDERS[2],
         ORDERS[3],
     )
-    tile = pltpu.VMEM(queries.shape, BF16)
+    tile = pltpu.VMEM((layers, CH, width), BF16)
     grad_k, grad_v = call(
         functools.partial(outer_kernel, ORDERS[3]),
         [wide(BF16), wide(BF16)],

time: 58.2 us -> 57.2 us (0.983)
  starting transfers between devices: 23.6 us -> 22.9 us
    ppermute x2, starting transfers between devices: 6.5 us -> 5.85 us  [shift(): lax.ppermute(array, 'seq', [(i, (i + step) % count) for i in range(count)])]
  transfers between devices with their start and end apart: 17 -> 17, of which waited for: 13 -> 13; matrix products, arithmetic and copies ran while one was open for 0% -> 0% of each run, Pallas kernels for 7% -> 6%
where the time goes in v5:
time: 57.2 us; the launch traced here: 57.1 us
  waiting for transfers between devices  25.6 us (45%)
  starting transfers between devices  22.9 us (40%)
  Pallas kernels  7.79 us (14%)
  between operations  0.7 us (1%)
    ppermute x12, starting transfers between devices, swap(): return lax.ppermute(array, 'seq', [(i, i ^ turn) for i in range(count)])  15.3 us
    ppermute x12, waiting for transfers between devices, swap(): return lax.ppermute(array, 'seq', [(i, i ^ turn) for i in range(count)])  13.5 us
    ppermute x2, waiting for transfers between devices, shift(): lax.ppermute(array, 'seq', [(i, (i + step) % count) for i in range(count)])  9.2 us
    pallas_call x8, Pallas kernels, call(): pl.pallas_call(body, out_shape=[a if i in hbm else pltpu.VMEM(a.shape, a....  7.79 us
    ppermute x2, starting transfers between devices, shift(): lax.ppermute(array, 'seq', [(i, (i + step) % count) for i in range(count)])  5.85 us
    ppermute x3, waiting for transfers between devices, across(): return lax.ppermute(array, 'head', pairs)  2.87 us
    ppermute x3, starting transfers between devices, across(): return lax.ppermute(array, 'head', pairs)  1.78 us
  transfers between devices with their start and end apart: 17, of which 13 were waited for; matrix products, arithmetic and copies ran while one was open for 0% of the time, Pallas kernels for 6%

profile of v5, /device:TPU:0, one launch (start us, length us, event | category | flops | bytes accessed | tf_op | source)
XLA Modules:
  0.0 57.1 jit_solution(2555887321182473959)
XLA Ops:
  0.6 1.8 %shard_map.84 = (bf16[2,128,512]{2,1,0:T(8,128)(2,1)S(1)}, bf16[2,128,512]{2,1,0:T(8,128)(2,1)S(1)}, bf16[2,128,512]{2,1,0:T(8,128)(2,1)S(1)}, bf16[2,128,512]{2...) custom-call(s32[1]{0:T(128)} %bitcast.place_ref, ...), custom_call_target="tpu_custom_call" | custom-call | flops 100663296 | bytes 2883588 | tf_op jit(solution)/shard_map/pallas_call | solution.py:191
  2.5 3.1 %collective-permute-start = (f32[2,128,128]{2,1,0:T(8,128)S(1)}, f32[2,128,128]{2,1,0:T(8,128)S(1)}, u32[]{:S(2)}, u32[]{:S(2)}) collective-permute-start(f32[2,128,128]{2,1,0:T(8,128)S(1)} %get-tuple-element.55), channel_id=1, source_target_pairs={{0,8},{4,12},{8,0},{12,4},{16,24},{20,28},{24,16},{28,20},{1,9},{5... | collective-permute-start | bytes 393224 | tf_op jit(solution)/shard_map/ppermute | solution.py:211
  5.6 1.5 %collective-permute-start.1 = (f32[2,128,128]{2,1,0:T(8,128)S(1)}, f32[2,128,128]{2,1,0:T(8,128)S(1)}, u32[]{:S(2)}, u32[]{:S(2)}) collective-permute-start(f32[2,128,128]{2,1,0:T(8,128)S(1)} %get-tuple-element.56), channel_id=1, source_target_pairs={{0,4},{4,0},{8,12},{12,8},{16,20},{20,16},{24,28},{28,24},{1,5},{5... | collective-permute-start | bytes 393224 | tf_op jit(solution)/shard_map/ppermute | solution.py:211
  7.1 2.2 %collective-permute-done.refs_1_ = f32[2,128,128]{2,1,0:T(8,128)S(1)} collective-permute-done((f32[2,128,128]{2,1,0:T(8,128)S(1)}, f32[2,128,128]{2,1,0:T(8,128)S(1)}, u32[]{:S(2)}, u32[]{:S(2)}) %collective-permute-start) | collective-permute-done | bytes 131104 | tf_op jit(solution)/shard_map/ppermute | solution.py:211
  9.3 4.0 %collective-permute-done.1.refs_2_ = f32[2,128,128]{2,1,0:T(8,128)S(1)} collective-permute-done((f32[2,128,128]{2,1,0:T(8,128)S(1)}, f32[2,128,128]{2,1,0:T(8,128)S(1)}, u32[]{:S(2)}, u32[]{:S(2)}) %collective-permute-start.1) | collective-permute-done | bytes 131104 | tf_op jit(solution)/shard_map/ppermute | solution.py:211
  13.4 2.7 %collective-permute-start.3 = (f32[2,128,128]{2,1,0:T(8,128)S(1)}, f32[2,128,128]{2,1,0:T(8,128)S(1)}, u32[]{:S(2)}, u32[]{:S(2)}) collective-permute-start(f32[2,128,128]{2,1,0:T(8,128)S(1)} %add_add_fusion.1), channel_id=1, source_target_pairs={{0,16},{4,20},{8,24},{12,28},{16,0},{20,4},{24,8},{28,12},{1,17},{... | collective-permute-start | bytes 393224 | tf_op jit(solution)/shard_map/ppermute | solution.py:215
  16.1 4.7 %collective-permute-done.3 = f32[2,128,128]{2,1,0:T(8,128)S(1)} collective-permute-done((f32[2,128,128]{2,1,0:T(8,128)S(1)}, f32[2,128,128]{2,1,0:T(8,128)S(1)}, u32[]{:S(2)}, u32[]{:S(2)}) %collective-permute-start.3) | collective-permute-done | bytes 131104 | tf_op jit(solution)/shard_map/ppermute | solution.py:215
  21.1 1.3 %collective-permute-start.5 = (f32[2,128,128]{2,1,0:T(8,128)S(1)}, f32[2,128,128]{2,1,0:T(8,128)S(1)}, u32[]{:S(2)}, u32[]{:S(2)}) collective-permute-start(f32[2,128,128]{2,1,0:T(8,128)S(1)} %get-tuple-element.60), channel_id=1, source_target_pairs={{0,4},{4,0},{8,12},{12,8},{16,20},{20,16},{24,28},{28,24},{1,5},{5... | collective-permute-start | bytes 393224 | tf_op jit(solution)/shard_map/ppermute | solution.py:211
  22.4 2.1 %collective-permute-start.6 = (f32[2,128,128]{2,1,0:T(8,128)S(1)}, f32[2,128,128]{2,1,0:T(8,128)S(1)}, u32[]{:S(2)}, u32[]{:S(2)}) collective-permute-start(f32[2,128,128]{2,1,0:T(8,128)S(1)} %get-tuple-element.61), channel_id=1, source_target_pairs={{0,8},{4,12},{8,0},{12,4},{16,24},{20,28},{24,16},{28,20},{1,9},{5... | collective-permute-start | bytes 393224 | tf_op jit(solution)/shard_map/ppermute | solution.py:211
  24.5 1.1 %shard_map.85 = (bf16[2,128,512]{2,1,0:T(8,128)(2,1)S(1)}, f32[2,128,512]{2,1,0:T(8,128)S(1)}) custom-call(bf16[2,128,512]{2,1,0:T(8,128)(2,1)S(1)} %get-tuple-element.43.q_ref, bf16[2,128,512]{2,1,0:T(8,128)(2,1)S(1)} %get-tuple-element.44.k_ref, bf16[2,128,512]{2,1,0:T(8,128)(2,1)S(1)} %get-tuple-element.45.v_ref, ...), custom_call_target="tpu_custom_call", output_to_operand_aliasing={{0}: (3, {}), {1}: (4, {})} | custom-call | flops 67108864 | bytes 2359296 | tf_op jit(solution)/shard_map/pallas_call | solution.py:191
  25.5 1.4 %collective-permute-done.4.rest_1_ = f32[2,128,128]{2,1,0:T(8,128)S(1)} collective-permute-done((f32[2,128,128]{2,1,0:T(8,128)S(1)}, f32[2,128,128]{2,1,0:T(8,128)S(1)}, u32[]{:S(2)}, u32[]{:S(2)}) %collective-permute-start.4) | collective-permute-done | bytes 131104 | tf_op jit(solution)/shard_map/ppermute | solution.py:211
  28.2 1.6 %collective-permute-start.8 = (f32[8,128]{1,0:T(8,128)S(1)}, f32[8,128]{1,0:T(8,128)S(1)}, u32[]{:S(2)}, u32[]{:S(2)}) collective-permute-start(f32[8,128]{1,0:T(8,128)S(1)} %get-tuple-element.63.rest_0_), channel_id=1, source_target_pairs={{0,2},{1,3},{2,0},{3,1},{4,6},{5,7},{6,4},{7,5},{8,10},{9,11},{10,... | collective-permute-start | bytes 12296 | tf_op jit(solution)/shard_map/ppermute | solution.py:295
  29.9 1.9 %collective-permute-done.8.rest_2_ = f32[8,128]{1,0:T(8,128)S(1)} collective-permute-done((f32[8,128]{1,0:T(8,128)S(1)}, f32[8,128]{1,0:T(8,128)S(1)}, u32[]{:S(2)}, u32[]{:S(2)}) %collective-permute-start.8) | collective-permute-done | bytes 4128 | tf_op jit(solution)/shard_map/ppermute | solution.py:295
  33.4 1.2 %collective-permute-start.10 = (f32[2,128,128]{2,1,0:T(8,128)S(1)}, f32[2,128,128]{2,1,0:T(8,128)S(1)}, u32[]{:S(2)}, u32[]{:S(2)}) collective-permute-start(f32[2,128,128]{2,1,0:T(8,128)S(1)} %get-tuple-element.73), channel_id=1, source_target_pairs={{0,4},{4,0},{8,12},{12,8},{16,20},{20,16},{24,28},{28,24},{1,5},{5... | collective-permute-start | bytes 393224 | tf_op jit(solution)/shard_map/ppermute | solution.py:211
  34.6 2.0 %collective-permute-start.11 = (f32[2,128,128]{2,1,0:T(8,128)S(1)}, f32[2,128,128]{2,1,0:T(8,128)S(1)}, u32[]{:S(2)}, u32[]{:S(2)}) collective-permute-start(f32[2,128,128]{2,1,0:T(8,128)S(1)} %get-tuple-element.74), channel_id=1, source_target_pairs={{0,12},{4,8},{8,4},{12,0},{16,28},{20,24},{24,20},{28,16},{1,13},{... | collective-permute-start | bytes 393224 | tf_op jit(solution)/shard_map/ppermute | solution.py:211
  36.9 2.0 %collective-permute-done.10.refs_1_ = f32[2,128,128]{2,1,0:T(8,128)S(1)} collective-permute-done((f32[2,128,128]{2,1,0:T(8,128)S(1)}, f32[2,128,128]{2,1,0:T(8,128)S(1)}, u32[]{:S(2)}, u32[]{:S(2)}) %collective-permute-start.10) | collective-permute-done | bytes 131104 | tf_op jit(solution)/shard_map/ppermute | solution.py:211
  38.9 1.5 %collective-permute-done.11.refs_2_ = f32[2,128,128]{2,1,0:T(8,128)S(1)} collective-permute-done((f32[2,128,128]{2,1,0:T(8,128)S(1)}, f32[2,128,128]{2,1,0:T(8,128)S(1)}, u32[]{:S(2)}, u32[]{:S(2)}) %collective-permute-start.11) | collective-permute-done | bytes 131104 | tf_op jit(solution)/shard_map/ppermute | solution.py:211
  40.4 1.1 %collective-permute-done.12.refs_3_ = f32[2,128,128]{2,1,0:T(8,128)S(1)} collective-permute-done((f32[2,128,128]{2,1,0:T(8,128)S(1)}, f32[2,128,128]{2,1,0:T(8,128)S(1)}, u32[]{:S(2)}, u32[]{:S(2)}) %collective-permute-start.12) | collective-permute-done | bytes 131104 | tf_op jit(solution)/shard_map/ppermute | solution.py:211
  41.6 3.2 %collective-permute-start.13 = (f32[2,128,128]{2,1,0:T(8,128)S(1)}, f32[2,128,128]{2,1,0:T(8,128)S(1)}, u32[]{:S(2)}, u32[]{:S(2)}) collective-permute-start(f32[2,128,128]{2,1,0:T(8,128)S(1)} %add_add_fusion), channel_id=1, source_target_pairs={{0,16},{4,20},{8,24},{12,28},{16,0},{20,4},{24,8},{28,12},{1,17},{... | collective-permute-start | bytes 393224 | tf_op jit(solution)/shard_map/ppermute | solution.py:215
  44.8 4.5 %collective-permute-done.13 = f32[2,128,128]{2,1,0:T(8,128)S(1)} collective-permute-done((f32[2,128,128]{2,1,0:T(8,128)S(1)}, f32[2,128,128]{2,1,0:T(8,128)S(1)}, u32[]{:S(2)}, u32[]{:S(2)}) %collective-permute-start.13) | collective-permute-done | bytes 131104 | tf_op jit(solution)/shard_map/ppermute | solution.py:215
  49.6 1.1 %collective-permute-start.15 = (f32[2,128,128]{2,1,0:T(8,128)S(1)}, f32[2,128,128]{2,1,0:T(8,128)S(1)}, u32[]{:S(2)}, u32[]{:S(2)}) collective-permute-start(f32[2,128,128]{2,1,0:T(8,128)S(1)} %get-tuple-element.78), channel_id=1, source_target_pairs={{0,4},{4,0},{8,12},{12,8},{16,20},{20,16},{24,28},{28,24},{1,5},{5... | collective-permute-start | bytes 393224 | tf_op jit(solution)/shard_map/ppermute | solution.py:211
  50.7 2.2 %collective-permute-start.16 = (f32[2,128,128]{2,1,0:T(8,128)S(1)}, f32[2,128,128]{2,1,0:T(8,128)S(1)}, u32[]{:S(2)}, u32[]{:S(2)}) collective-permute-start(f32[2,128,128]{2,1,0:T(8,128)S(1)} %get-tuple-element.79), channel_id=1, source_target_pairs={{0,8},{4,12},{8,0},{12,4},{16,24},{20,28},{24,16},{28,20},{1,9},{5... | collective-permute-start | bytes 393224 | tf_op jit(solution)/shard_map/ppermute | solution.py:211
  52.9 2.6 %shard_map.89 = (bf16[2,128,512]{2,1,0:T(8,128)(2,1)}, bf16[2,128,512]{2,1,0:T(8,128)(2,1)}, f32[2,128,512]{2,1,0:T(8,128)S(1)}, f32[2,128,512]{2,1,0:T(8,128)S(1)}) custom-call(bf16[2,128,512]{2,1,0:T(8,128)(2,1)S(1)} %get-tuple-element.43.q_ref, bf16[2,128,512]{2,1,0:T(8,128)(2,1)S(1)} %get-tuple-element.44.k_ref, ...), custom_call_target="tpu_custom_call" | custom-call | flops 167772160 | bytes 3805184 | tf_op jit(solution)/shard_map/pallas_call | solution.py:191
  56.0 1.1 %shard_map.91 = (bf16[2,128,512]{2,1,0:T(8,128)(2,1)}, bf16[2,128,512]{2,1,0:T(8,128)(2,1)}) custom-call(s32[1]{0:T(128)} %bitcast.place_ref, bf16[2,128,512]{2,1,0:T(8,128)(2,1)S(1)} %get-tuple-element.44.k_ref, bf16[2,128,512]{2,1,0:T(8,128)(2,1)S(1)} %get-tuple-element.45.v_ref, f32[2,128,512]{2,1,0:T(8,128)S(1)} %get-tuple-element.70.gkl_ref, ...), custom_call_target="tpu_custom_call" | custom-call | flops 67108864 | bytes 2621444 | tf_op jit(solution)/shard_map/pallas_call | solution.py:191
  (26 shorter events, 4.3 us)
Async XLA Ops:
  2.5 6.8 %collective-permute-start = (f32[2,128,128]{2,1,0:T(8,128)S(1)}, f32[2,128,128]{2,1,0:T(8,128)S(1)}, u32[]{:S(2)}, u32[]{:S(2)}) collective-permute-start(f32[2,128,128]{2,1,0:T(8,128)S(1)} %get-tuple-element.55), channel_id=1, source_target_pairs={{0,8},{4,12},{8,0},{12,4},{16,24},{20,28},{24,16},{28,20},{1,9},{5... | collective-permute-start | bytes 393224 | tf_op jit(solution)/shard_map/ppermute | solution.py:211
  5.6 7.8 %collective-permute-start.1 = (f32[2,128,128]{2,1,0:T(8,128)S(1)}, f32[2,128,128]{2,1,0:T(8,128)S(1)}, u32[]{:S(2)}, u32[]{:S(2)}) collective-permute-start(f32[2,128,128]{2,1,0:T(8,128)S(1)} %get-tuple-element.56), channel_id=1, source_target_pairs={{0,4},{4,0},{8,12},{12,8},{16,20},{20,16},{24,28},{28,24},{1,5},{5... | collective-permute-start | bytes 393224 | tf_op jit(solution)/shard_map/ppermute | solution.py:211
  7.1 6.3 %collective-permute-start.2 = (f32[2,128,128]{2,1,0:T(8,128)S(1)}, f32[2,128,128]{2,1,0:T(8,128)S(1)}, u32[]{:S(2)}, u32[]{:S(2)}) collective-permute-start(f32[2,128,128]{2,1,0:T(8,128)S(1)} %get-tuple-element.57), channel_id=1, source_target_pairs={{0,12},{4,8},{8,4},{12,0},{16,28},{20,24},{24,20},{28,16},{1,13},{... | collective-permute-start | bytes 393224 | tf_op jit(solution)/shard_map/ppermute | solution.py:211
  13.4 7.4 %collective-permute-start.3 = (f32[2,128,128]{2,1,0:T(8,128)S(1)}, f32[2,128,128]{2,1,0:T(8,128)S(1)}, u32[]{:S(2)}, u32[]{:S(2)}) collective-permute-start(f32[2,128,128]{2,1,0:T(8,128)S(1)} %add_add_fusion.1), channel_id=1, source_target_pairs={{0,16},{4,20},{8,24},{12,28},{16,0},{20,4},{24,8},{28,12},{1,17},{... | collective-permute-start | bytes 393224 | tf_op jit(solution)/shard_map/ppermute | solution.py:215
  20.9 6.0 %collective-permute-start.4 = (f32[2,128,128]{2,1,0:T(8,128)S(1)}, f32[2,128,128]{2,1,0:T(8,128)S(1)}, u32[]{:S(2)}, u32[]{:S(2)}) collective-permute-start(f32[2,128,128]{2,1,0:T(8,128)S(1)} %get-tuple-element.59), channel_id=1, source_target_pairs={{0,12},{4,8},{8,4},{12,0},{16,28},{20,24},{24,20},{28,16},{1,13},{... | collective-permute-start | bytes 393224 | tf_op jit(solution)/shard_map/ppermute | solution.py:211
  21.1 6.4 %collective-permute-start.5 = (f32[2,128,128]{2,1,0:T(8,128)S(1)}, f32[2,128,128]{2,1,0:T(8,128)S(1)}, u32[]{:S(2)}, u32[]{:S(2)}) collective-permute-start(f32[2,128,128]{2,1,0:T(8,128)S(1)} %get-tuple-element.60), channel_id=1, source_target_pairs={{0,4},{4,0},{8,12},{12,8},{16,20},{20,16},{24,28},{28,24},{1,5},{5... | collective-permute-start | bytes 393224 | tf_op jit(solution)/shard_map/ppermute | solution.py:211
  22.4 5.3 %collective-permute-start.6 = (f32[2,128,128]{2,1,0:T(8,128)S(1)}, f32[2,128,128]{2,1,0:T(8,128)S(1)}, u32[]{:S(2)}, u32[]{:S(2)}) collective-permute-start(f32[2,128,128]{2,1,0:T(8,128)S(1)} %get-tuple-element.61), channel_id=1, source_target_pairs={{0,8},{4,12},{8,0},{12,4},{16,24},{20,28},{24,16},{28,20},{1,9},{5... | collective-permute-start | bytes 393224 | tf_op jit(solution)/shard_map/ppermute | solution.py:211
  24.5 3.2 %copy-start = (bf16[2,128,512]{2,1,0:T(8,128)(2,1)S(1)}, bf16[2,128,512]{2,1,0:T(8,128)(2,1)}, u32[]{:S(2)}) copy-start(bf16[2,128,512]{2,1,0:T(8,128)(2,1)} %g_ref.1) | copy-start | bytes 786436
  24.5 3.2 %copy-start.1 = (f32[2,512]{1,0:T(2,128)S(1)}, f32[2,512]{1,0:T(2,128)}, u32[]{:S(2)}) copy-start(f32[2,512]{1,0:T(2,128)} %gain_ref.5) | copy-start | bytes 12292
  28.1 1.8 %collective-permute-start.7 = (f32[8,128]{1,0:T(8,128)S(1)}, f32[8,128]{1,0:T(8,128)S(1)}, u32[]{:S(2)}, u32[]{:S(2)}) collective-permute-start(f32[8,128]{1,0:T(8,128)S(1)} %get-tuple-element.63.rest_0_), channel_id=1, source_target_pairs={{0,3},{1,0},{2,1},{3,2},{4,7},{5,4},{6,5},{7,6},{8,11},{9,8},{10,9... | collective-permute-start | bytes 12296 | tf_op jit(solution)/shard_map/ppermute | solution.py:295
  28.2 3.7 %collective-permute-start.8 = (f32[8,128]{1,0:T(8,128)S(1)}, f32[8,128]{1,0:T(8,128)S(1)}, u32[]{:S(2)}, u32[]{:S(2)}) collective-permute-start(f32[8,128]{1,0:T(8,128)S(1)} %get-tuple-element.63.rest_0_), channel_id=1, source_target_pairs={{0,2},{1,3},{2,0},{3,1},{4,6},{5,7},{6,4},{7,5},{8,10},{9,11},{10,... | collective-permute-start | bytes 12296 | tf_op jit(solution)/shard_map/ppermute | solution.py:295
  29.8 3.0 %collective-permute-start.9 = (f32[8,128]{1,0:T(8,128)S(1)}, f32[8,128]{1,0:T(8,128)S(1)}, u32[]{:S(2)}, u32[]{:S(2)}) collective-permute-start(f32[8,128]{1,0:T(8,128)S(1)} %get-tuple-element.63.rest_0_), channel_id=1, source_target_pairs={{0,1},{1,2},{2,3},{3,0},{4,5},{5,6},{6,7},{7,4},{8,9},{9,10},{10,1... | collective-permute-start | bytes 12296 | tf_op jit(solution)/shard_map/ppermute | solution.py:295
  33.4 5.6 %collective-permute-start.10 = (f32[2,128,128]{2,1,0:T(8,128)S(1)}, f32[2,128,128]{2,1,0:T(8,128)S(1)}, u32[]{:S(2)}, u32[]{:S(2)}) collective-permute-start(f32[2,128,128]{2,1,0:T(8,128)S(1)} %get-tuple-element.73), channel_id=1, source_target_pairs={{0,4},{4,0},{8,12},{12,8},{16,20},{20,16},{24,28},{28,24},{1,5},{5... | collective-permute-start | bytes 393224 | tf_op jit(solution)/shard_map/ppermute | solution.py:211
  34.6 5.9 %collective-permute-start.11 = (f32[2,128,128]{2,1,0:T(8,128)S(1)}, f32[2,128,128]{2,1,0:T(8,128)S(1)}, u32[]{:S(2)}, u32[]{:S(2)}) collective-permute-start(f32[2,128,128]{2,1,0:T(8,128)S(1)} %get-tuple-element.74), channel_id=1, source_target_pairs={{0,12},{4,8},{8,4},{12,0},{16,28},{20,24},{24,20},{28,16},{1,13},{... | collective-permute-start | bytes 393224 | tf_op jit(solution)/shard_map/ppermute | solution.py:211
  36.6 5.0 %collective-permute-start.12 = (f32[2,128,128]{2,1,0:T(8,128)S(1)}, f32[2,128,128]{2,1,0:T(8,128)S(1)}, u32[]{:S(2)}, u32[]{:S(2)}) collective-permute-start(f32[2,128,128]{2,1,0:T(8,128)S(1)} %get-tuple-element.75), channel_id=1, source_target_pairs={{0,8},{4,12},{8,0},{12,4},{16,24},{20,28},{24,16},{28,20},{1,9},{5... | collective-permute-start | bytes 393224 | tf_op jit(solution)/shard_map/ppermute | solution.py:211
  41.6 7.7 %collective-permute-start.13 = (f32[2,128,128]{2,1,0:T(8,128)S(1)}, f32[2,128,128]{2,1,0:T(8,128)S(1)}, u32[]{:S(2)}, u32[]{:S(2)}) collective-permute-start(f32[2,128,128]{2,1,0:T(8,128)S(1)} %add_add_fusion), channel_id=1, source_target_pairs={{0,16},{4,20},{8,24},{12,28},{16,0},{20,4},{24,8},{28,12},{1,17},{... | collective-permute-start | bytes 393224 | tf_op jit(solution)/shard_map/ppermute | solution.py:215
  49.4 6.2 %collective-permute-start.14 = (f32[2,128,128]{2,1,0:T(8,128)S(1)}, f32[2,128,128]{2,1,0:T(8,128)S(1)}, u32[]{:S(2)}, u32[]{:S(2)}) collective-permute-start(f32[2,128,128]{2,1,0:T(8,128)S(1)} %get-tuple-element.77), channel_id=1, source_target_pairs={{0,12},{4,8},{8,4},{12,0},{16,28},{20,24},{24,20},{28,16},{1,13},{... | collective-permute-start | bytes 393224 | tf_op jit(solution)/shard_map/ppermute | solution.py:211
  49.6 6.4 %collective-permute-start.15 = (f32[2,128,128]{2,1,0:T(8,128)S(1)}, f32[2,128,128]{2,1,0:T(8,128)S(1)}, u32[]{:S(2)}, u32[]{:S(2)}) collective-permute-start(f32[2,128,128]{2,1,0:T(8,128)S(1)} %get-tuple-element.78), channel_id=1, source_target_pairs={{0,4},{4,0},{8,12},{12,8},{16,20},{20,16},{24,28},{28,24},{1,5},{5... | collective-permute-start | bytes 393224 | tf_op jit(solution)/shard_map/ppermute | solution.py:211
  50.7 5.3 %collective-permute-start.16 = (f32[2,128,128]{2,1,0:T(8,128)S(1)}, f32[2,128,128]{2,1,0:T(8,128)S(1)}, u32[]{:S(2)}, u32[]{:S(2)}) collective-permute-start(f32[2,128,128]{2,1,0:T(8,128)S(1)} %get-tuple-element.79), channel_id=1, source_target_pairs={{0,8},{4,12},{8,0},{12,4},{16,24},{20,28},{24,16},{28,20},{1,9},{5... | collective-permute-start | bytes 393224 | tf_op jit(solution)/shard_map/ppermute | solution.py:211

commit v6 on v5

--- a/solution.py
+++ b/solution.py
@@ -11,7 +11,7 @@
 CH = 128
 GROUP = 4
 EARLY = 2
-ORDERS = ((2, 1, 3), (3, 1, 2), (1, 3, 2), (3, 1, 2))
+ORDERS = ((2, 1, 3), (3, 1, 2), (3, 2, 1), (3, 1, 2))
 
 EPSILON = 1e-06
 SCALE = DH ** (-0.5)

time: 57.2 us -> 57.2 us (level)
  no operation moved by 1% of the time
where the time goes in v6:
time: 57.2 us; the launch traced here: 56.8 us
  waiting for transfers between devices  25.5 us (45%)
  starting transfers between devices  22.7 us (40%)
  Pallas kernels  7.8 us (14%)
  between operations  0.7 us (1%)
    ppermute x12, starting transfers between devices, swap(): return lax.ppermute(array, 'seq', [(i, i ^ turn) for i in range(count)])  15.3 us
    ppermute x12, waiting for transfers between devices, swap(): return lax.ppermute(array, 'seq', [(i, i ^ turn) for i in range(count)])  13.4 us
    ppermute x2, waiting for transfers between devices, shift(): lax.ppermute(array, 'seq', [(i, (i + step) % count) for i in range(count)])  9.2 us
    pallas_call x8, Pallas kernels, call(): pl.pallas_call(body, out_shape=[a if i in hbm else pltpu.VMEM(a.shape, a....  7.8 us
    ppermute x2, starting transfers between devices, shift(): lax.ppermute(array, 'seq', [(i, (i + step) % count) for i in range(count)])  5.64 us
    ppermute x3, waiting for transfers between devices, across(): return lax.ppermute(array, 'head', pairs)  2.87 us
    ppermute x3, starting transfers between devices, across(): return lax.ppermute(array, 'head', pairs)  1.78 us
  transfers between devices with their start and end apart: 17, of which 13 were waited for; matrix products, arithmetic and copies ran while one was open for 0% of the time, Pallas kernels for 6%

profile of v6, /device:TPU:0, one launch (start us, length us, event | category | flops | bytes accessed | tf_op | source)
XLA Modules:
  0.0 56.8 jit_solution(1226336629951152798)
XLA Ops:
  0.6 1.8 %shard_map.84 = (bf16[2,128,512]{2,1,0:T(8,128)(2,1)S(1)}, bf16[2,128,512]{2,1,0:T(8,128)(2,1)S(1)}, bf16[2,128,512]{2,1,0:T(8,128)(2,1)S(1)}, bf16[2,128,512]{2...) custom-call(s32[1]{0:T(128)} %bitcast.place_ref, ...), custom_call_target="tpu_custom_call" | custom-call | flops 100663296 | bytes 2883588 | tf_op jit(solution)/shard_map/pallas_call | solution.py:191
  2.5 3.1 %collective-permute-start = (f32[2,128,128]{2,1,0:T(8,128)S(1)}, f32[2,128,128]{2,1,0:T(8,128)S(1)}, u32[]{:S(2)}, u32[]{:S(2)}) collective-permute-start(f32[2,128,128]{2,1,0:T(8,128)S(1)} %get-tuple-element.55), channel_id=1, source_target_pairs={{0,8},{4,12},{8,0},{12,4},{16,24},{20,28},{24,16},{28,20},{1,9},{5... | collective-permute-start | bytes 393224 | tf_op jit(solution)/shard_map/ppermute | solution.py:211
  5.6 1.5 %collective-permute-start.1 = (f32[2,128,128]{2,1,0:T(8,128)S(1)}, f32[2,128,128]{2,1,0:T(8,128)S(1)}, u32[]{:S(2)}, u32[]{:S(2)}) collective-permute-start(f32[2,128,128]{2,1,0:T(8,128)S(1)} %get-tuple-element.56), channel_id=1, source_target_pairs={{0,4},{4,0},{8,12},{12,8},{16,20},{20,16},{24,28},{28,24},{1,5},{5... | collective-permute-start | bytes 393224 | tf_op jit(solution)/shard_map/ppermute | solution.py:211
  7.1 2.2 %collective-permute-done.refs_1_ = f32[2,128,128]{2,1,0:T(8,128)S(1)} collective-permute-done((f32[2,128,128]{2,1,0:T(8,128)S(1)}, f32[2,128,128]{2,1,0:T(8,128)S(1)}, u32[]{:S(2)}, u32[]{:S(2)}) %collective-permute-start) | collective-permute-done | bytes 131104 | tf_op jit(solution)/shard_map/ppermute | solution.py:211
  9.3 4.0 %collective-permute-done.1.refs_2_ = f32[2,128,128]{2,1,0:T(8,128)S(1)} collective-permute-done((f32[2,128,128]{2,1,0:T(8,128)S(1)}, f32[2,128,128]{2,1,0:T(8,128)S(1)}, u32[]{:S(2)}, u32[]{:S(2)}) %collective-permute-start.1) | collective-permute-done | bytes 131104 | tf_op jit(solution)/shard_map/ppermute | solution.py:211
  13.4 2.7 %collective-permute-start.3 = (f32[2,128,128]{2,1,0:T(8,128)S(1)}, f32[2,128,128]{2,1,0:T(8,128)S(1)}, u32[]{:S(2)}, u32[]{:S(2)}) collective-permute-start(f32[2,128,128]{2,1,0:T(8,128)S(1)} %add_add_fusion.1), channel_id=1, source_target_pairs={{0,16},{4,20},{8,24},{12,28},{16,0},{20,4},{24,8},{28,12},{1,17},{... | collective-permute-start | bytes 393224 | tf_op jit(solution)/shard_map/ppermute | solution.py:215
  16.1 4.7 %collective-permute-done.3 = f32[2,128,128]{2,1,0:T(8,128)S(1)} collective-permute-done((f32[2,128,128]{2,1,0:T(8,128)S(1)}, f32[2,128,128]{2,1,0:T(8,128)S(1)}, u32[]{:S(2)}, u32[]{:S(2)}) %collective-permute-start.3) | collective-permute-done | bytes 131104 | tf_op jit(solution)/shard_map/ppermute | solution.py:215
  21.1 1.3 %collective-permute-start.5 = (f32[2,128,128]{2,1,0:T(8,128)S(1)}, f32[2,128,128]{2,1,0:T(8,128)S(1)}, u32[]{:S(2)}, u32[]{:S(2)}) collective-permute-start(f32[2,128,128]{2,1,0:T(8,128)S(1)} %get-tuple-element.60), channel_id=1, source_target_pairs={{0,4},{4,0},{8,12},{12,8},{16,20},{20,16},{24,28},{28,24},{1,5},{5... | collective-permute-start | bytes 393224 | tf_op jit(solution)/shard_map/ppermute | solution.py:211
  22.4 2.1 %collective-permute-start.6 = (f32[2,128,128]{2,1,0:T(8,128)S(1)}, f32[2,128,128]{2,1,0:T(8,128)S(1)}, u32[]{:S(2)}, u32[]{:S(2)}) collective-permute-start(f32[2,128,128]{2,1,0:T(8,128)S(1)} %get-tuple-element.61), channel_id=1, source_target_pairs={{0,8},{4,12},{8,0},{12,4},{16,24},{20,28},{24,16},{28,20},{1,9},{5... | collective-permute-start | bytes 393224 | tf_op jit(solution)/shard_map/ppermute | solution.py:211
  24.5 1.1 %shard_map.85 = (bf16[2,128,512]{2,1,0:T(8,128)(2,1)S(1)}, f32[2,128,512]{2,1,0:T(8,128)S(1)}) custom-call(bf16[2,128,512]{2,1,0:T(8,128)(2,1)S(1)} %get-tuple-element.43.q_ref, bf16[2,128,512]{2,1,0:T(8,128)(2,1)S(1)} %get-tuple-element.44.k_ref, bf16[2,128,512]{2,1,0:T(8,128)(2,1)S(1)} %get-tuple-element.45.v_ref, ...), custom_call_target="tpu_custom_call", output_to_operand_aliasing={{0}: (3, {}), {1}: (4, {})} | custom-call | flops 67108864 | bytes 2359296 | tf_op jit(solution)/shard_map/pallas_call | solution.py:191
  25.5 1.4 %collective-permute-done.4.rest_1_ = f32[2,128,128]{2,1,0:T(8,128)S(1)} collective-permute-done((f32[2,128,128]{2,1,0:T(8,128)S(1)}, f32[2,128,128]{2,1,0:T(8,128)S(1)}, u32[]{:S(2)}, u32[]{:S(2)}) %collective-permute-start.4) | collective-permute-done | bytes 131104 | tf_op jit(solution)/shard_map/ppermute | solution.py:211
  28.2 1.6 %collective-permute-start.8 = (f32[8,128]{1,0:T(8,128)S(1)}, f32[8,128]{1,0:T(8,128)S(1)}, u32[]{:S(2)}, u32[]{:S(2)}) collective-permute-start(f32[8,128]{1,0:T(8,128)S(1)} %get-tuple-element.63.rest_0_), channel_id=1, source_target_pairs={{0,2},{1,3},{2,0},{3,1},{4,6},{5,7},{6,4},{7,5},{8,10},{9,11},{10,... | collective-permute-start | bytes 12296 | tf_op jit(solution)/shard_map/ppermute | solution.py:295
  29.9 1.9 %collective-permute-done.8.rest_2_ = f32[8,128]{1,0:T(8,128)S(1)} collective-permute-done((f32[8,128]{1,0:T(8,128)S(1)}, f32[8,128]{1,0:T(8,128)S(1)}, u32[]{:S(2)}, u32[]{:S(2)}) %collective-permute-start.8) | collective-permute-done | bytes 4128 | tf_op jit(solution)/shard_map/ppermute | solution.py:295
  31.8 0.9 %collective-permute-done.9.rest_3_ = f32[8,128]{1,0:T(8,128)S(1)} collective-permute-done((f32[8,128]{1,0:T(8,128)S(1)}, f32[8,128]{1,0:T(8,128)S(1)}, u32[]{:S(2)}, u32[]{:S(2)}) %collective-permute-start.9) | collective-permute-done | bytes 4128 | tf_op jit(solution)/shard_map/ppermute | solution.py:295
  33.4 2.1 %collective-permute-start.10 = (f32[2,128,128]{2,1,0:T(8,128)S(1)}, f32[2,128,128]{2,1,0:T(8,128)S(1)}, u32[]{:S(2)}, u32[]{:S(2)}) collective-permute-start(f32[2,128,128]{2,1,0:T(8,128)S(1)} %get-tuple-element.73), channel_id=1, source_target_pairs={{0,12},{4,8},{8,4},{12,0},{16,28},{20,24},{24,20},{28,16},{1,13},{... | collective-permute-start | bytes 393224 | tf_op jit(solution)/shard_map/ppermute | solution.py:211
  36.9 2.6 %collective-permute-done.10.refs_1_ = f32[2,128,128]{2,1,0:T(8,128)S(1)} collective-permute-done((f32[2,128,128]{2,1,0:T(8,128)S(1)}, f32[2,128,128]{2,1,0:T(8,128)S(1)}, u32[]{:S(2)}, u32[]{:S(2)}) %collective-permute-start.10) | collective-permute-done | bytes 131104 | tf_op jit(solution)/shard_map/ppermute | solution.py:211
  39.5 1.1 %collective-permute-done.11.refs_2_ = f32[2,128,128]{2,1,0:T(8,128)S(1)} collective-permute-done((f32[2,128,128]{2,1,0:T(8,128)S(1)}, f32[2,128,128]{2,1,0:T(8,128)S(1)}, u32[]{:S(2)}, u32[]{:S(2)}) %collective-permute-start.11) | collective-permute-done | bytes 131104 | tf_op jit(solution)/shard_map/ppermute | solution.py:211
  41.0 3.0 %collective-permute-start.13 = (f32[2,128,128]{2,1,0:T(8,128)S(1)}, f32[2,128,128]{2,1,0:T(8,128)S(1)}, u32[]{:S(2)}, u32[]{:S(2)}) collective-permute-start(f32[2,128,128]{2,1,0:T(8,128)S(1)} %add_add_fusion), channel_id=1, source_target_pairs={{0,16},{4,20},{8,24},{12,28},{16,0},{20,4},{24,8},{28,12},{1,17},{... | collective-permute-start | bytes 393224 | tf_op jit(solution)/shard_map/ppermute | solution.py:215
  44.0 4.5 %collective-permute-done.13 = f32[2,128,128]{2,1,0:T(8,128)S(1)} collective-permute-done((f32[2,128,128]{2,1,0:T(8,128)S(1)}, f32[2,128,128]{2,1,0:T(8,128)S(1)}, u32[]{:S(2)}, u32[]{:S(2)}) %collective-permute-start.13) | collective-permute-done | bytes 131104 | tf_op jit(solution)/shard_map/ppermute | solution.py:215
  49.3 1.0 %collective-permute-start.15 = (f32[2,128,128]{2,1,0:T(8,128)S(1)}, f32[2,128,128]{2,1,0:T(8,128)S(1)}, u32[]{:S(2)}, u32[]{:S(2)}) collective-permute-start(f32[2,128,128]{2,1,0:T(8,128)S(1)} %get-tuple-element.78), channel_id=1, source_target_pairs={{0,4},{4,0},{8,12},{12,8},{16,20},{20,16},{24,28},{28,24},{1,5},{5... | collective-permute-start | bytes 393224 | tf_op jit(solution)/shard_map/ppermute | solution.py:211
  50.3 1.8 %collective-permute-start.16 = (f32[2,128,128]{2,1,0:T(8,128)S(1)}, f32[2,128,128]{2,1,0:T(8,128)S(1)}, u32[]{:S(2)}, u32[]{:S(2)}) collective-permute-start(f32[2,128,128]{2,1,0:T(8,128)S(1)} %get-tuple-element.79), channel_id=1, source_target_pairs={{0,8},{4,12},{8,0},{12,4},{16,24},{20,28},{24,16},{28,20},{1,9},{5... | collective-permute-start | bytes 393224 | tf_op jit(solution)/shard_map/ppermute | solution.py:211
  52.2 2.6 %shard_map.89 = (bf16[2,128,512]{2,1,0:T(8,128)(2,1)}, bf16[2,128,512]{2,1,0:T(8,128)(2,1)}, f32[2,128,512]{2,1,0:T(8,128)S(1)}, f32[2,128,512]{2,1,0:T(8,128)S(1)}) custom-call(bf16[2,128,512]{2,1,0:T(8,128)(2,1)S(1)} %get-tuple-element.43.q_ref, bf16[2,128,512]{2,1,0:T(8,128)(2,1)S(1)} %get-tuple-element.44.k_ref, ...), custom_call_target="tpu_custom_call" | custom-call | flops 167772160 | bytes 3805184 | tf_op jit(solution)/shard_map/pallas_call | solution.py:191
  54.8 0.9 %collective-permute-done.15.rest_2_ = f32[2,128,128]{2,1,0:T(8,128)S(1)} collective-permute-done((f32[2,128,128]{2,1,0:T(8,128)S(1)}, f32[2,128,128]{2,1,0:T(8,128)S(1)}, u32[]{:S(2)}, u32[]{:S(2)}) %collective-permute-start.15) | collective-permute-done | bytes 131104 | tf_op jit(solution)/shard_map/ppermute | solution.py:211
  55.7 1.1 %shard_map.91 = (bf16[2,128,512]{2,1,0:T(8,128)(2,1)}, bf16[2,128,512]{2,1,0:T(8,128)(2,1)}) custom-call(s32[1]{0:T(128)} %bitcast.place_ref, bf16[2,128,512]{2,1,0:T(8,128)(2,1)S(1)} %get-tuple-element.44.k_ref, bf16[2,128,512]{2,1,0:T(8,128)(2,1)S(1)} %get-tuple-element.45.v_ref, f32[2,128,512]{2,1,0:T(8,128)S(1)} %get-tuple-element.70.gkl_ref, ...), custom_call_target="tpu_custom_call" | custom-call | flops 67108864 | bytes 2621444 | tf_op jit(solution)/shard_map/pallas_call | solution.py:191
  (26 shorter events, 5.0 us)
Async XLA Ops:
  2.5 6.8 %collective-permute-start = (f32[2,128,128]{2,1,0:T(8,128)S(1)}, f32[2,128,128]{2,1,0:T(8,128)S(1)}, u32[]{:S(2)}, u32[]{:S(2)}) collective-permute-start(f32[2,128,128]{2,1,0:T(8,128)S(1)} %get-tuple-element.55), channel_id=1, source_target_pairs={{0,8},{4,12},{8,0},{12,4},{16,24},{20,28},{24,16},{28,20},{1,9},{5... | collective-permute-start | bytes 393224 | tf_op jit(solution)/shard_map/ppermute | solution.py:211
  5.6 7.8 %collective-permute-start.1 = (f32[2,128,128]{2,1,0:T(8,128)S(1)}, f32[2,128,128]{2,1,0:T(8,128)S(1)}, u32[]{:S(2)}, u32[]{:S(2)}) collective-permute-start(f32[2,128,128]{2,1,0:T(8,128)S(1)} %get-tuple-element.56), channel_id=1, source_target_pairs={{0,4},{4,0},{8,12},{12,8},{16,20},{20,16},{24,28},{28,24},{1,5},{5... | collective-permute-start | bytes 393224 | tf_op jit(solution)/shard_map/ppermute | solution.py:211
  7.1 6.3 %collective-permute-start.2 = (f32[2,128,128]{2,1,0:T(8,128)S(1)}, f32[2,128,128]{2,1,0:T(8,128)S(1)}, u32[]{:S(2)}, u32[]{:S(2)}) collective-permute-start(f32[2,128,128]{2,1,0:T(8,128)S(1)} %get-tuple-element.57), channel_id=1, source_target_pairs={{0,12},{4,8},{8,4},{12,0},{16,28},{20,24},{24,20},{28,16},{1,13},{... | collective-permute-start | bytes 393224 | tf_op jit(solution)/shard_map/ppermute | solution.py:211
  13.4 7.4 %collective-permute-start.3 = (f32[2,128,128]{2,1,0:T(8,128)S(1)}, f32[2,128,128]{2,1,0:T(8,128)S(1)}, u32[]{:S(2)}, u32[]{:S(2)}) collective-permute-start(f32[2,128,128]{2,1,0:T(8,128)S(1)} %add_add_fusion.1), channel_id=1, source_target_pairs={{0,16},{4,20},{8,24},{12,28},{16,0},{20,4},{24,8},{28,12},{1,17},{... | collective-permute-start | bytes 393224 | tf_op jit(solution)/shard_map/ppermute | solution.py:215
  20.9 6.0 %collective-permute-start.4 = (f32[2,128,128]{2,1,0:T(8,128)S(1)}, f32[2,128,128]{2,1,0:T(8,128)S(1)}, u32[]{:S(2)}, u32[]{:S(2)}) collective-permute-start(f32[2,128,128]{2,1,0:T(8,128)S(1)} %get-tuple-element.59), channel_id=1, source_target_pairs={{0,12},{4,8},{8,4},{12,0},{16,28},{20,24},{24,20},{28,16},{1,13},{... | collective-permute-start | bytes 393224 | tf_op jit(solution)/shard_map/ppermute | solution.py:211
  21.1 6.4 %collective-permute-start.5 = (f32[2,128,128]{2,1,0:T(8,128)S(1)}, f32[2,128,128]{2,1,0:T(8,128)S(1)}, u32[]{:S(2)}, u32[]{:S(2)}) collective-permute-start(f32[2,128,128]{2,1,0:T(8,128)S(1)} %get-tuple-element.60), channel_id=1, source_target_pairs={{0,4},{4,0},{8,12},{12,8},{16,20},{20,16},{24,28},{28,24},{1,5},{5... | collective-permute-start | bytes 393224 | tf_op jit(solution)/shard_map/ppermute | solution.py:211
  22.4 5.3 %collective-permute-start.6 = (f32[2,128,128]{2,1,0:T(8,128)S(1)}, f32[2,128,128]{2,1,0:T(8,128)S(1)}, u32[]{:S(2)}, u32[]{:S(2)}) collective-permute-start(f32[2,128,128]{2,1,0:T(8,128)S(1)} %get-tuple-element.61), channel_id=1, source_target_pairs={{0,8},{4,12},{8,0},{12,4},{16,24},{20,28},{24,16},{28,20},{1,9},{5... | collective-permute-start | bytes 393224 | tf_op jit(solution)/shard_map/ppermute | solution.py:211
  24.5 3.2 %copy-start = (bf16[2,128,512]{2,1,0:T(8,128)(2,1)S(1)}, bf16[2,128,512]{2,1,0:T(8,128)(2,1)}, u32[]{:S(2)}) copy-start(bf16[2,128,512]{2,1,0:T(8,128)(2,1)} %g_ref.1) | copy-start | bytes 786436
  24.5 3.2 %copy-start.1 = (f32[2,512]{1,0:T(2,128)S(1)}, f32[2,512]{1,0:T(2,128)}, u32[]{:S(2)}) copy-start(f32[2,512]{1,0:T(2,128)} %gain_ref.5) | copy-start | bytes 12292
  28.1 1.8 %collective-permute-start.7 = (f32[8,128]{1,0:T(8,128)S(1)}, f32[8,128]{1,0:T(8,128)S(1)}, u32[]{:S(2)}, u32[]{:S(2)}) collective-permute-start(f32[8,128]{1,0:T(8,128)S(1)} %get-tuple-element.63.rest_0_), channel_id=1, source_target_pairs={{0,3},{1,0},{2,1},{3,2},{4,7},{5,4},{6,5},{7,6},{8,11},{9,8},{10,9... | collective-permute-start | bytes 12296 | tf_op jit(solution)/shard_map/ppermute | solution.py:295
  28.2 3.7 %collective-permute-start.8 = (f32[8,128]{1,0:T(8,128)S(1)}, f32[8,128]{1,0:T(8,128)S(1)}, u32[]{:S(2)}, u32[]{:S(2)}) collective-permute-start(f32[8,128]{1,0:T(8,128)S(1)} %get-tuple-element.63.rest_0_), channel_id=1, source_target_pairs={{0,2},{1,3},{2,0},{3,1},{4,6},{5,7},{6,4},{7,5},{8,10},{9,11},{10,... | collective-permute-start | bytes 12296 | tf_op jit(solution)/shard_map/ppermute | solution.py:295
  29.8 3.0 %collective-permute-start.9 = (f32[8,128]{1,0:T(8,128)S(1)}, f32[8,128]{1,0:T(8,128)S(1)}, u32[]{:S(2)}, u32[]{:S(2)}) collective-permute-start(f32[8,128]{1,0:T(8,128)S(1)} %get-tuple-element.63.rest_0_), channel_id=1, source_target_pairs={{0,1},{1,2},{2,3},{3,0},{4,5},{5,6},{6,7},{7,4},{8,9},{9,10},{10,1... | collective-permute-start | bytes 12296 | tf_op jit(solution)/shard_map/ppermute | solution.py:295
  33.4 6.2 %collective-permute-start.10 = (f32[2,128,128]{2,1,0:T(8,128)S(1)}, f32[2,128,128]{2,1,0:T(8,128)S(1)}, u32[]{:S(2)}, u32[]{:S(2)}) collective-permute-start(f32[2,128,128]{2,1,0:T(8,128)S(1)} %get-tuple-element.73), channel_id=1, source_target_pairs={{0,12},{4,8},{8,4},{12,0},{16,28},{20,24},{24,20},{28,16},{1,13},{... | collective-permute-start | bytes 393224 | tf_op jit(solution)/shard_map/ppermute | solution.py:211
  35.5 5.1 %collective-permute-start.11 = (f32[2,128,128]{2,1,0:T(8,128)S(1)}, f32[2,128,128]{2,1,0:T(8,128)S(1)}, u32[]{:S(2)}, u32[]{:S(2)}) collective-permute-start(f32[2,128,128]{2,1,0:T(8,128)S(1)} %get-tuple-element.74), channel_id=1, source_target_pairs={{0,8},{4,12},{8,0},{12,4},{16,24},{20,28},{24,16},{28,20},{1,9},{5... | collective-permute-start | bytes 393224 | tf_op jit(solution)/shard_map/ppermute | solution.py:211
  36.0 5.0 %collective-permute-start.12 = (f32[2,128,128]{2,1,0:T(8,128)S(1)}, f32[2,128,128]{2,1,0:T(8,128)S(1)}, u32[]{:S(2)}, u32[]{:S(2)}) collective-permute-start(f32[2,128,128]{2,1,0:T(8,128)S(1)} %get-tuple-element.75), channel_id=1, source_target_pairs={{0,4},{4,0},{8,12},{12,8},{16,20},{20,16},{24,28},{28,24},{1,5},{5... | collective-permute-start | bytes 393224 | tf_op jit(solution)/shard_map/ppermute | solution.py:211
  41.0 7.4 %collective-permute-start.13 = (f32[2,128,128]{2,1,0:T(8,128)S(1)}, f32[2,128,128]{2,1,0:T(8,128)S(1)}, u32[]{:S(2)}, u32[]{:S(2)}) collective-permute-start(f32[2,128,128]{2,1,0:T(8,128)S(1)} %add_add_fusion), channel_id=1, source_target_pairs={{0,16},{4,20},{8,24},{12,28},{16,0},{20,4},{24,8},{28,12},{1,17},{... | collective-permute-start | bytes 393224 | tf_op jit(solution)/shard_map/ppermute | solution.py:215
  48.6 6.2 %collective-permute-start.14 = (f32[2,128,128]{2,1,0:T(8,128)S(1)}, f32[2,128,128]{2,1,0:T(8,128)S(1)}, u32[]{:S(2)}, u32[]{:S(2)}) collective-permute-start(f32[2,128,128]{2,1,0:T(8,128)S(1)} %get-tuple-element.77), channel_id=1, source_target_pairs={{0,12},{4,8},{8,4},{12,0},{16,28},{20,24},{24,20},{28,16},{1,13},{... | collective-permute-start | bytes 393224 | tf_op jit(solution)/shard_map/ppermute | solution.py:211
  49.3 6.4 %collective-permute-start.15 = (f32[2,128,128]{2,1,0:T(8,128)S(1)}, f32[2,128,128]{2,1,0:T(8,128)S(1)}, u32[]{:S(2)}, u32[]{:S(2)}) collective-permute-start(f32[2,128,128]{2,1,0:T(8,128)S(1)} %get-tuple-element.78), channel_id=1, source_target_pairs={{0,4},{4,0},{8,12},{12,8},{16,20},{20,16},{24,28},{28,24},{1,5},{5... | collective-permute-start | bytes 393224 | tf_op jit(solution)/shard_map/ppermute | solution.py:211
  50.3 5.3 %collective-permute-start.16 = (f32[2,128,128]{2,1,0:T(8,128)S(1)}, f32[2,128,128]{2,1,0:T(8,128)S(1)}, u32[]{:S(2)}, u32[]{:S(2)}) collective-permute-start(f32[2,128,128]{2,1,0:T(8,128)S(1)} %get-tuple-element.79), channel_id=1, source_target_pairs={{0,8},{4,12},{8,0},{12,4},{16,24},{20,28},{24,16},{28,20},{1,9},{5... | collective-permute-start | bytes 393224 | tf_op jit(solution)/shard_map/ppermute | solution.py:211
